TPU v7x, 32 devices: a whole 2x2x4 slice. The times are simulated.
32 devices in a mesh: segment: 4 (over y, x), dp: 2 (over core), tensor: 4 (over z).
Axes of the slice: x: 2, y: 2, z: 4, core: 2. Of those that a mesh axis runs over, the one named last changes fastest.
Arguments:
- text_embed: bfloat16 [2, 2048, 8192], P('dp', 'segment', 'tensor'), may hold values from -6 to 6
- crop_feats: bfloat16 [4, 2, 1, 256, 1280], P('segment', 'dp'), may hold values from -6 to 6
- crop_dest: int32 [4, 2, 1], P('segment'), may hold values from 0 to 1, as said below
- vision_gain: bfloat16 [1280], replicated, may hold values from 0.5 to 1.5
- proj_weight: bfloat16 [1280, 8192], P(None, 'tensor'), may hold values from -0.15625 to 0.15625
- newline: bfloat16 [8192], P('tensor'), may hold values from -6 to 6
- norm_gain: bfloat16 [8192], P('tensor'), may hold values from 0.5 to 1.5
- xz_weight: bfloat16 [8192, 2048], P('tensor', 'dp'), may hold values from -0.0625 to 0.0625
- dt_weight: bfloat16 [8192, 8], P('tensor', 'dp'), may hold values from -0.0625 to 0.0625
- bc_weight: bfloat16 [8192, 512], P('tensor', 'dp'), may hold values from -0.0625 to 0.0625
- conv_x: bfloat16 [4, 1024], P(None, ('dp', 'tensor')), may hold values from -3 to 3
- conv_bc: bfloat16 [4, 512], P(None, 'dp'), may hold values from -3 to 3
- dt_bias: float32 [8], P(('dp', 'tensor')), may hold values from -6 to -2
- a_log: float32 [8], P(('dp', 'tensor')), may hold values from -4 to 1
- skip: float32 [8], P(('dp', 'tensor')), may hold values from 0.5 to 1.5
- out_gain: bfloat16 [1024], P(('dp', 'tensor')), may hold values from 0.5 to 1.5
- out_weight: bfloat16 [1024, 8192], P('dp', 'tensor'), may hold values from -0.1875 to 0.1875
Outputs:
- hidden_out: bfloat16 [2, 2048, 8192], P('dp', 'segment', 'tensor')
Inputs may be any that keep to these rules, and one draw needn't show every extreme that they name: `crop_dest`: in each section, the 1 crops of one encoder rank go to different sequences, at most 1 crops go to one sequence, and in every section some sequence receives exactly 1.
All inputs are finite; a program needn't handle non-finite values.
Results may differ from a plain program's by a relative error of at most 0.015.
Values may be sent and summed in bfloat16 or wider, within the bound.
No kernel may reach another device: no remote copies, remote signals or barrier semaphores. Data moves between devices by JAX's collectives and lax.ppermute only.
A program may use at most 128 MiB of HBM per device.

v0:
```python
import jax
import jax.numpy as jnp
from jax import lax
from jax.sharding import PartitionSpec as P


def passed_along(block, axis, distance):
    devices = range(lax.axis_size(axis))
    route = [(i - distance, i) for i in devices if i - distance in devices]
    return lax.ppermute(block, axis, route)


def per_device(
    text_embed,
    crop_feats,
    crop_dest,
    vision_gain,
    proj_weight,
    newline,
    norm_gain,
    xz_weight,
    dt_weight,
    bc_weight,
    conv_x,
    conv_bc,
    dt_bias,
    a_log,
    skip,
    out_gain,
    out_weight,
):
    highest = lax.Precision.HIGHEST
    eps = 1e-05
    dp_count = lax.axis_size("dp")
    tp_count = lax.axis_size("tensor")
    segment_count = lax.axis_size("segment")
    my_rank = lax.axis_index("dp")
    section = text_embed.shape[1]
    columns = text_embed.shape[2]
    crop_count = crop_feats.shape[2]
    crop_rows = crop_feats.shape[3]
    crop_span = crop_rows + 1
    heads_dev = dt_bias.shape[0]
    head_width = out_gain.shape[0] // heads_dev
    state_size = bc_weight.shape[1] // 2
    feats = crop_feats[0, 0].astype(jnp.float32)
    vision = (
        feats
        * lax.rsqrt(jnp.mean(feats * feats, -1, keepdims=True) + eps)
        * vision_gain.astype(jnp.float32)
    ).astype(jnp.bfloat16)
    encoded = jnp.dot(
        vision.reshape(crop_count * crop_rows, -1), proj_weight, preferred_element_type=jnp.float32
    )
    encoded = encoded.astype(jnp.bfloat16).reshape(crop_count, crop_rows, columns)
    table = crop_dest[0]
    sources = jnp.arange(dp_count, dtype=jnp.int32)
    mine = jnp.sum(jnp.where(sources[:, None] == my_rank, table, 0), axis=0)
    chosen = mine[None, :] == sources[:, None]
    outgoing = jnp.einsum(
        "dc,crq->drq", chosen.astype(jnp.bfloat16), encoded, preferred_element_type=jnp.float32
    ).astype(jnp.bfloat16)
    incoming = lax.all_to_all(outgoing, "dp", split_axis=0, concat_axis=0, tiled=True)
    sent_rows = incoming.shape[1]
    valid = jnp.any(table == my_rank, axis=1).astype(jnp.int32)
    order = jnp.cumsum(valid) - valid
    counted = jnp.sum(valid)
    positions = jnp.arange(section, dtype=jnp.int32)
    block = positions // crop_span
    within = positions % crop_span
    slot_ids = jnp.arange(section // crop_span + 1, dtype=jnp.int32)
    matched = (valid[None, :] == 1) & (order[None, :] == slot_ids[:, None])
    slot_source = jnp.sum(jnp.where(matched, sources[None, :], 0), axis=1)
    row_source = jnp.sum(
        jnp.where(block[:, None] == slot_ids[None, :], slot_source[None, :], 0), axis=1
    )
    row_index = row_source * sent_rows + jnp.minimum(within, sent_rows - 1)
    picked = jnp.take(incoming.reshape(dp_count * sent_rows, columns), row_index, axis=0)
    image = block < counted
    text = text_embed[0]
    crop_pos = image & (within < crop_rows)
    line_pos = image & (within == crop_rows)
    hidden = jnp.where(
        crop_pos[:, None], picked, jnp.where(line_pos[:, None], newline[None, :], text)
    )
    wide = hidden.astype(jnp.float32)
    row_total = lax.psum(jnp.sum(wide * wide, -1), "tensor")
    normed = (
        wide
        * lax.rsqrt(row_total / (columns * tp_count) + eps)[:, None]
        * norm_gain.astype(jnp.float32)
    ).astype(jnp.bfloat16)
    pair_cols = xz_weight.shape[1]
    step_cols = dt_weight.shape[1]
    piece = lax.all_gather(normed, "dp", axis=0, tiled=True)
    terms = jnp.concatenate(
        [
            jnp.dot(piece, xz_weight, preferred_element_type=jnp.float32),
            jnp.dot(piece, dt_weight, preferred_element_type=jnp.float32),
            jnp.dot(piece, bc_weight, preferred_element_type=jnp.float32),
        ],
        axis=1,
    )
    pair_mine, step_mine = (
        lax.psum_scatter(
            terms[:, :pair_cols].astype(jnp.bfloat16), "tensor", scatter_dimension=1, tiled=True
        ).astype(jnp.float32),
        lax.psum_scatter(
            terms[:, pair_cols : pair_cols + step_cols].astype(jnp.bfloat16),
            "tensor",
            scatter_dimension=1,
            tiled=True,
        ).astype(jnp.float32),
    )
    map_terms = terms[:, pair_cols + step_cols :]
    maps_all = lax.psum(map_terms.astype(jnp.bfloat16), "tensor").astype(jnp.float32)
    pairs = pair_mine.reshape(dp_count, section, heads_dev, 2, head_width)
    values = pairs[:, :, :, 0, :].reshape(dp_count, section, heads_dev * head_width)
    gates = pairs[:, :, :, 1, :]
    fresh = jnp.concatenate([values, maps_all.reshape(dp_count, section, 2 * state_size)], axis=2)
    kernel = jnp.concatenate([conv_x, conv_bc], axis=1).astype(jnp.float32)
    taps = kernel.shape[0]
    edge = passed_along(fresh[:, section - (taps - 1) :, :], "segment", 1)
    padded = jnp.concatenate([edge, fresh], axis=1)
    filtered = kernel[0] * padded[:, 0:section]
    for offset in range(1, taps):
        filtered = filtered + kernel[offset] * padded[:, offset : offset + section]
    activated = jax.nn.silu(filtered)
    inner_cols = heads_dev * head_width
    streams = activated[..., :inner_cols].reshape(dp_count, section, heads_dev, head_width)
    b_rows = activated[..., inner_cols : inner_cols + state_size]
    c_rows = activated[..., inner_cols + state_size :]
    step = jax.nn.softplus(step_mine.reshape(dp_count, section, heads_dev) + dt_bias)
    cumulative = jnp.cumsum(-jnp.exp(a_log) * step, axis=1)
    scores = jnp.einsum("nls,nms->nlm", c_rows, b_rows, precision=highest)
    mask = (positions[:, None] >= positions[None, :])[None, :, :, None]
    gaps = cumulative[:, :, None, :] - cumulative[:, None, :, :]
    weights = (
        jnp.where(mask, jnp.exp(jnp.where(mask, gaps, 0.0)), 0.0)
        * scores[..., None]
        * step[:, None, :, :]
    )
    inside = jnp.einsum("nlmh,nmhp->nlhp", weights, streams, precision=highest)
    final = cumulative[:, -1, :]
    carry_weight = jnp.exp(final[:, None, :] - cumulative) * step
    local_state = jnp.einsum("nlh,nls,nlhp->nhsp", carry_weight, b_rows, streams, precision=highest)
    decay = jnp.exp(final)
    prior = jnp.zeros_like(local_state)
    for turn in range(segment_count - 1):
        prior = passed_along(
            (decay[:, :, None, None] * prior + local_state).astype(jnp.bfloat16), "segment", 1
        ).astype(jnp.float32)
    across = jnp.exp(cumulative)[..., None] * jnp.einsum(
        "nls,nhsp->nlhp", c_rows, prior, precision=highest
    )
    outputs = inside + across + skip[None, None, :, None] * streams
    gated = outputs * jax.nn.silu(gates)
    group_total = lax.psum(jnp.sum(gated * gated, axis=(2, 3)), "tensor")
    scale = lax.rsqrt(group_total / (inner_cols * tp_count) + eps)
    normed_out = (
        gated * scale[..., None, None] * out_gain.astype(jnp.float32).reshape(heads_dev, head_width)
    ).astype(jnp.bfloat16)
    normed_out = normed_out.reshape(dp_count * section, inner_cols)
    term = jnp.dot(
        lax.all_gather(normed_out, "tensor", axis=1, tiled=True),
        out_weight,
        preferred_element_type=jnp.float32,
    )
    mixed = lax.psum_scatter(
        term.astype(jnp.bfloat16), "dp", scatter_dimension=0, tiled=True
    ).astype(jnp.float32)
    return (wide + mixed).astype(jnp.bfloat16)[None]


def solution(mesh):
    return jax.shard_map(
        per_device,
        mesh=mesh,
        in_specs=(
            P("dp", "segment", "tensor"),
            P("segment", "dp", None, None, None),
            P("segment", None, None),
            P(),
            P(None, "tensor"),
            P("tensor"),
            P("tensor"),
            P("tensor", "dp"),
            P("tensor", "dp"),
            P("tensor", "dp"),
            P(None, ("dp", "tensor")),
            P(None, "dp"),
            P(("dp", "tensor")),
            P(("dp", "tensor")),
            P(("dp", "tensor")),
            P(("dp", "tensor")),
            P("dp", "tensor"),
        ),
        out_specs=P("dp", "segment", "tensor"),
        check_vma=False,
    )
```

profile of v0, /device:TPU:0, one launch (start us, length us, event | category | flops | bytes accessed | tf_op | source)
XLA Modules:
  0.0 258.2 jit_solution(1296364862814400676)
XLA Ops:
  6.5 1.4 fusion.71
  8.6 1.3 fusion.21
  10.6 4.3 %fusion.4 = f32[256,2048]{1,0:T(8,128)S(1)} fusion(bf16[1280,2048]{1,0:T(8,128)(2,1)} %param.21, bf16[1,1,1,256,1280]{4,3,2,1,0:T(8,128)(2,1)} %param.18, f32[1280]{0:T(1024)S(1)} %convert_element_type.125, f32[256]{0:T(256)S(1)} %add_rsqrt_fusion.2), kind=kOutput, calls=%fused_computation.11 | convolution fusion | flops 1344536576 | bytes 8001536 | tf_op jit(solution)/shard_map/dot_general | solution.py:52
  15.0 1.8 multiply_convert_fusion
  16.8 5.0 %all-to-all-start = ((bf16[2,256,2048]{2,1,0:T(8,128)(2,1)}), bf16[2,256,2048]{2,1,0:T(8,128)(2,1)}, u32[]{:S(2)}, u32[]{:S(2)}) async-start(bf16[2,256,2048]{2,1,0:T(8,128)(2,1)} %multiply_convert_fusion), calls=%async_computation | async-start | bytes 4194304 | tf_op jit(solution)/shard_map/all_to_all | solution.py:63
  24.7 7.1 %gather_fusion = bf16[512,2048]{1,0:T(8,128)(2,1)} fusion(bf16[512,2048]{1,0:T(8,128)(2,1)} %bitcast.4, s32[1024]{0:T(1024)S(1)} %pad_clamp_fusion), kind=kCustom, calls=%fused_computation | custom fusion | bytes 4196352 | tf_op jit(solution)/shard_map/jit(_take)/gather | solution.py:78
  31.8 3.8 %fusion = (f32[512]{0:T(512)S(1)}, bf16[512,2048]{1,0:T(8,128)(2,1)}) fusion(bf16[1,512,2048]{2,1,0:T(8,128)(2,1)} %param.17, bf16[2048]{0:T(1024)(128)(2,1)S(1)} %copy-done.3, pred[512]{0:T(512)(128)(4,1)S(1)} %get-tuple-element.22, bf16[512,2048]{1,0:T(8,128)(2,1)} %gather_fusion, pred[512]{0:T(512)(128)(4,1)S(1)} %compare_and_fusion.1, ...), kind=kLoop, calls=%fused_computation.4 | loop fusion | flops 6290944 | bytes 6299136 | tf_op jit(solution)/shard_map/reduce_sum | solution.py:87
  35.6 13.4 %psum.21 = f32[512]{0:T(512)S(1)} all-reduce(f32[512]{0:T(512)S(1)} %get-tuple-element.16), channel_id=1, replica_groups=mesh['segment'=4,'dp'=2,'tensor'=4] {'tensor'}, use_global_device_ids=true, to_apply=%region_7.8 | all-reduce | flops 512 | bytes 4096 | tf_op jit(solution)/shard_map/psum | solution.py:87
  49.0 3.5 %fusion.2 = bf16[512,2048]{1,0:T(8,128)(2,1)} fusion(bf16[512,2048]{1,0:T(8,128)(2,1)} %get-tuple-element.17, f32[2048]{0:T(1024)S(1)} %convert_element_type.131, f32[512]{0:T(512)S(1)} %add_rsqrt_fusion.1), kind=kLoop, calls=%fused_computation.6 | loop fusion | flops 4194304 | bytes 4204544 | tf_op jit(solution)/shard_map/convert_element_type | solution.py:92
  52.6 12.0 %all-gather.3.cloned.1.call-done = bf16[1024,2048]{1,0:T(8,128)(2,1)} async-done(((bf16[512,2048]{1,0:T(8,128)(2,1)}), bf16[1024,2048]{1,0:T(8,128)(2,1)}) %all-gather.3.cloned.1.call-update) | async-done | bytes 4194320 | tf_op jit(solution)/shard_map/all_gather | solution.py:95
  64.6 4.2 %convolution_convert_fusion.3 = bf16[1024,256]{1,0:T(8,128)(2,1)} fusion(bf16[1024,2048]{1,0:T(8,128)(2,1)} %all-gather.3.cloned.1.call-done, bf16[2048,256]{1,0:T(8,128)(2,1)S(1)} %copy-done.7), kind=kOutput, calls=%fused_computation.41 | convolution fusion | flops 1074003968 | bytes 5767168 | tf_op jit(solution)/shard_map/dot_general | solution.py:100
  68.9 9.3 %convolution_convert_fusion.2 = bf16[1024,1024]{1,0:T(8,128)(2,1)} fusion(bf16[1024,2048]{1,0:T(8,128)(2,1)} %all-gather.3.cloned.1.call-done, bf16[2048,1024]{1,0:T(8,128)(2,1)} %param.24), kind=kOutput, calls=%fused_computation.24 | convolution fusion | flops 4296015872 | bytes 10485760 | tf_op jit(solution)/shard_map/dot_general | solution.py:98
  80.2 3.4 %convolution_convert_fusion.4 = bf16[1024,4]{0,1:T(4,128)(2,1)S(1)} fusion(bf16[1024,2048]{1,0:T(8,128)(2,1)} %all-gather.3.cloned.1.call-done, bf16[2048,4]{0,1:T(4,128)(2,1)S(1)} %copy-done.1), kind=kOutput, calls=%fused_computation.48 | convolution fusion | flops 16781312 | bytes 4218880 | tf_op jit(solution)/shard_map/dot_general | solution.py:99
  83.6 12.2 %all-reduce = bf16[1024,4]{0,1:T(4,128)(2,1)S(1)} all-reduce(bf16[1024,4]{0,1:T(4,128)(2,1)S(1)} %convolution_convert_fusion.4), channel_id=3, replica_groups=mesh['segment'=4,'dp'=2,'tensor'=4] {'tensor'}, use_global_device_ids=true, to_apply=%region_10.11.clone | all-reduce | flops 4096 | bytes 16384
  96.4 1.3 fusion.77
  99.2 9.2 %all-reduce.3.cloned.1.call-done = bf16[2,512,256]{2,1,0:T(8,128)(2,1)} async-done(((bf16[2,512,256]{2,1,0:T(8,128)(2,1)}), bf16[2,512,256]{2,1,0:T(8,128)(2,1)}) %all-reduce.3.cloned.1.call-update) | async-done | bytes 524304 | tf_op jit(solution)/shard_map/psum | solution.py:116
  109.6 45.0 %reduce-scatter.3.cloned.1.call-done = bf16[1024,256]{1,0:T(8,128)(2,1)} async-done(((bf16[1024,1024]{1,0:T(8,128)(2,1)}), bf16[1024,256]{1,0:T(8,128)(2,1)}) %reduce-scatter.3.cloned.1.call-update) | async-done | bytes 524304 | tf_op jit(solution)/shard_map/reduce_scatter | solution.py:105
  154.6 2.5 reshape.561
  157.1 2.5 fusion.80
  159.6 3.4 %collective-permute-start = (f32[2,3,384]{2,1,0:T(4,128)S(1)}, f32[2,3,384]{2,1,0:T(4,128)S(1)}, u32[]{:S(2)}, u32[]{:S(2)}) collective-permute-start(f32[2,3,384]{2,1,0:T(4,128)S(1)} %fusion.57), channel_id=1, source_target_pairs={{0,8},{8,16},{16,24},{1,9},{9,17},{17,25},{2,10},{10,18},{18,26},{... | collective-permute-start | bytes 27656 | tf_op jit(solution)/shard_map/ppermute | solution.py:10
  163.0 1.4 collective-permute-done
  166.6 4.2 %collective-permute-start.1 = (bf16[2,1,128,128]{3,2,0,1:T(8,128)(2,1)S(1)}, bf16[2,1,128,128]{3,2,0,1:T(8,128)(2,1)S(1)}, u32[]{:S(2)}, u32[]{:S(2)}) collective-permute-start(bf16[2,1,128,128]{3,2,0,1:T(8,128)(2,1)S(1)} %fusion.55), channel_id=1, source_target_pairs={{0,8},{8,16},{16,24},{1,9},{9,17},{17,25},{2,10},{10,18},{18,26},{... | collective-permute-start | bytes 196616 | tf_op jit(solution)/shard_map/ppermute | solution.py:10
  172.8 4.3 %collective-permute-start.2 = (bf16[2,1,128,128]{3,2,0,1:T(8,128)(2,1)S(1)}, bf16[2,1,128,128]{3,2,0,1:T(8,128)(2,1)S(1)}, u32[]{:S(2)}, u32[]{:S(2)}) collective-permute-start(bf16[2,1,128,128]{3,2,0,1:T(8,128)(2,1)S(1)} %fusion.53), channel_id=1, source_target_pairs={{0,8},{8,16},{16,24},{1,9},{9,17},{17,25},{2,10},{10,18},{18,26},{... | collective-permute-start | bytes 196616 | tf_op jit(solution)/shard_map/ppermute | solution.py:10
  177.2 1.8 collective-permute-done.2
  179.1 5.2 %collective-permute-start.3 = (bf16[2,1,128,128]{3,2,0,1:T(8,128)(2,1)S(1)}, bf16[2,1,128,128]{3,2,0,1:T(8,128)(2,1)S(1)}, u32[]{:S(2)}, u32[]{:S(2)}) collective-permute-start(bf16[2,1,128,128]{3,2,0,1:T(8,128)(2,1)S(1)} %fusion.54), channel_id=1, source_target_pairs={{0,8},{8,16},{16,24},{1,9},{9,17},{17,25},{2,10},{10,18},{18,26},{... | collective-permute-start | bytes 196616 | tf_op jit(solution)/shard_map/ppermute | solution.py:10
  184.2 1.8 fusion.46
  186.5 2.5 multiply_reduce_fusion
  189.0 10.0 %psum.23 = f32[2,512]{1,0:T(2,128)S(1)} all-reduce(f32[2,512]{1,0:T(2,128)S(1)} %get-tuple-element.20), channel_id=1, replica_groups=mesh['segment'=4,'dp'=2,'tensor'=4] {'tensor'}, use_global_device_ids=true, to_apply=%region_14.15 | all-reduce | flops 1024 | bytes 8192 | tf_op jit(solution)/shard_map/psum | solution.py:158
  200.3 30.9 %all-gather.5.cloned.1.call-done = bf16[1024,512]{1,0:T(8,128)(2,1)} async-done(((bf16[1024,128]{1,0:T(8,128)(2,1)}), bf16[1024,512]{1,0:T(8,128)(2,1)}) %all-gather.5.cloned.1.call-update) | async-done | bytes 1048592 | tf_op jit(solution)/shard_map/all_gather | solution.py:165
  231.2 5.5 %convolution_convert_fusion = bf16[1024,2048]{1,0:T(8,128)(2,1)} fusion(bf16[1024,512]{1,0:T(8,128)(2,1)} %all-gather.5.cloned.1.call-done, bf16[512,2048]{1,0:T(8,128)(2,1)S(1)} %copy-done), kind=kOutput, calls=%fused_computation.9 | convolution fusion | flops 2149580800 | bytes 7340032 | tf_op jit(solution)/shard_map/dot_general | solution.py:164
  236.7 10.5 %reduce-scatter.5.cloned.1.call-done = bf16[512,2048]{1,0:T(8,128)(2,1)} async-done(((bf16[1024,2048]{1,0:T(8,128)(2,1)}), bf16[512,2048]{1,0:T(8,128)(2,1)}) %reduce-scatter.5.cloned.1.call-update) | async-done | bytes 2097168 | tf_op jit(solution)/shard_map/reduce_scatter | solution.py:169
  247.2 4.4 %fusion.5 = bf16[1,512,2048]{2,1,0:T(8,128)(2,1)} fusion(bf16[512,2048]{1,0:T(8,128)(2,1)} %reduce-scatter.5.cloned.1.call-done, bf16[512,2048]{1,0:T(8,128)(2,1)} %get-tuple-element.17), kind=kLoop, calls=%fused_computation.12 | loop fusion | flops 4194304 | bytes 6291456 | tf_op jit(solution)/shard_map/broadcast_in_dim | solution.py:172
  (82 shorter events, 13.6 us)
Async XLA Ops:
  6.5 224.6 %copy-start = (bf16[512,2048]{1,0:T(8,128)(2,1)S(1)}, bf16[512,2048]{1,0:T(8,128)(2,1)}, u32[]{:S(2)}) copy-start(bf16[512,2048]{1,0:T(8,128)(2,1)} %param.33) | copy-start | bytes 6291460
  16.8 5.0 %copy-start.6 = (s32[1,2,1]{1,2,0:T(1,128)S(1)}, s32[1,2,1]{1,2,0:T(1,128)}, u32[]{:S(2)}) copy-start(s32[1,2,1]{1,2,0:T(1,128)} %param.19) | copy-start | bytes 28
  16.8 6.8 %copy-start.2 = (bf16[2048]{0:T(1024)(128)(2,1)S(1)}, bf16[2048]{0:T(1024)(128)(2,1)}, u32[]{:S(2)}) copy-start(bf16[2048]{0:T(1024)(128)(2,1)} %param.23) | copy-start | bytes 12292
  16.8 7.9 %all-to-all-start = ((bf16[2,256,2048]{2,1,0:T(8,128)(2,1)}), bf16[2,256,2048]{2,1,0:T(8,128)(2,1)}, u32[]{:S(2)}, u32[]{:S(2)}) async-start(bf16[2,256,2048]{2,1,0:T(8,128)(2,1)} %multiply_convert_fusion), calls=%async_computation | async-start | bytes 4194304 | tf_op jit(solution)/shard_map/all_to_all | solution.py:63
  21.7 42.8 %all-gather.3.cloned.1.call-start = ((), (), s32[]{:S(2)}) async-start(), calls=%async_computation.3 | async-start | bytes 6291456 | tf_op jit(solution)/shard_map/all_gather | solution.py:95
  24.7 7.1 %copy-start.3 = (bf16[2048]{0:T(1024)(128)(2,1)S(1)}, bf16[2048]{0:T(1024)(128)(2,1)}, u32[]{:S(2)}) copy-start(bf16[2048]{0:T(1024)(128)(2,1)} %param.22) | copy-start | bytes 12292
  52.5 12.1 %copy-start.7 = (bf16[2048,256]{1,0:T(8,128)(2,1)S(1)}, bf16[2048,256]{1,0:T(8,128)(2,1)}, u32[]{:S(2)}) copy-start(bf16[2048,256]{1,0:T(8,128)(2,1)} %param.26) | copy-start | bytes 3145732
  52.5 55.9 %all-reduce.3.cloned.1.call-start = ((), (), s32[]{:S(2)}) async-start(), calls=%async_computation.5 | async-start | bytes 1048576 | tf_op jit(solution)/shard_map/psum | solution.py:116
  68.8 85.8 %reduce-scatter.3.cloned.1.call-start = ((), (), s32[]{:S(2)}) async-start(), calls=%async_computation.4 | async-start | bytes 2621440 | tf_op jit(solution)/shard_map/reduce_scatter | solution.py:105
  78.2 1.4 copy-start.9
  78.2 2.0 copy-start.4
  78.2 2.0 copy-start.5
  78.2 2.0 copy-start.1
  78.2 153.0 %all-gather.5.cloned.1.call-start = ((), (), s32[]{:S(2)}) async-start(), calls=%async_computation.6 | async-start | bytes 1310720 | tf_op jit(solution)/shard_map/all_gather | solution.py:165
  159.6 4.8 %collective-permute-start = (f32[2,3,384]{2,1,0:T(4,128)S(1)}, f32[2,3,384]{2,1,0:T(4,128)S(1)}, u32[]{:S(2)}, u32[]{:S(2)}) collective-permute-start(f32[2,3,384]{2,1,0:T(4,128)S(1)} %fusion.57), channel_id=1, source_target_pairs={{0,8},{8,16},{16,24},{1,9},{9,17},{17,25},{2,10},{10,18},{18,26},{... | collective-permute-start | bytes 27656 | tf_op jit(solution)/shard_map/ppermute | solution.py:10
  164.5 7.0 %copy-start.8 = (bf16[128]{0:T(256)(128)(2,1)S(1)}, bf16[128]{0:T(256)(128)(2,1)}, u32[]{:S(2)}) copy-start(bf16[128]{0:T(256)(128)(2,1)} %param.32) | copy-start | bytes 772
  166.6 6.1 %collective-permute-start.1 = (bf16[2,1,128,128]{3,2,0,1:T(8,128)(2,1)S(1)}, bf16[2,1,128,128]{3,2,0,1:T(8,128)(2,1)S(1)}, u32[]{:S(2)}, u32[]{:S(2)}) collective-permute-start(bf16[2,1,128,128]{3,2,0,1:T(8,128)(2,1)S(1)} %fusion.55), channel_id=1, source_target_pairs={{0,8},{8,16},{16,24},{1,9},{9,17},{17,25},{2,10},{10,18},{18,26},{... | collective-permute-start | bytes 196616 | tf_op jit(solution)/shard_map/ppermute | solution.py:10
  172.8 6.2 %collective-permute-start.2 = (bf16[2,1,128,128]{3,2,0,1:T(8,128)(2,1)S(1)}, bf16[2,1,128,128]{3,2,0,1:T(8,128)(2,1)S(1)}, u32[]{:S(2)}, u32[]{:S(2)}) collective-permute-start(bf16[2,1,128,128]{3,2,0,1:T(8,128)(2,1)S(1)} %fusion.53), channel_id=1, source_target_pairs={{0,8},{8,16},{16,24},{1,9},{9,17},{17,25},{2,10},{10,18},{18,26},{... | collective-permute-start | bytes 196616 | tf_op jit(solution)/shard_map/ppermute | solution.py:10
  179.1 7.1 %collective-permute-start.3 = (bf16[2,1,128,128]{3,2,0,1:T(8,128)(2,1)S(1)}, bf16[2,1,128,128]{3,2,0,1:T(8,128)(2,1)S(1)}, u32[]{:S(2)}, u32[]{:S(2)}) collective-permute-start(bf16[2,1,128,128]{3,2,0,1:T(8,128)(2,1)S(1)} %fusion.54), channel_id=1, source_target_pairs={{0,8},{8,16},{16,24},{1,9},{9,17},{17,25},{2,10},{10,18},{18,26},{... | collective-permute-start | bytes 196616 | tf_op jit(solution)/shard_map/ppermute | solution.py:10
  200.0 47.2 %reduce-scatter.5.cloned.1.call-start = ((), (), s32[]{:S(2)}) async-start(), calls=%async_computation.7 | async-start | bytes 6291456 | tf_op jit(solution)/shard_map/reduce_scatter | solution.py:169
Sparse Core Ops, SparseCore 0:
  52.7 11.8 all-gather.2
  68.9 39.4 all-reduce.2
  110.7 43.8 reduce-scatter.2
  200.1 31.0 all-gather.4
  236.8 10.3 reduce-scatter.4
where the time goes:
time: 259 us; the launch traced here: 258 us
  waiting for transfers between devices  113 us (44%)
  blocking collectives  35.7 us (14%)
  matrix products  32.6 us (13%)
  other arithmetic  24.9 us (10%)
  starting transfers between devices  22.4 us (9%)
  between operations  15.4 us (6%)
  local copies, waits for them, and re-layouts  13.9 us (5%)
    reduce_scatter x1, waiting for transfers between devices, per_device(): lax.psum_scatter(terms[:, :pair_cols].astype(jnp.bfloat16), 'tensor', sca...  45 us
    all_gather x1, waiting for transfers between devices, per_device(): lax.all_gather(normed_out, 'tensor', axis=1, tiled=True)  30.9 us
    ppermute x4, starting transfers between devices, passed_along(): return lax.ppermute(block, axis, route)  17 us
    psum x1, blocking collectives, per_device(): row_total = lax.psum(jnp.sum(wide * wide, -1), 'tensor')  13.4 us
    unnamed x1, blocking collectives  12.2 us
    all_gather x1, waiting for transfers between devices, per_device(): piece = lax.all_gather(normed, 'dp', axis=0, tiled=True)  12 us
    reduce_scatter x1, waiting for transfers between devices, per_device(): lax.psum_scatter(term.astype(jnp.bfloat16), 'dp', scatter_dimension=0, ti...  10.5 us
    psum x1, blocking collectives, per_device(): group_total = lax.psum(jnp.sum(gated * gated, axis=(2, 3)), 'tensor')  10 us
  transfers between devices with their start and end apart: 10, of which 10 were waited for; matrix products, arithmetic and copies ran while one was open for 8% of the time, Pallas kernels for 0%

commit v1 on v0

--- a/solution.py
+++ b/solution.py
@@ -1,7 +1,14 @@
 import jax
 import jax.numpy as jnp
 from jax import lax
+from jax.experimental import pallas as pl
+from jax.experimental.pallas import tpu as pltpu
 from jax.sharding import PartitionSpec as P
+
+EPS = 1e-05
+F32 = jnp.float32
+BF16 = jnp.bfloat16
+HIGHEST = lax.Precision.HIGHEST
 
 
 def passed_along(block, axis, distance):
@@ -10,7 +17,11 @@
     return lax.ppermute(block, axis, route)
 
 
-def per_device(
+def swapped(block, axis, bits):
+    return lax.ppermute(block, axis, [(i, i ^ bits) for i in range(lax.axis_size(axis))])
+
+
+def per_device_any(
     text_embed,
     crop_feats,
     crop_dest,
@@ -172,6 +183,393 @@
     return (wide + mixed).astype(jnp.bfloat16)[None]
 
 
+def contract(a, b, dims, precision=None):
+    return lax.dot_general(
+        a, b, (dims, ((), ())), precision=precision, preferred_element_type=F32
+    )
+
+
+def eye(n):
+    return (
+        lax.broadcasted_iota(jnp.int32, (n, n), 0) == lax.broadcasted_iota(jnp.int32, (n, n), 1)
+    ).astype(F32)
+
+
+def columns_of(rows):
+    return contract(eye(rows.shape[1]), rows, ((1,), (1,)), HIGHEST)
+
+
+def silu(a):
+    return a / (1.0 + jnp.exp(-a))
+
+
+def encode_body(place, mine, other, gain, weight, out, normed):
+    rows = mine.shape[0]
+
+    @pl.when(pl.program_id(0) == 0)
+    def _():
+        stays = place[0] == 1
+        for index, (a, b) in enumerate(((mine, other), (other, mine))):
+            feats = jnp.where(stays, a[...], b[...]).astype(F32)
+            scale = lax.rsqrt(jnp.mean(feats * feats, -1, keepdims=True) + EPS)
+            normed[index * rows : (index + 1) * rows, :] = (
+                feats * scale * gain[...].astype(F32)
+            ).astype(BF16)
+
+    out[...] = jnp.dot(normed[...], weight[...], preferred_element_type=F32).astype(BF16)
+
+
+def encode(place, mine, other, gain, weight):
+    rows, width = mine.shape
+    columns = weight.shape[1]
+    tile = columns // 4
+    return pl.pallas_call(
+        encode_body,
+        grid=(4,),
+        in_specs=[
+            pl.BlockSpec(memory_space=pltpu.SMEM),
+            pl.BlockSpec((rows, width), lambda i: (0, 0)),
+            pl.BlockSpec((rows, width), lambda i: (0, 0)),
+            pl.BlockSpec((1, width), lambda i: (0, 0)),
+            pl.BlockSpec((width, tile), lambda i: (0, i)),
+        ],
+        out_specs=pl.BlockSpec((2 * rows, tile), lambda i: (0, i)),
+        out_shape=jax.ShapeDtypeStruct((2 * rows, columns), BF16),
+        scratch_shapes=[pltpu.VMEM((2 * rows, width), BF16)],
+        name="encode",
+    )(place, mine, other, gain, weight)
+
+
+def project_body(
+    crops, text_mine, text_other, edge_mine, edge_other, newline, gain, xz, bc, dt, first, second,
+    rows, meta,
+):
+    half = text_mine.shape[0]
+    step = pl.program_id(0)
+
+    @pl.when(step == 0)
+    def _():
+        scale = gain[...].astype(F32)
+        top = lax.broadcasted_iota(jnp.int32, (half, 1), 0) == 0
+        line = newline[...].astype(F32)
+        pick = (
+            lax.broadcasted_iota(jnp.int32, (8, 128), 0)
+            == lax.broadcasted_iota(jnp.int32, (8, 128), 1)
+        ).astype(F32)
+        lane = lax.broadcasted_iota(jnp.int32, (half + 16, 128), 1)
+        for part in range(4):
+            base = (part // 2) * half
+            if part % 2 == 0:
+                main = crops[base : base + half, :].astype(F32)
+                edge = (edge_mine, edge_other)[part // 2][...].astype(F32)
+            else:
+                main = (text_mine, text_other)[part // 2][...].astype(F32)
+                main = jnp.where(top, line, main)
+                edge = crops[base + half - 16 : base + half, :].astype(F32)[8:]
+            rows[part, 0:half, :] = (main * scale).astype(BF16)
+            rows[part, half : half + 16, :] = jnp.concatenate(
+                [edge * scale, jnp.zeros_like(edge)], 0
+            ).astype(BF16)
+            squares = jnp.concatenate(
+                [
+                    jnp.sum(main * main, -1, keepdims=True),
+                    jnp.sum(edge * edge, -1, keepdims=True),
+                    jnp.zeros((8, 1), F32),
+                ],
+                0,
+            )
+            steps = jnp.dot(rows[part], dt[...], preferred_element_type=F32)
+            both = jnp.where(lane == 4, squares, steps)
+            across = contract(pick, both, ((1,), (1,)), HIGHEST).astype(BF16)
+            meta[part, 0] = across[:, 0:128]
+            meta[part, 1] = across[:, 128:256]
+            meta[part, 2] = jnp.concatenate(
+                [across[:, half : half + 16], jnp.zeros((8, 112), BF16)], 1
+            )
+            meta[part, 3] = jnp.zeros((8, 128), BF16)
+            meta[part, 4] = jnp.zeros((8, 128), BF16)
+
+    def write(weight):
+        for part in range(4):
+            result = jnp.dot(rows[part], weight, preferred_element_type=F32).astype(BF16)
+            first[part, 0 : half + 8, :] = result[0 : half + 8, 0:128]
+            first[part, half + 8 : half + 16, :] = meta[part, step]
+            second[part] = result[0 : half + 8, 128:256]
+
+    @pl.when(step < 4)
+    def _():
+        write(xz[...])
+
+    @pl.when(step == 4)
+    def _():
+        write(bc[...])
+
+
+def project(crops, text, text_other, edge_mine, edge_other, newline, gain, xz, bc, dt):
+    section, columns = text.shape
+    half = section // 2
+    return pl.pallas_call(
+        project_body,
+        grid=(5,),
+        in_specs=[
+            pl.BlockSpec((2 * half, columns), lambda i: (0, 0)),
+            pl.BlockSpec((half, columns), lambda i: (1, 0)),
+            pl.BlockSpec((half, columns), lambda i: (0, 0)),
+            pl.BlockSpec((8, columns), lambda i: (0, 0)),
+            pl.BlockSpec((8, columns), lambda i: (0, 0)),
+            pl.BlockSpec((1, columns), lambda i: (0, 0)),
+            pl.BlockSpec((1, columns), lambda i: (0, 0)),
+            pl.BlockSpec((columns, 256), lambda i: (0, jnp.minimum(i, 3))),
+            pl.BlockSpec((columns, 256), lambda i: (0, 0)),
+            pl.BlockSpec((columns, 128), lambda i: (0, 0)),
+        ],
+        out_specs=[
+            pl.BlockSpec((4, half + 16, 128), lambda i: (0, 0, i)),
+            pl.BlockSpec((4, half + 8, 128), lambda i: (0, 0, i)),
+        ],
+        out_shape=[
+            jax.ShapeDtypeStruct((4, half + 16, 640), BF16),
+            jax.ShapeDtypeStruct((4, half + 8, 640), BF16),
+        ],
+        scratch_shapes=[
+            pltpu.VMEM((4, half + 16, columns), BF16),
+            pltpu.VMEM((4, 5, 8, 128), BF16),
+        ],
+        name="project",
+    )(crops, text, text_other, edge_mine, edge_other, newline, gain, xz, bc, dt)
+
+
+def filtered(main, edge, taps):
+    rows = main.shape[0]
+    padded = jnp.concatenate([edge, main], 0)
+    count = taps.shape[0]
+    total = taps[count - 1 : count] * main
+    for back in range(1, count):
+        total = total + taps[count - 1 - back : count - back] * padded[8 - back : 8 - back + rows]
+    return total
+
+
+def scan_body(width, first, params, taps_b, streams, maps, meta, state):
+    half = first.shape[0] - 16
+    sums = first[half : half + 16, 0 : half + 128].astype(F32)[8:16]
+    scale = lax.rsqrt(sums[4:5] / width + EPS)
+    head = lax.broadcasted_iota(jnp.int32, (8, 512), 1) // 128
+    owner = (head == lax.broadcasted_iota(jnp.int32, (8, 512), 0)).astype(F32)
+    scalars = params[5:8, :]
+    bias = jnp.sum(owner * scalars[0:1], 1, keepdims=True) * (1.0 / 128)
+    rate = jnp.sum(owner * scalars[1:2], 1, keepdims=True) * (1.0 / 128)
+    raw = sums[:, 0:half] * scale[:, 0:half] + bias
+    step = jnp.maximum(raw, 0.0) + jnp.log1p(jnp.exp(-jnp.abs(raw)))
+    decays = -jnp.exp(rate) * step
+    upper = (
+        lax.broadcasted_iota(jnp.int32, (half, half), 0)
+        <= lax.broadcasted_iota(jnp.int32, (half, half), 1)
+    ).astype(F32)
+    cumulative = contract(decays, upper, ((1,), (0,)), HIGHEST)
+    final = cumulative[:, half - 1 : half]
+    carry = jnp.exp(final - cumulative) * step
+    scale_main = columns_of(jnp.broadcast_to(scale[:, 0:half], (8, half)))[:, 0:1]
+    scale_edge = columns_of(jnp.broadcast_to(scale[:, half : half + 128], (8, 128)))[0:8, 0:1]
+    taps_x = params[0:4, :]
+    edge = first[half : half + 16, :].astype(F32)[0:8] * scale_edge
+    x = silu(filtered(first[0:half, 0:512].astype(F32) * scale_main, edge[:, 0:512], taps_x))
+    b = silu(
+        filtered(
+            first[0:half, 512:640].astype(F32) * scale_main, edge[:, 512:640], taps_b[...].astype(F32)
+        )
+    )
+    carried = contract(columns_of(carry), owner, ((1,), (0,)), HIGHEST)
+    b16 = b.astype(BF16)
+    state[0:128, :] = contract(b16, (x * carried).astype(BF16), ((0,), (0,))).astype(BF16)
+    total = jnp.sum(jnp.exp(final) * owner, 0, keepdims=True)
+    state[128:144, :] = jnp.broadcast_to(total, (16, 512)).astype(BF16)
+    streams[...] = x.astype(BF16)
+    maps[...] = b16
+    meta[0:8, 0:half] = cumulative
+    meta[8:16, 0:half] = step
+    meta[16:24, 0:half] = jnp.broadcast_to(scale[:, 0:half], (8, half))
+    meta[0:8, half : half + 128] = jnp.broadcast_to(scale[:, half : half + 128], (8, 128))
+
+
+def scan(width, first, params, taps_b):
+    half = first.shape[0] - 16
+    return pl.pallas_call(
+        lambda *refs: scan_body(width, *refs),
+        out_shape=[
+            jax.ShapeDtypeStruct((half, 512), BF16),
+            jax.ShapeDtypeStruct((half, 128), BF16),
+            jax.ShapeDtypeStruct((24, half + 128), F32),
+            jax.ShapeDtypeStruct((144, 512), BF16),
+        ],
+        name="scan",
+    )(first, params, taps_b)
+
+
+def mix_body(second, streams, maps, meta, prior, params, taps_c, out):
+    half = streams.shape[0]
+    cumulative = meta[0:8, 0:half]
+    step = meta[8:16, 0:half]
+    cum_cols = columns_of(cumulative)
+    scale_main = columns_of(meta[16:24, 0:half])[:, 0:1]
+    scale_edge = columns_of(meta[0:8, half : half + 128])[0:8, 0:1]
+    both = second[half - 8 : half + 8, 512:640].astype(F32)[8:16] * scale_edge
+    c = silu(
+        filtered(second[0:half, 512:640].astype(F32) * scale_main, both, taps_c[...].astype(F32))
+    ).astype(BF16)
+    scores = contract(c, maps[...], ((1,), (1,)))
+    lower = lax.broadcasted_iota(jnp.int32, (half, half), 0) >= lax.broadcasted_iota(
+        jnp.int32, (half, half), 1
+    )
+    across = jnp.dot(c, prior[...].astype(BF16), preferred_element_type=F32)
+    gated = []
+    squares = jnp.zeros((half, 1), F32)
+    for head in range(4):
+        cols = slice(128 * head, 128 * head + 128)
+        x = streams[:, cols]
+        gaps = cum_cols[:, head : head + 1] - cumulative[head : head + 1]
+        weights = (
+            jnp.where(lower, jnp.exp(jnp.where(lower, gaps, 0.0)), 0.0)
+            * scores
+            * step[head : head + 1]
+        )
+        y = jnp.dot(weights.astype(BF16), x, preferred_element_type=F32)
+        y = y + jnp.exp(cum_cols[:, head : head + 1]) * across[:, cols]
+        y = y + params[7:8, cols] * x.astype(F32)
+        value = y * silu(second[0:half, cols].astype(F32) * scale_main)
+        squares = squares + jnp.sum(value * value, -1, keepdims=True)
+        gated.append(value)
+    norm = lax.rsqrt(squares / 512 + EPS)
+    for head in range(4):
+        cols = slice(128 * head, 128 * head + 128)
+        out[:, cols] = (gated[head] * norm * params[4:5, cols]).astype(BF16)
+
+
+def mix(second, streams, maps, meta, prior, params, taps_c):
+    return pl.pallas_call(
+        mix_body,
+        out_shape=jax.ShapeDtypeStruct(streams.shape, BF16),
+        name="mix",
+    )(second, streams, maps, meta, prior, params, taps_c)
+
+
+def output_body(gathered, weight_mine, weight_other, crops, text, newline, out):
+    half = crops.shape[0]
+    top = lax.broadcasted_iota(jnp.int32, (half, 1), 0) == 0
+    tail = jnp.where(top, newline[...].astype(F32), text[...].astype(F32))
+    for index, hidden in enumerate((crops[...].astype(F32), tail)):
+        mixed = jnp.dot(gathered[index], weight_mine[...], preferred_element_type=F32)
+        mixed = mixed + jnp.dot(
+            gathered[2 + index], weight_other[...], preferred_element_type=F32
+        )
+        out[index * half : (index + 1) * half, :] = (hidden + mixed).astype(BF16)
+
+
+def output(gathered, weight_mine, weight_other, crops, text, newline):
+    section, columns = text.shape
+    half = section // 2
+    tile = columns // 4
+    inner = gathered.shape[2]
+    return pl.pallas_call(
+        output_body,
+        grid=(4,),
+        in_specs=[
+            pl.BlockSpec((4, half, inner), lambda i: (0, 0, 0)),
+            pl.BlockSpec((inner, tile), lambda i: (0, i)),
+            pl.BlockSpec((inner, tile), lambda i: (0, i)),
+            pl.BlockSpec((half, tile), lambda i: (0, i)),
+            pl.BlockSpec((half, tile), lambda i: (1, i)),
+            pl.BlockSpec((1, tile), lambda i: (0, i)),
+        ],
+        out_specs=pl.BlockSpec((section, tile), lambda i: (0, i)),
+        out_shape=jax.ShapeDtypeStruct((section, columns), BF16),
+        name="output",
+    )(gathered, weight_mine, weight_other, crops, text, newline)
+
+
+def per_device_halves(
+    text_embed, crop_feats, crop_dest, vision_gain, proj_weight, newline, norm_gain, xz_weight,
+    dt_weight, bc_weight, conv_x, conv_bc, dt_bias, a_log, skip, out_gain, out_weight,
+):
+    my_rank = lax.axis_index("dp")
+    my_chip = lax.axis_index("tensor")
+    my_segment = lax.axis_index("segment")
+    segment_count = lax.axis_size("segment")
+    text = text_embed[0]
+    section, columns = text.shape
+    half = section // 2
+    width = columns * lax.axis_size("tensor")
+    state_size = bc_weight.shape[1] // 2
+    feats = crop_feats[0, 0, 0]
+    feats_other = swapped(feats, "dp", 1)
+    text_other = swapped(text[half:], "dp", 1)
+    edge_mine = passed_along(text[section - 8 :], "segment", 1)
+    edge_other = swapped(edge_mine, "dp", 1)
+    weight_other = swapped(out_weight, "dp", 1)
+    stays = jnp.where(my_rank == 0, crop_dest[0, 0, 0] == 0, crop_dest[0, 1, 0] == 1)
+    crops = encode(
+        stays.astype(jnp.int32).reshape(1), feats, feats_other, vision_gain[None], proj_weight
+    )
+    dt_wide = jnp.pad(dt_weight, ((0, 0), (0, 128 - dt_weight.shape[1])))
+    first, second = project(
+        crops, text, text_other, edge_mine, edge_other, newline[None], norm_gain[None], xz_weight,
+        bc_weight, dt_wide,
+    )
+    own = jnp.concatenate(
+        [conv_x.astype(F32), out_gain.astype(F32)[None]]
+        + [jnp.broadcast_to(value[:, None], (1, 128)) for value in (dt_bias, a_log, skip)],
+        0,
+    )
+    own, first = lax.optimization_barrier((own, first))
+    params = lax.all_gather(own, "tensor", axis=1, tiled=True)
+    first = lax.psum_scatter(first, "tensor", scatter_dimension=0, tiled=False)
+    second = lax.psum_scatter(second, "tensor", scatter_dimension=0, tiled=False)
+    streams, maps, meta, state = scan(width, first, params, conv_bc[:, :state_size])
+    partner = swapped(state, "tensor", 1).astype(F32)
+    state = state.astype(F32)
+    late = my_chip % 2 == 1
+    early_state = jnp.where(late, partner, state)[:128]
+    late_state = jnp.where(late, state, partner)[:128]
+    early_decay = jnp.where(late, partner, state)[128:129]
+    late_decay = jnp.where(late, state, partner)[128:129]
+    whole = jnp.concatenate(
+        [
+            late_decay * early_state + late_state,
+            jnp.broadcast_to(early_decay * late_decay, (16, 512)),
+        ],
+        0,
+    ).astype(BF16)
+    others = [None] + [swapped(whole, "segment", bits) for bits in range(1, segment_count)]
+    prior = jnp.zeros((128, 512), F32)
+    for source in range(segment_count - 1):
+        bits = my_segment ^ source
+        piece = others[1]
+        for index in range(2, segment_count):
+            piece = jnp.where(bits == index, others[index], piece)
+        piece = piece.astype(F32)
+        prior = jnp.where(source < my_segment, piece[128:129] * prior + piece[:128], prior)
+    prior = jnp.where(late, early_decay * prior + early_state, prior)
+    normed = mix(second, streams, maps, meta, prior, params, conv_bc[:, state_size:])
+    normed = jnp.where(my_chip < 2, normed, swapped(normed, "dp", 1))
+    gathered = lax.all_gather(normed, "tensor", axis=0, tiled=False)
+    return output(gathered, out_weight, weight_other, crops, text, newline[None])[None]
+
+
+def per_device(*args):
+    text_embed, crop_feats = args[0], args[1]
+    sizes = tuple(lax.axis_size(axis) for axis in ("segment", "dp", "tensor"))
+    heads_dev = args[12].shape[0]
+    head_width = args[15].shape[0] // heads_dev
+    state_size = args[9].shape[1] // 2
+    fits = (
+        sizes == (4, 2, 4)
+        and heads_dev == 1
+        and (head_width, state_size) == (128, 128)
+        and crop_feats.shape[2:4] == (1, 256)
+        and text_embed.shape[1] == 512
+    )
+    return (per_device_halves if fits else per_device_any)(*args)
+
+
 def solution(mesh):
     return jax.shard_map(
         per_device,

time: 259 us -> 161 us (0.62)
  waiting for transfers between devices: 113 us -> 74.1 us
  Pallas kernels: 0 us -> 35.8 us
  matrix products: 32.6 us -> 0 us
  blocking collectives: 35.7 us -> 14 us
  other arithmetic: 24.9 us -> 3.62 us
  starting transfers between devices: 22.4 us -> 9.09 us
  local copies, waits for them, and re-layouts: 13.9 us -> 7.39 us
    pallas_call x0 -> x5, Pallas kernels: none -> 35.8 us  [the longest x1 15.1 us: project(): pl.pallas_call(project_body, grid=(5,), in_specs=[pl.BlockSpec((2 * half,...]
    reduce_scatter x2 -> x1, waiting for transfers between devices: 55.5 us -> 19.8 us  [per_device_halves(): first = lax.psum_scatter(first, 'tensor', scatter_dimension=0, tiled=False)]
    dot_general x9 -> x0, matrix products: 32.6 us -> none  [the longest x1 9.28 us: per_device(): jnp.dot(piece, xz_weight, preferred_element_type=jnp.float32)]
    psum x2 -> x0, blocking collectives: 23.4 us -> none  [the longest x1 13.4 us: per_device(): row_total = lax.psum(jnp.sum(wide * wide, -1), 'tensor')]
    all_gather x2 -> x1, waiting for transfers between devices: 42.9 us -> 26.3 us  [per_device_halves(): gathered = lax.all_gather(normed, 'tensor', axis=0, tiled=False)]
    all_gather x0 -> x1, blocking collectives: none -> 14 us  [per_device_halves(): params = lax.all_gather(own, 'tensor', axis=1, tiled=True)]
    ppermute x0 -> x9, waiting for transfers between devices: none -> 13.6 us  [swapped(): lax.ppermute(block, axis, [(i, i ^ bits) for i in range(lax.axis_size(axi...]
    unnamed x5 -> x4, waiting for transfers between devices: 0.08 us -> 12.9 us
  transfers between devices with their start and end apart: 10 -> 13, of which waited for: 10 -> 8; matrix products, arithmetic and copies ran while one was open for 8% -> 5% of each run, Pallas kernels for 0% -> 9%
where the time goes in v1:
time: 161 us
  waiting for transfers between devices  74.1 us (46%)
  Pallas kernels  35.8 us (22%)
  between operations  16.6 us (10%)
  blocking collectives  14 us (9%)
  starting transfers between devices  9.09 us (6%)
  local copies, waits for them, and re-layouts  7.39 us (5%)
  other arithmetic  3.62 us (2%)
    all_gather x1, waiting for transfers between devices, per_device_halves(): gathered = lax.all_gather(normed, 'tensor', axis=0, tiled=False)  26.3 us
    reduce_scatter x1, waiting for transfers between devices, per_device_halves(): first = lax.psum_scatter(first, 'tensor', scatter_dimension=0, tiled=False)  19.8 us
    pallas_call x1, Pallas kernels, project(): pl.pallas_call(project_body, grid=(5,), in_specs=[pl.BlockSpec((2 * half,...  15.1 us
    all_gather x1, blocking collectives, per_device_halves(): params = lax.all_gather(own, 'tensor', axis=1, tiled=True)  14 us
    ppermute x9, waiting for transfers between devices, swapped(): lax.ppermute(block, axis, [(i, i ^ bits) for i in range(lax.axis_size(axi...  13.6 us
    unnamed x4, waiting for transfers between devices  12.9 us
    pallas_call x1, Pallas kernels, encode(): pl.pallas_call(encode_body, grid=(4,), in_specs=[pl.BlockSpec(memory_spac...  7.28 us
    pallas_call x1, Pallas kernels, output(): pl.pallas_call(output_body, grid=(4,), in_specs=[pl.BlockSpec((4, half, i...  6.77 us
  transfers between devices with their start and end apart: 13, of which 8 were waited for; matrix products, arithmetic and copies ran while one was open for 5% of the time, Pallas kernels for 9%

profile of v1, /device:TPU:0, one launch (start us, length us, event | category | flops | bytes accessed | tf_op | source)
XLA Modules:
  0.0 160.6 jit_solution(14488467194619799710)
XLA Ops:
  6.6 1.4 slice_bitcast_fusion
  8.0 0.5 collective-permute-start.1
  8.6 0.8 slice_bitcast_fusion.1
  9.3 4.8 %collective-permute-start.2 = (bf16[8,2048]{1,0:T(8,128)(2,1)S(1)}, bf16[8,2048]{1,0:T(8,128)(2,1)S(1)}, u32[]{:S(2)}, u32[]{:S(2)}) collective-permute-start(bf16[8,2048]{1,0:T(8,128)(2,1)S(1)} %slice_bitcast_fusion.1), channel_id=1, source_target_pairs={{0,8},{8,16},{16,24},{1,9},{9,17},{17,25},{2,10},{10,18},{18,26},{... | collective-permute-start | bytes 98312 | tf_op jit(solution)/shard_map/ppermute | solution.py:17
  14.2 1.6 collective-permute-done.2.edge_mine
  15.7 0.6 fusion.5
  19.6 0.6 broadcast_in_dim.55.gain
  20.2 0.6 broadcast_in_dim.56.newline
  20.8 0.6 broadcast_in_dim.57.gain
  21.7 0.9 pad.4.dt
  22.7 7.3 %encode.1.crops = bf16[512,2048]{1,0:T(8,128)(2,1)} custom-call(s32[1]{0:T(128)} %bitcast.2.place, bf16[256,1280]{1,0:T(8,128)(2,1)} %bitcast.3.mine, bf16[256,1280]{1,0:T(8,128)(2,1)} %collective-permute-done.other, bf16[1,1280]{1,0:T(2,128)(2,1)} %broadcast_in_dim.55.gain, bf16[1280,2048]{1,0:T(8,128)(2,1)} %weight.1), custom_call_target="tpu_custom_call" | custom-call | tf_op jit(solution)/shard_map/encode/pallas_call | solution.py:226
  30.0 0.6 copy-done.3
  31.0 15.1 %project.1 = (bf16[4,272,640]{2,1,0:T(8,128)(2,1)}, bf16[4,264,640]{2,1,0:T(8,128)(2,1)}) custom-call(bf16[512,2048]{1,0:T(8,128)(2,1)} %encode.1.crops, bf16[512,2048]{1,0:T(8,128)(2,1)} %bitcast.28, bf16[256,2048]{1,0:T(8,128)(2,1)} %copy-done.1, bf16[8,2048]{1,0:T(8,128)(2,1)} %copy-done.2, bf16[8,2048]{1,0:T(8,128)(2,1)} %copy-done.3, ...), custom_call_target="tpu_custom_call" | custom-call | tf_op jit(solution)/shard_map/project/pallas_call | solution.py:311
  46.2 0.7 reduce-scatter.7.cloned.1.call-update
  47.0 0.6 fusion.4
  47.6 14.0 %all_gather.9.refs_1_.params = f32[8,512]{1,0:T(8,128)} all-gather(f32[8,128]{1,0:T(8,128)S(1)} %concatenate.7), channel_id=1, replica_groups=mesh['segment'=4,'dp'=2,'tensor'=4] {'tensor'}, dimensions={1}, use_global_device_ids=true | all-gather | bytes 20480 | tf_op jit(solution)/shard_map/all_gather | solution.py:523
  61.5 19.8 %reduce-scatter.5.cloned.1.call-done = bf16[1,272,640]{2,1,0:T(8,128)(2,1)} async-done(((bf16[4,272,640]{2,1,0:T(8,128)(2,1)}), bf16[1,272,640]{2,1,0:T(8,128)(2,1)}) %reduce-scatter.5.cloned.1.call-update) | async-done | bytes 348176 | tf_op jit(solution)/shard_map/reduce_scatter | solution.py:524
  81.3 3.3 %scan.1 = (bf16[256,512]{1,0:T(8,128)(2,1)}, bf16[256,128]{1,0:T(8,128)(2,1)}, f32[24,384]{1,0:T(8,128)}, bf16[144,512]{1,0:T(8,128)(2,1)}) custom-call(bf16[272,640]{1,0:T(8,128)(2,1)} %bitcast.31, f32[8,512]{1,0:T(8,128)} %all_gather.9.refs_1_.params, bf16[4,128]{1,0:T(4,128)(2,1)} %get-tuple-element.27.refs_2_), custom_call_target="tpu_custom_call" | custom-call | tf_op jit(solution)/shard_map/scan/pallas_call | solution.py:396
  84.6 5.7 %collective-permute-done.4 = bf16[144,512]{1,0:T(8,128)(2,1)S(1)} collective-permute-done((bf16[144,512]{1,0:T(8,128)(2,1)}, bf16[144,512]{1,0:T(8,128)(2,1)S(1)}, u32[]{:S(2)}, u32[]{:S(2)}) %collective-permute-start.4) | collective-permute-done | bytes 147488 | tf_op jit(solution)/shard_map/ppermute | solution.py:21
  90.3 1.0 convert_select_fusion.1
  91.4 1.6 collective-permute-start.7
  93.0 1.5 collective-permute-start.6
  94.5 0.5 collective-permute-start.5
  95.0 3.0 %collective-permute-done.7 = bf16[144,512]{1,0:T(8,128)(2,1)S(1)} collective-permute-done((bf16[144,512]{1,0:T(8,128)(2,1)S(1)}, bf16[144,512]{1,0:T(8,128)(2,1)S(1)}, u32[]{:S(2)}, u32[]{:S(2)}) %collective-permute-start.7) | collective-permute-done | bytes 147488 | tf_op jit(solution)/shard_map/ppermute | solution.py:21
  97.9 3.2 %collective-permute-done.6 = bf16[144,512]{1,0:T(8,128)(2,1)S(1)} collective-permute-done((bf16[144,512]{1,0:T(8,128)(2,1)S(1)}, bf16[144,512]{1,0:T(8,128)(2,1)S(1)}, u32[]{:S(2)}, u32[]{:S(2)}) %collective-permute-start.6) | collective-permute-done | bytes 147488 | tf_op jit(solution)/shard_map/ppermute | solution.py:21
  101.3 0.8 add_select_fusion.prior
  102.1 12.2 %reduce-scatter.7.cloned.1.call-done = bf16[1,264,640]{2,1,0:T(8,128)(2,1)} async-done(((bf16[4,264,640]{2,1,0:T(8,128)(2,1)}), bf16[1,264,640]{2,1,0:T(8,128)(2,1)}) %reduce-scatter.7.cloned.1.call-update) | async-done | bytes 337936
  114.3 3.3 %mix.1 = bf16[256,512]{1,0:T(8,128)(2,1)} custom-call(bf16[264,640]{1,0:T(8,128)(2,1)} %bitcast.32, bf16[256,512]{1,0:T(8,128)(2,1)} %get-tuple-element.17.streams, bf16[256,128]{1,0:T(8,128)(2,1)} %get-tuple-element.18.maps, f32[24,384]{1,0:T(8,128)} %get-tuple-element.19.meta, f32[128,512]{1,0:T(8,128)} %add_select_fusion.prior, ...), custom_call_target="tpu_custom_call" | custom-call | tf_op jit(solution)/shard_map/mix/pallas_call | solution.py:448
  117.6 1.7 %collective-permute-done.8 = bf16[256,512]{1,0:T(8,128)(2,1)S(1)} collective-permute-done((bf16[256,512]{1,0:T(8,128)(2,1)}, bf16[256,512]{1,0:T(8,128)(2,1)S(1)}, u32[]{:S(2)}, u32[]{:S(2)}) %collective-permute-start.8) | collective-permute-done | bytes 262176 | tf_op jit(solution)/shard_map/ppermute | solution.py:21
  119.3 1.7 %broadcast_select_fusion = bf16[256,512]{1,0:T(8,128)(2,1)} fusion(bf16[256,512]{1,0:T(8,128)(2,1)} %mix.1, bf16[256,512]{1,0:T(8,128)(2,1)S(1)} %collective-permute-done.8, pred[]{:T(512)S(6)} %lt.9), kind=kLoop, calls=%fused_computation.12 | loop fusion | flops 131072 | bytes 786433 | tf_op jit(solution)/shard_map/jit(_where)/select_n | solution.py:552
  121.1 26.3 %all-gather.3.cloned.1.call-done = bf16[1024,512]{1,0:T(8,128)(2,1)} async-done(((bf16[256,512]{1,0:T(8,128)(2,1)}), bf16[1024,512]{1,0:T(8,128)(2,1)}) %all-gather.3.cloned.1.call-update) | async-done | bytes 1048592 | tf_op jit(solution)/shard_map/all_gather | solution.py:553
  147.3 6.8 %output.1 = bf16[512,2048]{1,0:T(8,128)(2,1)} custom-call(bf16[4,256,512]{2,1,0:T(8,128)(2,1)} %bitcast.30, bf16[512,2048]{1,0:T(8,128)(2,1)} %weight_mine.1, bf16[512,2048]{1,0:T(8,128)(2,1)} %collective-permute-done.9.weight_other, bf16[512,2048]{1,0:T(8,128)(2,1)} %encode.1.crops, bf16[512,2048]{1,0:T(8,128)(2,1)} %bitcast.29, ...), custom_call_target="tpu_custom_call" | custom-call | tf_op jit(solution)/shard_map/output/pallas_call | solution.py:472
  (54 shorter events, 1.2 us)
Async XLA Ops:
  6.5 7.6 %copy-start.11 = (bf16[128]{0:T(256)(128)(2,1)S(1)}, bf16[128]{0:T(256)(128)(2,1)}, u32[]{:S(2)}) copy-start(bf16[128]{0:T(256)(128)(2,1)} %param.32) | copy-start | bytes 772
  6.5 9.2 %copy-start.9 = (s32[1,2,1]{1,2,0:T(1,128)S(1)}, s32[1,2,1]{1,2,0:T(1,128)}, u32[]{:S(2)}) copy-start(s32[1,2,1]{1,2,0:T(1,128)} %param.19) | copy-start | bytes 28
  6.5 13.1 %copy-start.7 = (bf16[1280]{0:T(1024)(128)(2,1)S(1)}, bf16[1280]{0:T(1024)(128)(2,1)}, u32[]{:S(2)}) copy-start(bf16[1280]{0:T(1024)(128)(2,1)} %param.20) | copy-start | bytes 7684
  6.5 13.7 %copy-start.5 = (bf16[2048]{0:T(1024)(128)(2,1)S(1)}, bf16[2048]{0:T(1024)(128)(2,1)}, u32[]{:S(2)}) copy-start(bf16[2048]{0:T(1024)(128)(2,1)} %param.22) | copy-start | bytes 12292
  6.5 14.3 %copy-start.6 = (bf16[2048]{0:T(1024)(128)(2,1)S(1)}, bf16[2048]{0:T(1024)(128)(2,1)}, u32[]{:S(2)}) copy-start(bf16[2048]{0:T(1024)(128)(2,1)} %param.23) | copy-start | bytes 12292
  6.5 14.9 %copy-start.4 = (bf16[2048,4]{0,1:T(4,128)(2,1)S(1)}, bf16[2048,4]{0,1:T(4,128)(2,1)}, u32[]{:S(2)}) copy-start(bf16[2048,4]{0,1:T(4,128)(2,1)} %param.25) | copy-start | bytes 49156
  6.6 16.1 %copy-start.10 = (bf16[4,128]{1,0:T(4,128)(2,1)S(1)}, bf16[4,128]{1,0:T(4,128)(2,1)}, u32[]{:S(2)}) copy-start(bf16[4,128]{1,0:T(4,128)(2,1)} %param.27) | copy-start | bytes 3076
  6.6 74.7 %reduce-scatter.5.cloned.1.call-start = ((), (), s32[]{:S(2)}) async-start(), calls=%async_computation.2 | async-start | bytes 1740800 | tf_op jit(solution)/shard_map/reduce_scatter | solution.py:524
  8.0 22.0 %collective-permute-start.1 = (bf16[256,2048]{1,0:T(8,128)(2,1)S(1)}, bf16[256,2048]{1,0:T(8,128)(2,1)S(1)}, u32[]{:S(2)}, u32[]{:S(2)}) collective-permute-start(bf16[256,2048]{1,0:T(8,128)(2,1)S(1)} %slice_bitcast_fusion), channel_id=1, source_target_pairs={{0,4},{4,0},{1,5},{5,1},{2,6},{6,2},{3,7},{7,3},{8,12},{12,8},{9,1... | collective-permute-start | bytes 3145736 | tf_op jit(solution)/shard_map/ppermute | solution.py:21
  8.5 14.2 %collective-permute-start = (bf16[256,1280]{1,0:T(8,128)(2,1)}, bf16[256,1280]{1,0:T(8,128)(2,1)}, u32[]{:S(2)}, u32[]{:S(2)}) collective-permute-start(bf16[256,1280]{1,0:T(8,128)(2,1)} %bitcast.3.mine), channel_id=1, source_target_pairs={{0,4},{4,0},{1,5},{5,1},{2,6},{6,2},{3,7},{7,3},{8,12},{12,8},{9,1... | collective-permute-start | bytes 1966088 | tf_op jit(solution)/shard_map/ppermute | solution.py:21
  9.3 6.4 %collective-permute-start.2 = (bf16[8,2048]{1,0:T(8,128)(2,1)S(1)}, bf16[8,2048]{1,0:T(8,128)(2,1)S(1)}, u32[]{:S(2)}, u32[]{:S(2)}) collective-permute-start(bf16[8,2048]{1,0:T(8,128)(2,1)S(1)} %slice_bitcast_fusion.1), channel_id=1, source_target_pairs={{0,8},{8,16},{16,24},{1,9},{9,17},{17,25},{2,10},{10,18},{18,26},{... | collective-permute-start | bytes 98312 | tf_op jit(solution)/shard_map/ppermute | solution.py:17
  15.7 14.2 %copy-start.2 = (bf16[8,2048]{1,0:T(8,128)(2,1)}, bf16[8,2048]{1,0:T(8,128)(2,1)S(1)}, u32[]{:S(2)}) copy-start(bf16[8,2048]{1,0:T(8,128)(2,1)S(1)} %collective-permute-done.2.edge_mine) | copy-start | bytes 98308
  15.7 14.2 %collective-permute-start.3 = (bf16[8,2048]{1,0:T(8,128)(2,1)S(1)}, bf16[8,2048]{1,0:T(8,128)(2,1)S(1)}, u32[]{:S(2)}, u32[]{:S(2)}) collective-permute-start(bf16[8,2048]{1,0:T(8,128)(2,1)S(1)} %collective-permute-done.2.edge_mine), channel_id=1, source_target_pairs={{0,4},{4,0},{1,5},{5,1},{2,6},{6,2},{3,7},{7,3},{8,12},{12,8},{9,1... | collective-permute-start | bytes 98312 | tf_op jit(solution)/shard_map/ppermute | solution.py:21
  30.0 0.6 copy-start.3
  30.0 1.0 copy-start.1
  46.1 0.8 copy-start.8
  46.2 48.8 %copy-start = (bf16[512,2048]{1,0:T(8,128)(2,1)S(1)}, bf16[512,2048]{1,0:T(8,128)(2,1)}, u32[]{:S(2)}) copy-start(bf16[512,2048]{1,0:T(8,128)(2,1)} %weight_mine.1) | copy-start | bytes 6291460
  46.2 68.1 %reduce-scatter.7.cloned.1.call-start = ((), (), s32[]{:S(2)}) async-start(), calls=%async_computation.4 | async-start | bytes 1689600
  46.9 100.4 %all-gather.3.cloned.1.call-start = ((), (), s32[]{:S(2)}) async-start(), calls=%async_computation.3 | async-start | bytes 1310720 | tf_op jit(solution)/shard_map/all_gather | solution.py:553
  84.6 5.7 %collective-permute-start.4 = (bf16[144,512]{1,0:T(8,128)(2,1)}, bf16[144,512]{1,0:T(8,128)(2,1)S(1)}, u32[]{:S(2)}, u32[]{:S(2)}) collective-permute-start(bf16[144,512]{1,0:T(8,128)(2,1)} %get-tuple-element.20), channel_id=1, source_target_pairs={{0,1},{1,0},{2,3},{3,2},{4,5},{5,4},{6,7},{7,6},{8,9},{9,8},{10,11... | collective-permute-start | bytes 442376 | tf_op jit(solution)/shard_map/ppermute | solution.py:21
  91.4 6.5 %collective-permute-start.7 = (bf16[144,512]{1,0:T(8,128)(2,1)S(1)}, bf16[144,512]{1,0:T(8,128)(2,1)S(1)}, u32[]{:S(2)}, u32[]{:S(2)}) collective-permute-start(bf16[144,512]{1,0:T(8,128)(2,1)S(1)} %pad_maximum_fusion), channel_id=1, source_target_pairs={{0,8},{8,0},{16,24},{24,16},{1,9},{9,1},{17,25},{25,17},{2,10},{10... | collective-permute-start | bytes 442376 | tf_op jit(solution)/shard_map/ppermute | solution.py:21
  93.0 8.2 %collective-permute-start.6 = (bf16[144,512]{1,0:T(8,128)(2,1)S(1)}, bf16[144,512]{1,0:T(8,128)(2,1)S(1)}, u32[]{:S(2)}, u32[]{:S(2)}) collective-permute-start(bf16[144,512]{1,0:T(8,128)(2,1)S(1)} %pad_maximum_fusion), channel_id=1, source_target_pairs={{0,16},{8,24},{16,0},{24,8},{1,17},{9,25},{17,1},{25,9},{2,18},{10... | collective-permute-start | bytes 442376 | tf_op jit(solution)/shard_map/ppermute | solution.py:21
  94.5 6.7 %collective-permute-start.5 = (bf16[144,512]{1,0:T(8,128)(2,1)S(1)}, bf16[144,512]{1,0:T(8,128)(2,1)S(1)}, u32[]{:S(2)}, u32[]{:S(2)}) collective-permute-start(bf16[144,512]{1,0:T(8,128)(2,1)S(1)} %pad_maximum_fusion), channel_id=1, source_target_pairs={{0,24},{8,16},{16,8},{24,0},{1,25},{9,17},{17,9},{25,1},{2,26},{10... | collective-permute-start | bytes 442376 | tf_op jit(solution)/shard_map/ppermute | solution.py:21
  95.0 26.1 %collective-permute-start.9 = (bf16[512,2048]{1,0:T(8,128)(2,1)S(1)}, bf16[512,2048]{1,0:T(8,128)(2,1)}, u32[]{:S(2)}, u32[]{:S(2)}) collective-permute-start(bf16[512,2048]{1,0:T(8,128)(2,1)S(1)} %copy-done), channel_id=1, source_target_pairs={{0,4},{4,0},{1,5},{5,1},{2,6},{6,2},{3,7},{7,3},{8,12},{12,8},{9,1... | collective-permute-start | bytes 6291464 | tf_op jit(solution)/shard_map/ppermute | solution.py:21
  117.6 1.7 %collective-permute-start.8 = (bf16[256,512]{1,0:T(8,128)(2,1)}, bf16[256,512]{1,0:T(8,128)(2,1)S(1)}, u32[]{:S(2)}, u32[]{:S(2)}) collective-permute-start(bf16[256,512]{1,0:T(8,128)(2,1)} %mix.1), channel_id=1, source_target_pairs={{0,4},{4,0},{1,5},{5,1},{2,6},{6,2},{3,7},{7,3},{8,12},{12,8},{9,1... | collective-permute-start | bytes 786440 | tf_op jit(solution)/shard_map/ppermute | solution.py:21
Sparse Core Ops, SparseCore 0:
  46.3 34.9 reduce-scatter.4
  83.6 30.5 reduce-scatter.6
  121.2 26.1 all-gather.2

commit v2 on v1

--- a/solution.py
+++ b/solution.py
@@ -203,140 +203,145 @@
     return a / (1.0 + jnp.exp(-a))
 
 
-def encode_body(place, mine, other, gain, weight, out, normed):
-    rows = mine.shape[0]
-
-    @pl.when(pl.program_id(0) == 0)
-    def _():
-        stays = place[0] == 1
-        for index, (a, b) in enumerate(((mine, other), (other, mine))):
-            feats = jnp.where(stays, a[...], b[...]).astype(F32)
-            scale = lax.rsqrt(jnp.mean(feats * feats, -1, keepdims=True) + EPS)
-            normed[index * rows : (index + 1) * rows, :] = (
-                feats * scale * gain[...].astype(F32)
-            ).astype(BF16)
-
-    out[...] = jnp.dot(normed[...], weight[...], preferred_element_type=F32).astype(BF16)
-
-
-def encode(place, mine, other, gain, weight):
-    rows, width = mine.shape
-    columns = weight.shape[1]
-    tile = columns // 4
+def enter_body(
+    table, feats_mine, feats_other, vision_gain, proj, text, text_other, edge_mine, edge_other,
+    newline, gain, xz, bc, dt, crops_out, first_out, second_out,
+    feats, normed, proj_tiles, tails, weights, crops, rows, first, second, sems, out_sems,
+):
+    half = tails.shape[1]
+    span = half + 16
+    tiles, _, tile = proj_tiles.shape
+    arrivals = [
+        pltpu.make_async_copy(feats_mine, feats.at[0], sems.at[0]),
+        pltpu.make_async_copy(feats_other, feats.at[1], sems.at[1]),
+    ]
+    arrivals += [
+        pltpu.make_async_copy(proj.at[:, pl.ds(i * tile, tile)], proj_tiles.at[i], sems.at[2 + i])
+        for i in range(tiles)
+    ]
+    arrivals += [
+        pltpu.make_async_copy(text.at[pl.ds(half, half), :], tails.at[0], sems.at[2 + tiles]),
+        pltpu.make_async_copy(text_other, tails.at[1], sems.at[3 + tiles]),
+        pltpu.make_async_copy(bc, weights.at[4], sems.at[4 + tiles]),
+    ]
+    arrivals += [
+        pltpu.make_async_copy(
+            xz.at[:, pl.ds(i * 256, 256)], weights.at[i], sems.at[5 + tiles + i]
+        )
+        for i in range(4)
+    ]
+    for copy in arrivals:
+        copy.start()
+    gain_row = gain[...].reshape(1, -1)
+    rank = lax.axis_index("dp")
+    stays = table[0, rank, 0] == rank
+    arrivals[0].wait()
+    arrivals[1].wait()
+    for index in range(2):
+        block = jnp.where(stays, feats[index], feats[1 - index]).astype(F32)
+        scale = lax.rsqrt(jnp.mean(block * block, -1, keepdims=True) + EPS)
+        normed[index * half : (index + 1) * half, :] = (
+            block * scale * vision_gain[...].reshape(1, -1).astype(F32)
+        ).astype(BF16)
+    departures = []
+    for i in range(tiles):
+        arrivals[2 + i].wait()
+        cols = slice(i * tile, (i + 1) * tile)
+        result = jnp.dot(normed[...], proj_tiles[i], preferred_element_type=F32).astype(BF16)
+        crops[:, cols] = result
+        scaled = result * gain_row[:, cols]
+        rows[0:half, cols] = scaled[:half]
+        rows[2 * span : 2 * span + half, cols] = scaled[half:]
+    departures.append(pltpu.make_async_copy(crops, crops_out, out_sems.at[0]))
+    departures[-1].start()
+    top = lax.broadcasted_iota(jnp.int32, (8, 1), 0) == 0
+    ones = jnp.ones((8, rows.shape[1]), BF16)
+    sums = []
+    for part in range(4):
+        index = part // 2
+        base = part * span
+        if part % 2 == 0:
+            main = crops[index * half : (index + 1) * half, :]
+            edge = (edge_mine, edge_other)[index][...]
+        else:
+            arrivals[2 + tiles + index].wait()
+            head = tails[index, 0:8, :].astype(F32)
+            line = newline[...].reshape(1, -1).astype(F32)
+            tails[index, 0:8, :] = jnp.where(top, line, head).astype(BF16)
+            main = tails[index]
+            rows[base : base + half, :] = main * gain_row
+            edge = crops[(index + 1) * half - 8 : (index + 1) * half, :]
+        wide = edge.astype(F32)
+        last = jnp.concatenate([wide, jnp.zeros_like(wide)], 0).astype(BF16)
+        rows[base + half : base + span, :] = last * gain_row
+        sums.append(
+            jnp.concatenate(
+                [
+                    contract(ones, main * main, ((1,), (1,))),
+                    contract(ones, last * last, ((1,), (1,))),
+                ],
+                1,
+            )
+        )
+    for i in (4, 0, 1, 2, 3):
+        arrivals[5 + tiles + i if i < 4 else 4 + tiles].wait()
+        result = jnp.dot(rows[...], weights[i], preferred_element_type=F32).astype(BF16)
+        for part in range(4):
+            block = result[part * span : (part + 1) * span]
+            if i == 4:
+                first[part, :, 512:768] = block
+            else:
+                cols = slice(128 * i, 128 * i + 128)
+                first[part, :, cols] = block[:, 0:128]
+                second[part, :, cols] = block[0:half, 128:256]
+    for part in range(4):
+        steps = contract(dt[...], rows[part * span : (part + 1) * span, :], ((1,), (1,)))
+        both = jnp.concatenate([steps[0:4], sums[part][4:8]], 0)
+        first[part, half + 8 : span, 0:span] = both.astype(BF16)
+    for source, target, i in ((first, first_out, 1), (second, second_out, 2)):
+        departures.append(pltpu.make_async_copy(source, target, out_sems.at[i]))
+        departures[-1].start()
+    for copy in departures:
+        copy.wait()
+
+
+def enter(
+    table, feats_mine, feats_other, vision_gain, proj, text, text_other, edge_mine, edge_other,
+    newline, gain, xz, bc, dt,
+):
+    half, vision = feats_mine.shape
+    columns = text.shape[1]
+    tiles = 4
+    whole = pl.BlockSpec(memory_space=pl.ANY)
+    near = pl.BlockSpec(memory_space=pltpu.VMEM)
     return pl.pallas_call(
-        encode_body,
-        grid=(4,),
-        in_specs=[
-            pl.BlockSpec(memory_space=pltpu.SMEM),
-            pl.BlockSpec((rows, width), lambda i: (0, 0)),
-            pl.BlockSpec((rows, width), lambda i: (0, 0)),
-            pl.BlockSpec((1, width), lambda i: (0, 0)),
-            pl.BlockSpec((width, tile), lambda i: (0, i)),
-        ],
-        out_specs=pl.BlockSpec((2 * rows, tile), lambda i: (0, i)),
-        out_shape=jax.ShapeDtypeStruct((2 * rows, columns), BF16),
-        scratch_shapes=[pltpu.VMEM((2 * rows, width), BF16)],
-        name="encode",
-    )(place, mine, other, gain, weight)
-
-
-def project_body(
-    crops, text_mine, text_other, edge_mine, edge_other, newline, gain, xz, bc, dt, first, second,
-    rows, meta,
-):
-    half = text_mine.shape[0]
-    step = pl.program_id(0)
-
-    @pl.when(step == 0)
-    def _():
-        scale = gain[...].astype(F32)
-        top = lax.broadcasted_iota(jnp.int32, (half, 1), 0) == 0
-        line = newline[...].astype(F32)
-        pick = (
-            lax.broadcasted_iota(jnp.int32, (8, 128), 0)
-            == lax.broadcasted_iota(jnp.int32, (8, 128), 1)
-        ).astype(F32)
-        lane = lax.broadcasted_iota(jnp.int32, (half + 16, 128), 1)
-        for part in range(4):
-            base = (part // 2) * half
-            if part % 2 == 0:
-                main = crops[base : base + half, :].astype(F32)
-                edge = (edge_mine, edge_other)[part // 2][...].astype(F32)
-            else:
-                main = (text_mine, text_other)[part // 2][...].astype(F32)
-                main = jnp.where(top, line, main)
-                edge = crops[base + half - 16 : base + half, :].astype(F32)[8:]
-            rows[part, 0:half, :] = (main * scale).astype(BF16)
-            rows[part, half : half + 16, :] = jnp.concatenate(
-                [edge * scale, jnp.zeros_like(edge)], 0
-            ).astype(BF16)
-            squares = jnp.concatenate(
-                [
-                    jnp.sum(main * main, -1, keepdims=True),
-                    jnp.sum(edge * edge, -1, keepdims=True),
-                    jnp.zeros((8, 1), F32),
-                ],
-                0,
-            )
-            steps = jnp.dot(rows[part], dt[...], preferred_element_type=F32)
-            both = jnp.where(lane == 4, squares, steps)
-            across = contract(pick, both, ((1,), (1,)), HIGHEST).astype(BF16)
-            meta[part, 0] = across[:, 0:128]
-            meta[part, 1] = across[:, 128:256]
-            meta[part, 2] = jnp.concatenate(
-                [across[:, half : half + 16], jnp.zeros((8, 112), BF16)], 1
-            )
-            meta[part, 3] = jnp.zeros((8, 128), BF16)
-            meta[part, 4] = jnp.zeros((8, 128), BF16)
-
-    def write(weight):
-        for part in range(4):
-            result = jnp.dot(rows[part], weight, preferred_element_type=F32).astype(BF16)
-            first[part, 0 : half + 8, :] = result[0 : half + 8, 0:128]
-            first[part, half + 8 : half + 16, :] = meta[part, step]
-            second[part] = result[0 : half + 8, 128:256]
-
-    @pl.when(step < 4)
-    def _():
-        write(xz[...])
-
-    @pl.when(step == 4)
-    def _():
-        write(bc[...])
-
-
-def project(crops, text, text_other, edge_mine, edge_other, newline, gain, xz, bc, dt):
-    section, columns = text.shape
-    half = section // 2
-    return pl.pallas_call(
-        project_body,
-        grid=(5,),
-        in_specs=[
-            pl.BlockSpec((2 * half, columns), lambda i: (0, 0)),
-            pl.BlockSpec((half, columns), lambda i: (1, 0)),
-            pl.BlockSpec((half, columns), lambda i: (0, 0)),
-            pl.BlockSpec((8, columns), lambda i: (0, 0)),
-            pl.BlockSpec((8, columns), lambda i: (0, 0)),
-            pl.BlockSpec((1, columns), lambda i: (0, 0)),
-            pl.BlockSpec((1, columns), lambda i: (0, 0)),
-            pl.BlockSpec((columns, 256), lambda i: (0, jnp.minimum(i, 3))),
-            pl.BlockSpec((columns, 256), lambda i: (0, 0)),
-            pl.BlockSpec((columns, 128), lambda i: (0, 0)),
-        ],
-        out_specs=[
-            pl.BlockSpec((4, half + 16, 128), lambda i: (0, 0, i)),
-            pl.BlockSpec((4, half + 8, 128), lambda i: (0, 0, i)),
-        ],
+        enter_body,
+        in_specs=[pl.BlockSpec(memory_space=pltpu.SMEM), whole, whole, near, whole, whole, whole]
+        + [near, near, near, near, whole, whole, near],
+        out_specs=[whole, whole, whole],
         out_shape=[
-            jax.ShapeDtypeStruct((4, half + 16, 640), BF16),
-            jax.ShapeDtypeStruct((4, half + 8, 640), BF16),
+            jax.ShapeDtypeStruct((2 * half, columns), BF16),
+            jax.ShapeDtypeStruct((4, half + 16, 768), BF16),
+            jax.ShapeDtypeStruct((4, half, 512), BF16),
         ],
         scratch_shapes=[
-            pltpu.VMEM((4, half + 16, columns), BF16),
-            pltpu.VMEM((4, 5, 8, 128), BF16),
+            pltpu.VMEM((2, half, vision), BF16),
+            pltpu.VMEM((2 * half, vision), BF16),
+            pltpu.VMEM((tiles, vision, columns // tiles), BF16),
+            pltpu.VMEM((2, half, columns), BF16),
+            pltpu.VMEM((5, columns, 256), BF16),
+            pltpu.VMEM((2 * half, columns), BF16),
+            pltpu.VMEM((4 * (half + 16), columns), BF16),
+            pltpu.VMEM((4, half + 16, 768), BF16),
+            pltpu.VMEM((4, half, 512), BF16),
+            pltpu.SemaphoreType.DMA((9 + tiles,)),
+            pltpu.SemaphoreType.DMA((3,)),
         ],
-        name="project",
-    )(crops, text, text_other, edge_mine, edge_other, newline, gain, xz, bc, dt)
+        name="enter",
+    )(
+        table, feats_mine, feats_other, vision_gain, proj, text, text_other, edge_mine, edge_other,
+        newline, gain, xz, bc, dt,
+    )
 
 
 def filtered(main, edge, taps):
@@ -349,7 +354,7 @@
     return total
 
 
-def scan_body(width, first, params, taps_b, streams, maps, meta, state):
+def scan_body(width, first, params, taps_maps, streams, maps, meta, state):
     half = first.shape[0] - 16
     sums = first[half : half + 16, 0 : half + 128].astype(F32)[8:16]
     scale = lax.rsqrt(sums[4:5] / width + EPS)
@@ -373,69 +378,76 @@
     taps_x = params[0:4, :]
     edge = first[half : half + 16, :].astype(F32)[0:8] * scale_edge
     x = silu(filtered(first[0:half, 0:512].astype(F32) * scale_main, edge[:, 0:512], taps_x))
-    b = silu(
+    both = silu(
         filtered(
-            first[0:half, 512:640].astype(F32) * scale_main, edge[:, 512:640], taps_b[...].astype(F32)
+            first[0:half, 512:768].astype(F32) * scale_main,
+            edge[:, 512:768],
+            taps_maps[...].astype(F32),
         )
-    )
+    ).astype(BF16)
     carried = contract(columns_of(carry), owner, ((1,), (0,)), HIGHEST)
-    b16 = b.astype(BF16)
-    state[0:128, :] = contract(b16, (x * carried).astype(BF16), ((0,), (0,))).astype(BF16)
+    state[0:128, :] = contract(both[:, 0:128], (x * carried).astype(BF16), ((0,), (0,))).astype(BF16)
     total = jnp.sum(jnp.exp(final) * owner, 0, keepdims=True)
     state[128:144, :] = jnp.broadcast_to(total, (16, 512)).astype(BF16)
     streams[...] = x.astype(BF16)
-    maps[...] = b16
-    meta[0:8, 0:half] = cumulative
-    meta[8:16, 0:half] = step
-    meta[16:24, 0:half] = jnp.broadcast_to(scale[:, 0:half], (8, half))
-    meta[0:8, half : half + 128] = jnp.broadcast_to(scale[:, half : half + 128], (8, 128))
-
-
-def scan(width, first, params, taps_b):
+    maps[...] = both
+    meta[0:8, :] = cumulative
+    meta[8:16, :] = step
+    meta[16:24, :] = jnp.broadcast_to(scale[:, 0:half], (8, half))
+
+
+def scan(width, first, params, taps_maps):
     half = first.shape[0] - 16
     return pl.pallas_call(
         lambda *refs: scan_body(width, *refs),
         out_shape=[
             jax.ShapeDtypeStruct((half, 512), BF16),
-            jax.ShapeDtypeStruct((half, 128), BF16),
-            jax.ShapeDtypeStruct((24, half + 128), F32),
+            jax.ShapeDtypeStruct((half, 256), BF16),
+            jax.ShapeDtypeStruct((24, half), F32),
             jax.ShapeDtypeStruct((144, 512), BF16),
         ],
         name="scan",
-    )(first, params, taps_b)
-
-
-def mix_body(second, streams, maps, meta, prior, params, taps_c, out):
+    )(first, params, taps_maps)
+
+
+def inside_body(streams, maps, meta, params, out):
     half = streams.shape[0]
-    cumulative = meta[0:8, 0:half]
-    step = meta[8:16, 0:half]
+    cumulative = meta[0:8, :]
+    step = meta[8:16, :]
     cum_cols = columns_of(cumulative)
-    scale_main = columns_of(meta[16:24, 0:half])[:, 0:1]
-    scale_edge = columns_of(meta[0:8, half : half + 128])[0:8, 0:1]
-    both = second[half - 8 : half + 8, 512:640].astype(F32)[8:16] * scale_edge
-    c = silu(
-        filtered(second[0:half, 512:640].astype(F32) * scale_main, both, taps_c[...].astype(F32))
-    ).astype(BF16)
-    scores = contract(c, maps[...], ((1,), (1,)))
+    scores = contract(maps[:, 128:256], maps[:, 0:128], ((1,), (1,)))
     lower = lax.broadcasted_iota(jnp.int32, (half, half), 0) >= lax.broadcasted_iota(
         jnp.int32, (half, half), 1
     )
-    across = jnp.dot(c, prior[...].astype(BF16), preferred_element_type=F32)
+    scores = jnp.where(lower, scores, 0.0)
+    for head in range(4):
+        cols = slice(128 * head, 128 * head + 128)
+        x = streams[:, cols]
+        gaps = cum_cols[:, head : head + 1] - cumulative[head : head + 1]
+        weights = jnp.exp(jnp.where(lower, gaps, 0.0)) * scores * step[head : head + 1]
+        y = jnp.dot(weights.astype(BF16), x, preferred_element_type=F32)
+        out[:, cols] = y + params[7:8, cols] * x.astype(F32)
+
+
+def inside(streams, maps, meta, params):
+    return pl.pallas_call(
+        inside_body,
+        out_shape=jax.ShapeDtypeStruct(streams.shape, F32),
+        name="inside",
+    )(streams, maps, meta, params)
+
+
+def gate_body(second, local, maps, meta, prior, params, out):
+    half = local.shape[0]
+    scale = columns_of(meta[16:24, :])[:, 0:1]
+    entry = jnp.exp(columns_of(meta[0:8, :]))
+    across = jnp.dot(maps[:, 128:256], prior[...].astype(BF16), preferred_element_type=F32)
     gated = []
     squares = jnp.zeros((half, 1), F32)
     for head in range(4):
         cols = slice(128 * head, 128 * head + 128)
-        x = streams[:, cols]
-        gaps = cum_cols[:, head : head + 1] - cumulative[head : head + 1]
-        weights = (
-            jnp.where(lower, jnp.exp(jnp.where(lower, gaps, 0.0)), 0.0)
-            * scores
-            * step[head : head + 1]
-        )
-        y = jnp.dot(weights.astype(BF16), x, preferred_element_type=F32)
-        y = y + jnp.exp(cum_cols[:, head : head + 1]) * across[:, cols]
-        y = y + params[7:8, cols] * x.astype(F32)
-        value = y * silu(second[0:half, cols].astype(F32) * scale_main)
+        y = local[:, cols] + entry[:, head : head + 1] * across[:, cols]
+        value = y * silu(second[:, cols].astype(F32) * scale)
         squares = squares + jnp.sum(value * value, -1, keepdims=True)
         gated.append(value)
     norm = lax.rsqrt(squares / 512 + EPS)
@@ -444,18 +456,18 @@
         out[:, cols] = (gated[head] * norm * params[4:5, cols]).astype(BF16)
 
 
-def mix(second, streams, maps, meta, prior, params, taps_c):
+def gate(second, local, maps, meta, prior, params):
     return pl.pallas_call(
-        mix_body,
-        out_shape=jax.ShapeDtypeStruct(streams.shape, BF16),
-        name="mix",
-    )(second, streams, maps, meta, prior, params, taps_c)
+        gate_body,
+        out_shape=jax.ShapeDtypeStruct(local.shape, BF16),
+        name="gate",
+    )(second, local, maps, meta, prior, params)
 
 
 def output_body(gathered, weight_mine, weight_other, crops, text, newline, out):
     half = crops.shape[0]
     top = lax.broadcasted_iota(jnp.int32, (half, 1), 0) == 0
-    tail = jnp.where(top, newline[...].astype(F32), text[...].astype(F32))
+    tail = jnp.where(top, newline[...].reshape(1, -1).astype(F32), text[...].astype(F32))
     for index, hidden in enumerate((crops[...].astype(F32), tail)):
         mixed = jnp.dot(gathered[index], weight_mine[...], preferred_element_type=F32)
         mixed = mixed + jnp.dot(
@@ -478,7 +490,7 @@
             pl.BlockSpec((inner, tile), lambda i: (0, i)),
             pl.BlockSpec((half, tile), lambda i: (0, i)),
             pl.BlockSpec((half, tile), lambda i: (1, i)),
-            pl.BlockSpec((1, tile), lambda i: (0, i)),
+            pl.BlockSpec((tile,), lambda i: (i,)),
         ],
         out_specs=pl.BlockSpec((section, tile), lambda i: (0, i)),
         out_shape=jax.ShapeDtypeStruct((section, columns), BF16),
@@ -490,7 +502,6 @@
     text_embed, crop_feats, crop_dest, vision_gain, proj_weight, newline, norm_gain, xz_weight,
     dt_weight, bc_weight, conv_x, conv_bc, dt_bias, a_log, skip, out_gain, out_weight,
 ):
-    my_rank = lax.axis_index("dp")
     my_chip = lax.axis_index("tensor")
     my_segment = lax.axis_index("segment")
     segment_count = lax.axis_size("segment")
@@ -498,21 +509,15 @@
     section, columns = text.shape
     half = section // 2
     width = columns * lax.axis_size("tensor")
-    state_size = bc_weight.shape[1] // 2
     feats = crop_feats[0, 0, 0]
     feats_other = swapped(feats, "dp", 1)
     text_other = swapped(text[half:], "dp", 1)
     edge_mine = passed_along(text[section - 8 :], "segment", 1)
     edge_other = swapped(edge_mine, "dp", 1)
     weight_other = swapped(out_weight, "dp", 1)
-    stays = jnp.where(my_rank == 0, crop_dest[0, 0, 0] == 0, crop_dest[0, 1, 0] == 1)
-    crops = encode(
-        stays.astype(jnp.int32).reshape(1), feats, feats_other, vision_gain[None], proj_weight
-    )
-    dt_wide = jnp.pad(dt_weight, ((0, 0), (0, 128 - dt_weight.shape[1])))
-    first, second = project(
-        crops, text, text_other, edge_mine, edge_other, newline[None], norm_gain[None], xz_weight,
-        bc_weight, dt_wide,
+    crops, first, second = enter(
+        crop_dest, feats, feats_other, vision_gain, proj_weight, text, text_other, edge_mine,
+        edge_other, newline, norm_gain, xz_weight, bc_weight, dt_weight.T,
     )
     own = jnp.concatenate(
         [conv_x.astype(F32), out_gain.astype(F32)[None]]
@@ -523,7 +528,8 @@
     params = lax.all_gather(own, "tensor", axis=1, tiled=True)
     first = lax.psum_scatter(first, "tensor", scatter_dimension=0, tiled=False)
     second = lax.psum_scatter(second, "tensor", scatter_dimension=0, tiled=False)
-    streams, maps, meta, state = scan(width, first, params, conv_bc[:, :state_size])
+    streams, maps, meta, state = scan(width, first, params, conv_bc)
+    local = inside(streams, maps, meta, params)
     partner = swapped(state, "tensor", 1).astype(F32)
     state = state.astype(F32)
     late = my_chip % 2 == 1
@@ -548,10 +554,12 @@
         piece = piece.astype(F32)
         prior = jnp.where(source < my_segment, piece[128:129] * prior + piece[:128], prior)
     prior = jnp.where(late, early_decay * prior + early_state, prior)
-    normed = mix(second, streams, maps, meta, prior, params, conv_bc[:, state_size:])
-    normed = jnp.where(my_chip < 2, normed, swapped(normed, "dp", 1))
+    normed = gate(second, local, maps, meta, prior, params)
+    normed = lax.ppermute(
+        normed, ("dp", "tensor"), [(i, i if i % 4 < 2 else i ^ 4) for i in range(8)]
+    )
     gathered = lax.all_gather(normed, "tensor", axis=0, tiled=False)
-    return output(gathered, out_weight, weight_other, crops, text, newline[None])[None]
+    return output(gathered, out_weight, weight_other, crops, text, newline)[None]
 
 
 def per_device(*args):

time: 161 us -> 157 us (0.975)
  local copies, waits for them, and re-layouts: 7.39 us -> 4.71 us
  waiting for transfers between devices: 74.1 us -> 71.6 us
  starting transfers between devices: 9.09 us -> 11.2 us
  Pallas kernels: 35.8 us -> 37.8 us
  other arithmetic: 3.62 us -> 1.93 us
    unnamed x4 -> x3, waiting for transfers between devices: 12.9 us -> 0.73 us
    reduce_scatter x0 -> x1, waiting for transfers between devices: none -> 8.74 us  [per_device_halves(): lax.psum_scatter(second, 'tensor', scatter_dimension=0, tiled=False)]
    ppermute x9 -> x8, waiting for transfers between devices: 13.6 us -> 7.58 us  [swapped(): lax.ppermute(block, axis, [(i, i ^ bits) for i in range(lax.axis_size(axi...]
    reduce_scatter x1, waiting for transfers between devices: 19.8 us -> 24.2 us  [per_device_halves(): first = lax.psum_scatter(first, 'tensor', scatter_dimension=0, tiled=False)]
    all_gather x1, waiting for transfers between devices: 26.3 us -> 28.8 us  [per_device_halves(): gathered = lax.all_gather(normed, 'tensor', axis=0, tiled=False)]
    pallas_call x3, Pallas kernels: 25.7 us -> 27.7 us  [the longest x1 22 us: enter(): pl.pallas_call(enter_body, in_specs=[pl.BlockSpec(memory_space=pltpu.SMEM...]
    broadcast_in_dim x3 -> x0, local copies, waits for them, and re-layouts: 1.8 us -> none  [the longest x1 0.6 us: per_device_halves(): newline[None]]
    select_n x1 -> x0, other arithmetic: 1.68 us -> none  [per_device_halves(): normed = jnp.where(my_chip < 2, normed, swapped(normed, 'dp', 1))]
  transfers between devices with their start and end apart: 13 -> 13, of which waited for: 8 -> 7; matrix products, arithmetic and copies ran while one was open for 5% -> 2% of each run, Pallas kernels for 9% -> 6%
where the time goes in v2:
time: 157 us
  waiting for transfers between devices  71.6 us (46%)
  Pallas kernels  37.8 us (24%)
  between operations  15.3 us (10%)
  blocking collectives  14.3 us (9%)
  starting transfers between devices  11.2 us (7%)
  local copies, waits for them, and re-layouts  4.71 us (3%)
  other arithmetic  1.93 us (1%)
    all_gather x1, waiting for transfers between devices, per_device_halves(): gathered = lax.all_gather(normed, 'tensor', axis=0, tiled=False)  28.8 us
    reduce_scatter x1, waiting for transfers between devices, per_device_halves(): first = lax.psum_scatter(first, 'tensor', scatter_dimension=0, tiled=False)  24.2 us
    pallas_call x1, Pallas kernels, enter(): pl.pallas_call(enter_body, in_specs=[pl.BlockSpec(memory_space=pltpu.SMEM...  22 us
    all_gather x1, blocking collectives, per_device_halves(): params = lax.all_gather(own, 'tensor', axis=1, tiled=True)  14.3 us
    reduce_scatter x1, waiting for transfers between devices, per_device_halves(): lax.psum_scatter(second, 'tensor', scatter_dimension=0, tiled=False)  8.74 us
    ppermute x8, waiting for transfers between devices, swapped(): lax.ppermute(block, axis, [(i, i ^ bits) for i in range(lax.axis_size(axi...  7.58 us
    pallas_call x1, Pallas kernels, output(): pl.pallas_call(output_body, grid=(4,), in_specs=[pl.BlockSpec((4, half, i...  6.78 us
    ppermute x1, starting transfers between devices, passed_along(): return lax.ppermute(block, axis, route)  4.8 us
  transfers between devices with their start and end apart: 13, of which 7 were waited for; matrix products, arithmetic and copies ran while one was open for 2% of the time, Pallas kernels for 6%

profile of v2, /device:TPU:0, one launch (start us, length us, event | category | flops | bytes accessed | tf_op | source)
XLA Modules:
  0.0 156.8 jit_solution(12434112895500310879)
XLA Ops:
  6.6 1.4 slice_bitcast_fusion
  7.9 0.5 collective-permute-start.1
  8.5 0.1 collective-permute-start
  8.5 0.8 slice_bitcast_fusion.1
  9.3 4.8 %collective-permute-start.2 = (bf16[8,2048]{1,0:T(8,128)(2,1)S(1)}, bf16[8,2048]{1,0:T(8,128)(2,1)S(1)}, u32[]{:S(2)}, u32[]{:S(2)}) collective-permute-start(bf16[8,2048]{1,0:T(8,128)(2,1)S(1)} %slice_bitcast_fusion.1), channel_id=1, source_target_pairs={{0,8},{8,16},{16,24},{1,9},{9,17},{17,25},{2,10},{10,18},{18,26},{... | collective-permute-start | bytes 98312 | tf_op jit(solution)/shard_map/ppermute | solution.py:17
  14.1 1.6 %collective-permute-done.2.edge_mine = bf16[8,2048]{1,0:T(8,128)(2,1)S(1)} collective-permute-done((bf16[8,2048]{1,0:T(8,128)(2,1)S(1)}, bf16[8,2048]{1,0:T(8,128)(2,1)S(1)}, u32[]{:S(2)}, u32[]{:S(2)}) %collective-permute-start.2) | collective-permute-done | bytes 32800 | tf_op jit(solution)/shard_map/ppermute | solution.py:17
  15.7 0.7 copy.18.table
  18.5 0.5 copy-done.6
  19.0 0.3 copy-done.3
  19.3 0.3 copy-done.1
  19.6 22.0 %enter.1 = (bf16[512,2048]{1,0:T(8,128)(2,1)}, bf16[4,272,768]{2,1,0:T(8,128)(2,1)}, bf16[4,256,512]{2,1,0:T(8,128)(2,1)}) custom-call(s32[1,2,1]{2,1,0:T(2,128)} %copy.18.table, bf16[256,1280]{1,0:T(8,128)(2,1)} %bitcast.28, bf16[256,1280]{1,0:T(8,128)(2,1)} %copy-done.3, bf16[1280]{0:T(1024)(128)(2,1)} %vision_gain.1, bf16[1280,2048]{1,0:T(8,128)(2,1)} %proj.1, ...), custom_call_target="tpu_custom_call" | custom-call | tf_op jit(solution)/shard_map/enter/pallas_call | solution.py:317
  41.7 0.7 reduce-scatter.3.cloned.1.call-update
  42.4 14.3 %all_gather.9.refs_1_.params = f32[8,512]{1,0:T(8,128)} all-gather(f32[8,128]{1,0:T(8,128)S(1)} %concatenate.7), channel_id=1, replica_groups=mesh['segment'=4,'dp'=2,'tensor'=4] {'tensor'}, dimensions={1}, use_global_device_ids=true | all-gather | bytes 20480 | tf_op jit(solution)/shard_map/all_gather | solution.py:528
  56.7 24.2 %reduce-scatter.5.cloned.1.call-done = bf16[1,272,768]{2,1,0:T(8,128)(2,1)} async-done(((bf16[4,272,768]{2,1,0:T(8,128)(2,1)}), bf16[1,272,768]{2,1,0:T(8,128)(2,1)}) %reduce-scatter.5.cloned.1.call-update) | async-done | bytes 417808 | tf_op jit(solution)/shard_map/reduce_scatter | solution.py:529
  80.9 3.4 %scan.1 = (bf16[256,512]{1,0:T(8,128)(2,1)}, bf16[256,256]{1,0:T(8,128)(2,1)}, f32[24,256]{1,0:T(8,128)}, bf16[144,512]{1,0:T(8,128)(2,1)}) custom-call(bf16[272,768]{1,0:T(8,128)(2,1)} %bitcast.30, f32[8,512]{1,0:T(8,128)} %all_gather.9.refs_1_.params, bf16[4,256]{1,0:T(4,128)(2,1)} %refs_2_.1), custom_call_target="tpu_custom_call" | custom-call | tf_op jit(solution)/shard_map/scan/pallas_call | solution.py:401
  84.3 0.6 collective-permute-start.4
  84.8 5.1 %collective-permute-done.4 = bf16[144,512]{1,0:T(8,128)(2,1)S(1)} collective-permute-done((bf16[144,512]{1,0:T(8,128)(2,1)}, bf16[144,512]{1,0:T(8,128)(2,1)S(1)}, u32[]{:S(2)}, u32[]{:S(2)}) %collective-permute-start.4) | collective-permute-done | bytes 147488 | tf_op jit(solution)/shard_map/ppermute | solution.py:21
  90.0 1.0 convert_select_fusion.1
  91.0 2.4 %collective-permute-start.5 = (bf16[144,512]{1,0:T(8,128)(2,1)S(1)}, bf16[144,512]{1,0:T(8,128)(2,1)S(1)}, u32[]{:S(2)}, u32[]{:S(2)}) collective-permute-start(bf16[144,512]{1,0:T(8,128)(2,1)S(1)} %pad_maximum_fusion), channel_id=1, source_target_pairs={{0,24},{8,16},{16,8},{24,0},{1,25},{9,17},{17,9},{25,1},{2,26},{10... | collective-permute-start | bytes 442376 | tf_op jit(solution)/shard_map/ppermute | solution.py:21
  93.5 0.6 collective-permute-start.6
  94.0 0.6 collective-permute-start.7
  94.6 2.7 %inside.1.local = f32[256,512]{1,0:T(8,128)} custom-call(bf16[256,512]{1,0:T(8,128)(2,1)} %get-tuple-element.18.streams, bf16[256,256]{1,0:T(8,128)(2,1)} %get-tuple-element.19.maps, f32[24,256]{1,0:T(8,128)} %get-tuple-element.20.meta, f32[8,512]{1,0:T(8,128)} %all_gather.9.refs_1_.params), custom_call_target="tpu_custom_call" | custom-call | tf_op jit(solution)/shard_map/inside/pallas_call | solution.py:433
  97.4 1.2 collective-permute-done.5
  98.6 1.2 collective-permute-done.6
  99.8 0.1 select_convert_fusion
  99.9 0.8 add_select_fusion.prior
  100.7 8.7 %reduce-scatter.3.cloned.1.call-done = bf16[1,256,512]{2,1,0:T(8,128)(2,1)} async-done(((bf16[4,256,512]{2,1,0:T(8,128)(2,1)}), bf16[1,256,512]{2,1,0:T(8,128)(2,1)}) %reduce-scatter.3.cloned.1.call-update) | async-done | bytes 262160 | tf_op jit(solution)/shard_map/reduce_scatter | solution.py:530
  109.5 2.9 %gate.1 = bf16[256,512]{1,0:T(8,128)(2,1)} custom-call(bf16[256,512]{1,0:T(8,128)(2,1)} %bitcast.31, f32[256,512]{1,0:T(8,128)} %inside.1.local, bf16[256,256]{1,0:T(8,128)(2,1)} %get-tuple-element.19.maps, f32[24,256]{1,0:T(8,128)} %get-tuple-element.20.meta, f32[128,512]{1,0:T(8,128)} %add_select_fusion.prior, f32[8,512]{1,0:T(8,128)} %all_gather.9.refs_1_.params), custom_call_target="tpu_custom_call" | custom-call | tf_op jit(solution)/shard_map/gate/pallas_call | solution.py:460
  112.4 1.6 %collective-permute-start.8 = (bf16[256,512]{1,0:T(8,128)(2,1)}, bf16[256,512]{1,0:T(8,128)(2,1)S(1)}, u32[]{:S(2)}, u32[]{:S(2)}) collective-permute-start(bf16[256,512]{1,0:T(8,128)(2,1)} %gate.1), channel_id=1, source_target_pairs={{0,0},{1,1},{2,6},{3,7},{4,4},{5,5},{6,2},{7,3},{8,8},{9,9},{10,14... | collective-permute-start | bytes 786440 | tf_op jit(solution)/shard_map/ppermute | solution.py:558
  114.0 0.7 copy-done.4
  114.7 28.8 %all-gather.3.cloned.1.call-done = bf16[1024,512]{1,0:T(8,128)(2,1)} async-done(((bf16[256,512]{1,0:T(8,128)(2,1)}), bf16[1024,512]{1,0:T(8,128)(2,1)}) %all-gather.3.cloned.1.call-update) | async-done | bytes 1048592 | tf_op jit(solution)/shard_map/all_gather | solution.py:561
  143.5 6.8 %output.1 = bf16[512,2048]{1,0:T(8,128)(2,1)} custom-call(bf16[4,256,512]{2,1,0:T(8,128)(2,1)} %bitcast.27, bf16[512,2048]{1,0:T(8,128)(2,1)} %weight_mine.1, bf16[512,2048]{1,0:T(8,128)(2,1)} %collective-permute-done.9.weight_other, bf16[512,2048]{1,0:T(8,128)(2,1)} %get-tuple-element.22.crops, bf16[512,2048]{1,0:T(8,128)(2,1)} %bitcast.26, ...), custom_call_target="tpu_custom_call" | custom-call | tf_op jit(solution)/shard_map/output/pallas_call | solution.py:484
  (43 shorter events, 0.3 us)
Async XLA Ops:
  6.5 1.9 %copy-start.2 = (bf16[1,1,1,256,1280]{4,3,2,1,0:T(8,128)(2,1)S(1)}, bf16[1,1,1,256,1280]{4,3,2,1,0:T(8,128)(2,1)}, u32[]{:S(2)}) copy-start(bf16[1,1,1,256,1280]{4,3,2,1,0:T(8,128)(2,1)} %param.18) | copy-start | bytes 1966084
  6.5 9.2 %copy-start.8 = (bf16[128]{0:T(256)(128)(2,1)S(1)}, bf16[128]{0:T(256)(128)(2,1)}, u32[]{:S(2)}) copy-start(bf16[128]{0:T(256)(128)(2,1)} %param.32) | copy-start | bytes 772
  6.5 9.2 %copy-start.9 = (s32[1,2,1]{1,2,0:T(1,128)S(1)}, s32[1,2,1]{1,2,0:T(1,128)}, u32[]{:S(2)}) copy-start(s32[1,2,1]{1,2,0:T(1,128)} %param.19) | copy-start | bytes 28
  6.5 11.8 %copy-start.7 = (bf16[4,128]{1,0:T(4,128)(2,1)S(1)}, bf16[4,128]{1,0:T(4,128)(2,1)}, u32[]{:S(2)}) copy-start(bf16[4,128]{1,0:T(4,128)(2,1)} %param.27) | copy-start | bytes 3076
  6.5 74.4 %reduce-scatter.5.cloned.1.call-start = ((), (), s32[]{:S(2)}) async-start(), calls=%async_computation.3 | async-start | bytes 2088960 | tf_op jit(solution)/shard_map/reduce_scatter | solution.py:529
  7.9 10.5 %collective-permute-start.1 = (bf16[256,2048]{1,0:T(8,128)(2,1)S(1)}, bf16[256,2048]{1,0:T(8,128)(2,1)S(1)}, u32[]{:S(2)}, u32[]{:S(2)}) collective-permute-start(bf16[256,2048]{1,0:T(8,128)(2,1)S(1)} %slice_bitcast_fusion), channel_id=1, source_target_pairs={{0,4},{4,0},{1,5},{5,1},{2,6},{6,2},{3,7},{7,3},{8,12},{12,8},{9,1... | collective-permute-start | bytes 3145736 | tf_op jit(solution)/shard_map/ppermute | solution.py:21
  8.5 10.0 %collective-permute-start = (bf16[256,1280]{1,0:T(8,128)(2,1)S(1)}, bf16[256,1280]{1,0:T(8,128)(2,1)S(1)}, u32[]{:S(2)}, u32[]{:S(2)}) collective-permute-start(bf16[256,1280]{1,0:T(8,128)(2,1)S(1)} %bitcast.29), channel_id=1, source_target_pairs={{0,4},{4,0},{1,5},{5,1},{2,6},{6,2},{3,7},{7,3},{8,12},{12,8},{9,1... | collective-permute-start | bytes 1966088 | tf_op jit(solution)/shard_map/ppermute | solution.py:21
  9.3 6.4 %collective-permute-start.2 = (bf16[8,2048]{1,0:T(8,128)(2,1)S(1)}, bf16[8,2048]{1,0:T(8,128)(2,1)S(1)}, u32[]{:S(2)}, u32[]{:S(2)}) collective-permute-start(bf16[8,2048]{1,0:T(8,128)(2,1)S(1)} %slice_bitcast_fusion.1), channel_id=1, source_target_pairs={{0,8},{8,16},{16,24},{1,9},{9,17},{17,25},{2,10},{10,18},{18,26},{... | collective-permute-start | bytes 98312 | tf_op jit(solution)/shard_map/ppermute | solution.py:17
  15.7 2.8 %copy-start.5 = (bf16[8,2048]{1,0:T(8,128)(2,1)}, bf16[8,2048]{1,0:T(8,128)(2,1)S(1)}, u32[]{:S(2)}) copy-start(bf16[8,2048]{1,0:T(8,128)(2,1)S(1)} %collective-permute-done.2.edge_mine) | copy-start | bytes 98308
  15.7 2.7 %collective-permute-start.3 = (bf16[8,2048]{1,0:T(8,128)(2,1)S(1)}, bf16[8,2048]{1,0:T(8,128)(2,1)S(1)}, u32[]{:S(2)}, u32[]{:S(2)}) collective-permute-start(bf16[8,2048]{1,0:T(8,128)(2,1)S(1)} %collective-permute-done.2.edge_mine), channel_id=1, source_target_pairs={{0,4},{4,0},{1,5},{5,1},{2,6},{6,2},{3,7},{7,3},{8,12},{12,8},{9,1... | collective-permute-start | bytes 98312 | tf_op jit(solution)/shard_map/ppermute | solution.py:21
  18.4 0.6 copy-start.6
  18.4 0.8 copy-start.3
  18.4 1.2 copy-start.1
  41.6 53.0 %copy-start = (bf16[512,2048]{1,0:T(8,128)(2,1)S(1)}, bf16[512,2048]{1,0:T(8,128)(2,1)}, u32[]{:S(2)}) copy-start(bf16[512,2048]{1,0:T(8,128)(2,1)} %weight_mine.1) | copy-start | bytes 6291460
  41.6 67.8 %reduce-scatter.3.cloned.1.call-start = ((), (), s32[]{:S(2)}) async-start(), calls=%async_computation.2 | async-start | bytes 1310720 | tf_op jit(solution)/shard_map/reduce_scatter | solution.py:530
  42.4 101.1 %all-gather.3.cloned.1.call-start = ((), (), s32[]{:S(2)}) async-start(), calls=%async_computation.4 | async-start | bytes 1310720 | tf_op jit(solution)/shard_map/all_gather | solution.py:561
  84.3 5.7 %collective-permute-start.4 = (bf16[144,512]{1,0:T(8,128)(2,1)}, bf16[144,512]{1,0:T(8,128)(2,1)S(1)}, u32[]{:S(2)}, u32[]{:S(2)}) collective-permute-start(bf16[144,512]{1,0:T(8,128)(2,1)} %get-tuple-element.21), channel_id=1, source_target_pairs={{0,1},{1,0},{2,3},{3,2},{4,5},{5,4},{6,7},{7,6},{8,9},{9,8},{10,11... | collective-permute-start | bytes 442376 | tf_op jit(solution)/shard_map/ppermute | solution.py:21
  91.0 7.5 %collective-permute-start.5 = (bf16[144,512]{1,0:T(8,128)(2,1)S(1)}, bf16[144,512]{1,0:T(8,128)(2,1)S(1)}, u32[]{:S(2)}, u32[]{:S(2)}) collective-permute-start(bf16[144,512]{1,0:T(8,128)(2,1)S(1)} %pad_maximum_fusion), channel_id=1, source_target_pairs={{0,24},{8,16},{16,8},{24,0},{1,25},{9,17},{17,9},{25,1},{2,26},{10... | collective-permute-start | bytes 442376 | tf_op jit(solution)/shard_map/ppermute | solution.py:21
  93.5 6.3 %collective-permute-start.6 = (bf16[144,512]{1,0:T(8,128)(2,1)S(1)}, bf16[144,512]{1,0:T(8,128)(2,1)S(1)}, u32[]{:S(2)}, u32[]{:S(2)}) collective-permute-start(bf16[144,512]{1,0:T(8,128)(2,1)S(1)} %pad_maximum_fusion), channel_id=1, source_target_pairs={{0,16},{8,24},{16,0},{24,8},{1,17},{9,25},{17,1},{25,9},{2,18},{10... | collective-permute-start | bytes 442376 | tf_op jit(solution)/shard_map/ppermute | solution.py:21
  94.0 5.8 %collective-permute-start.7 = (bf16[144,512]{1,0:T(8,128)(2,1)S(1)}, bf16[144,512]{1,0:T(8,128)(2,1)S(1)}, u32[]{:S(2)}, u32[]{:S(2)}) collective-permute-start(bf16[144,512]{1,0:T(8,128)(2,1)S(1)} %pad_maximum_fusion), channel_id=1, source_target_pairs={{0,8},{8,0},{16,24},{24,16},{1,9},{9,1},{17,25},{25,17},{2,10},{10... | collective-permute-start | bytes 442376 | tf_op jit(solution)/shard_map/ppermute | solution.py:21
  94.6 20.1 %collective-permute-start.9 = (bf16[512,2048]{1,0:T(8,128)(2,1)S(1)}, bf16[512,2048]{1,0:T(8,128)(2,1)}, u32[]{:S(2)}, u32[]{:S(2)}) collective-permute-start(bf16[512,2048]{1,0:T(8,128)(2,1)S(1)} %copy-done), channel_id=1, source_target_pairs={{0,4},{4,0},{1,5},{5,1},{2,6},{6,2},{3,7},{7,3},{8,12},{12,8},{9,1... | collective-permute-start | bytes 6291464 | tf_op jit(solution)/shard_map/ppermute | solution.py:21
  112.4 1.6 %collective-permute-start.8 = (bf16[256,512]{1,0:T(8,128)(2,1)}, bf16[256,512]{1,0:T(8,128)(2,1)S(1)}, u32[]{:S(2)}, u32[]{:S(2)}) collective-permute-start(bf16[256,512]{1,0:T(8,128)(2,1)} %gate.1), channel_id=1, source_target_pairs={{0,0},{1,1},{2,6},{3,7},{4,4},{5,5},{6,2},{7,3},{8,8},{9,9},{10,14... | collective-permute-start | bytes 786440 | tf_op jit(solution)/shard_map/ppermute | solution.py:558
  114.0 0.7 copy-start.4
Sparse Core Ops, SparseCore 0:
  41.7 39.1 reduce-scatter.4
  83.2 26.2 reduce-scatter.2
  114.8 28.6 all-gather.2

commit v3 on v2

--- a/solution.py
+++ b/solution.py
@@ -204,110 +204,107 @@
 
 
 def enter_body(
-    table, feats_mine, feats_other, vision_gain, proj, text, text_other, edge_mine, edge_other,
-    newline, gain, xz, bc, dt, crops_out, first_out, second_out,
-    feats, normed, proj_tiles, tails, weights, crops, rows, first, second, sems, out_sems,
+    table, feats_mine, feats_other, vision_gain, proj, text, text_other, newline, gain, xz, bc, dt,
+    crops_out, rows_out, first_out,
+    feats, normed, proj_tiles, tails, weights, crops, rows, first, sems, out_sems,
 ):
     half = tails.shape[1]
-    span = half + 16
     tiles, _, tile = proj_tiles.shape
-    arrivals = [
+    columns = rows.shape[1]
+    load_feats = [
         pltpu.make_async_copy(feats_mine, feats.at[0], sems.at[0]),
         pltpu.make_async_copy(feats_other, feats.at[1], sems.at[1]),
     ]
-    arrivals += [
+    load_proj = [
         pltpu.make_async_copy(proj.at[:, pl.ds(i * tile, tile)], proj_tiles.at[i], sems.at[2 + i])
         for i in range(tiles)
     ]
-    arrivals += [
+    load_tails = [
         pltpu.make_async_copy(text.at[pl.ds(half, half), :], tails.at[0], sems.at[2 + tiles]),
         pltpu.make_async_copy(text_other, tails.at[1], sems.at[3 + tiles]),
-        pltpu.make_async_copy(bc, weights.at[4], sems.at[4 + tiles]),
-    ]
-    arrivals += [
+    ]
+    load_weights = [
         pltpu.make_async_copy(
-            xz.at[:, pl.ds(i * 256, 256)], weights.at[i], sems.at[5 + tiles + i]
+            xz.at[:, pl.ds(i * 256, 128)],
+            weights.at[i // 2, :, pl.ds(i % 2 * 128, 128)],
+            sems.at[4 + tiles + i],
         )
         for i in range(4)
     ]
-    for copy in arrivals:
+    load_weights.append(pltpu.make_async_copy(bc, weights.at[2], sems.at[8 + tiles]))
+    for copy in load_feats + load_proj[:2] + load_tails + load_proj[2:] + load_weights:
         copy.start()
     gain_row = gain[...].reshape(1, -1)
     rank = lax.axis_index("dp")
     stays = table[0, rank, 0] == rank
-    arrivals[0].wait()
-    arrivals[1].wait()
+    load_feats[0].wait()
+    load_feats[1].wait()
     for index in range(2):
         block = jnp.where(stays, feats[index], feats[1 - index]).astype(F32)
         scale = lax.rsqrt(jnp.mean(block * block, -1, keepdims=True) + EPS)
         normed[index * half : (index + 1) * half, :] = (
             block * scale * vision_gain[...].reshape(1, -1).astype(F32)
         ).astype(BF16)
-    departures = []
+    ones = jnp.ones((8, 128), BF16)
+
+    def folded(block):
+        total = jnp.zeros((block.shape[0], 128), F32)
+        for start in range(0, block.shape[1], 128):
+            piece = block[:, start : start + 128].astype(F32)
+            total = total + piece * piece
+        return total
+
+    squares = [None] * 4
     for i in range(tiles):
-        arrivals[2 + i].wait()
+        load_proj[i].wait()
         cols = slice(i * tile, (i + 1) * tile)
         result = jnp.dot(normed[...], proj_tiles[i], preferred_element_type=F32).astype(BF16)
         crops[:, cols] = result
         scaled = result * gain_row[:, cols]
         rows[0:half, cols] = scaled[:half]
-        rows[2 * span : 2 * span + half, cols] = scaled[half:]
-    departures.append(pltpu.make_async_copy(crops, crops_out, out_sems.at[0]))
-    departures[-1].start()
-    top = lax.broadcasted_iota(jnp.int32, (8, 1), 0) == 0
-    ones = jnp.ones((8, rows.shape[1]), BF16)
-    sums = []
+        rows[2 * half : 3 * half, cols] = scaled[half:]
+        for index in range(2):
+            more = folded(result[index * half : (index + 1) * half])
+            squares[2 * index] = more if i == 0 else squares[2 * index] + more
+        if i < 2:
+            load_tails[i].wait()
+            head = tails[i, 0:8, :].astype(F32)
+            line = newline[...].reshape(1, -1).astype(F32)
+            top = lax.broadcasted_iota(jnp.int32, (8, 1), 0) == 0
+            tails[i, 0:8, :] = jnp.where(top, line, head).astype(BF16)
+            main = tails[i]
+            base = (2 * i + 1) * half
+            rows[base : base + half, :] = main * gain_row
+            squares[2 * i + 1] = folded(main)
+    departures = [
+        pltpu.make_async_copy(crops, crops_out, out_sems.at[0]),
+        pltpu.make_async_copy(rows, rows_out, out_sems.at[1]),
+    ]
+    for copy in departures:
+        copy.start()
+    for copy in load_weights:
+        copy.wait()
     for part in range(4):
-        index = part // 2
-        base = part * span
-        if part % 2 == 0:
-            main = crops[index * half : (index + 1) * half, :]
-            edge = (edge_mine, edge_other)[index][...]
-        else:
-            arrivals[2 + tiles + index].wait()
-            head = tails[index, 0:8, :].astype(F32)
-            line = newline[...].reshape(1, -1).astype(F32)
-            tails[index, 0:8, :] = jnp.where(top, line, head).astype(BF16)
-            main = tails[index]
-            rows[base : base + half, :] = main * gain_row
-            edge = crops[(index + 1) * half - 8 : (index + 1) * half, :]
-        wide = edge.astype(F32)
-        last = jnp.concatenate([wide, jnp.zeros_like(wide)], 0).astype(BF16)
-        rows[base + half : base + span, :] = last * gain_row
-        sums.append(
-            jnp.concatenate(
-                [
-                    contract(ones, main * main, ((1,), (1,))),
-                    contract(ones, last * last, ((1,), (1,))),
-                ],
-                1,
-            )
+        main = rows[part * half : (part + 1) * half, :]
+        for i in range(3):
+            first[part, 0:half, i * 256 : i * 256 + 256] = jnp.dot(
+                main, weights[i], preferred_element_type=F32
+            ).astype(BF16)
+        steps = contract(dt[...], main, ((1,), (1,)))
+        sums = contract(ones, squares[part].astype(BF16), ((1,), (1,)))
+        first[part, half : half + 8, 0:half] = jnp.concatenate(
+            [steps[0:4], sums[0:4]], 0
+        ).astype(BF16)
+        departures.append(
+            pltpu.make_async_copy(first.at[part], first_out.at[part], out_sems.at[2 + part])
         )
-    for i in (4, 0, 1, 2, 3):
-        arrivals[5 + tiles + i if i < 4 else 4 + tiles].wait()
-        result = jnp.dot(rows[...], weights[i], preferred_element_type=F32).astype(BF16)
-        for part in range(4):
-            block = result[part * span : (part + 1) * span]
-            if i == 4:
-                first[part, :, 512:768] = block
-            else:
-                cols = slice(128 * i, 128 * i + 128)
-                first[part, :, cols] = block[:, 0:128]
-                second[part, :, cols] = block[0:half, 128:256]
-    for part in range(4):
-        steps = contract(dt[...], rows[part * span : (part + 1) * span, :], ((1,), (1,)))
-        both = jnp.concatenate([steps[0:4], sums[part][4:8]], 0)
-        first[part, half + 8 : span, 0:span] = both.astype(BF16)
-    for source, target, i in ((first, first_out, 1), (second, second_out, 2)):
-        departures.append(pltpu.make_async_copy(source, target, out_sems.at[i]))
         departures[-1].start()
     for copy in departures:
         copy.wait()
 
 
 def enter(
-    table, feats_mine, feats_other, vision_gain, proj, text, text_other, edge_mine, edge_other,
-    newline, gain, xz, bc, dt,
+    table, feats_mine, feats_other, vision_gain, proj, text, text_other, newline, gain, xz, bc, dt
 ):
     half, vision = feats_mine.shape
     columns = text.shape[1]
@@ -317,31 +314,51 @@
     return pl.pallas_call(
         enter_body,
         in_specs=[pl.BlockSpec(memory_space=pltpu.SMEM), whole, whole, near, whole, whole, whole]
-        + [near, near, near, near, whole, whole, near],
+        + [near, near, whole, whole, near],
         out_specs=[whole, whole, whole],
         out_shape=[
             jax.ShapeDtypeStruct((2 * half, columns), BF16),
-            jax.ShapeDtypeStruct((4, half + 16, 768), BF16),
-            jax.ShapeDtypeStruct((4, half, 512), BF16),
+            jax.ShapeDtypeStruct((4 * half, columns), BF16),
+            jax.ShapeDtypeStruct((4, half + 8, 768), BF16),
         ],
         scratch_shapes=[
             pltpu.VMEM((2, half, vision), BF16),
             pltpu.VMEM((2 * half, vision), BF16),
             pltpu.VMEM((tiles, vision, columns // tiles), BF16),
             pltpu.VMEM((2, half, columns), BF16),
-            pltpu.VMEM((5, columns, 256), BF16),
+            pltpu.VMEM((3, columns, 256), BF16),
             pltpu.VMEM((2 * half, columns), BF16),
-            pltpu.VMEM((4 * (half + 16), columns), BF16),
-            pltpu.VMEM((4, half + 16, 768), BF16),
-            pltpu.VMEM((4, half, 512), BF16),
+            pltpu.VMEM((4 * half, columns), BF16),
+            pltpu.VMEM((4, half + 8, 768), BF16),
             pltpu.SemaphoreType.DMA((9 + tiles,)),
-            pltpu.SemaphoreType.DMA((3,)),
+            pltpu.SemaphoreType.DMA((6,)),
         ],
         name="enter",
-    )(
-        table, feats_mine, feats_other, vision_gain, proj, text, text_other, edge_mine, edge_other,
-        newline, gain, xz, bc, dt,
-    )
+    )(table, feats_mine, feats_other, vision_gain, proj, text, text_other, newline, gain, xz, bc, dt)
+
+
+def gates_body(rows, weight, out):
+    for head in range(4):
+        out[0, :, 128 * head : 128 * head + 128] = jnp.dot(
+            rows[...],
+            weight[:, 256 * head + 128 : 256 * head + 256],
+            preferred_element_type=F32,
+        ).astype(BF16)
+
+
+def gates(rows, weight):
+    half, columns = rows.shape[0] // 4, rows.shape[1]
+    return pl.pallas_call(
+        gates_body,
+        grid=(4,),
+        in_specs=[
+            pl.BlockSpec((half, columns), lambda i: (i, 0)),
+            pl.BlockSpec(weight.shape, lambda i: (0, 0)),
+        ],
+        out_specs=pl.BlockSpec((1, half, 512), lambda i: (i, 0, 0)),
+        out_shape=jax.ShapeDtypeStruct((4, half, 512), BF16),
+        name="gates",
+    )(rows, weight)
 
 
 def filtered(main, edge, taps):
@@ -354,16 +371,18 @@
     return total
 
 
-def scan_body(width, first, params, taps_maps, streams, maps, meta, state):
-    half = first.shape[0] - 16
-    sums = first[half : half + 16, 0 : half + 128].astype(F32)[8:16]
+def scan_body(width, first, before, params, taps_maps, streams, maps, meta, state):
+    half = first.shape[0] - 8
+    sums = first[half : half + 8, 0:half].astype(F32)
     scale = lax.rsqrt(sums[4:5] / width + EPS)
+    sums_before = before[8:16, half - 128 : half].astype(F32)
+    scale_before = lax.rsqrt(sums_before[4:5] / width + EPS)
     head = lax.broadcasted_iota(jnp.int32, (8, 512), 1) // 128
     owner = (head == lax.broadcasted_iota(jnp.int32, (8, 512), 0)).astype(F32)
     scalars = params[5:8, :]
     bias = jnp.sum(owner * scalars[0:1], 1, keepdims=True) * (1.0 / 128)
     rate = jnp.sum(owner * scalars[1:2], 1, keepdims=True) * (1.0 / 128)
-    raw = sums[:, 0:half] * scale[:, 0:half] + bias
+    raw = sums * scale + bias
     step = jnp.maximum(raw, 0.0) + jnp.log1p(jnp.exp(-jnp.abs(raw)))
     decays = -jnp.exp(rate) * step
     upper = (
@@ -373,10 +392,10 @@
     cumulative = contract(decays, upper, ((1,), (0,)), HIGHEST)
     final = cumulative[:, half - 1 : half]
     carry = jnp.exp(final - cumulative) * step
-    scale_main = columns_of(jnp.broadcast_to(scale[:, 0:half], (8, half)))[:, 0:1]
-    scale_edge = columns_of(jnp.broadcast_to(scale[:, half : half + 128], (8, 128)))[0:8, 0:1]
+    scale_main = columns_of(jnp.broadcast_to(scale, (8, half)))[:, 0:1]
+    scale_edge = columns_of(jnp.broadcast_to(scale_before, (8, 128)))[120:128, 0:1]
     taps_x = params[0:4, :]
-    edge = first[half : half + 16, :].astype(F32)[0:8] * scale_edge
+    edge = before[0:8, :].astype(F32) * scale_edge
     x = silu(filtered(first[0:half, 0:512].astype(F32) * scale_main, edge[:, 0:512], taps_x))
     both = silu(
         filtered(
@@ -393,11 +412,11 @@
     maps[...] = both
     meta[0:8, :] = cumulative
     meta[8:16, :] = step
-    meta[16:24, :] = jnp.broadcast_to(scale[:, 0:half], (8, half))
-
-
-def scan(width, first, params, taps_maps):
-    half = first.shape[0] - 16
+    meta[16:24, :] = jnp.broadcast_to(scale, (8, half))
+
+
+def scan(width, first, before, params, taps_maps):
+    half = first.shape[0] - 8
     return pl.pallas_call(
         lambda *refs: scan_body(width, *refs),
         out_shape=[
@@ -407,7 +426,7 @@
             jax.ShapeDtypeStruct((144, 512), BF16),
         ],
         name="scan",
-    )(first, params, taps_maps)
+    )(first, before, params, taps_maps)
 
 
 def inside_body(streams, maps, meta, params, out):
@@ -464,38 +483,85 @@
     )(second, local, maps, meta, prior, params)
 
 
-def output_body(gathered, weight_mine, weight_other, crops, text, newline, out):
-    half = crops.shape[0]
-    top = lax.broadcasted_iota(jnp.int32, (half, 1), 0) == 0
-    tail = jnp.where(top, newline[...].reshape(1, -1).astype(F32), text[...].astype(F32))
-    for index, hidden in enumerate((crops[...].astype(F32), tail)):
-        mixed = jnp.dot(gathered[index], weight_mine[...], preferred_element_type=F32)
-        mixed = mixed + jnp.dot(
-            gathered[2 + index], weight_other[...], preferred_element_type=F32
+def output_body(
+    here, near, far, both, weight_mine, weight_other, crops, text, newline, out_hbm,
+    blocks, weights, hidden, out, sems, out_sems,
+):
+    half = hidden.shape[1]
+    tiles, _, _, tile = weights.shape
+    chip = lax.axis_index("tensor")
+    load_hidden = [
+        pltpu.make_async_copy(crops.at[pl.ds(0, half), :], hidden.at[0], sems.at[0]),
+        pltpu.make_async_copy(text.at[pl.ds(half, half), :], hidden.at[1], sems.at[1]),
+    ]
+    load_blocks = [
+        pltpu.make_async_copy(source, blocks.at[jnp.bitwise_xor(chip, bits)], sems.at[2 + bits])
+        for bits, source in enumerate((here, near, far, both))
+    ]
+    load_weights = [
+        [
+            pltpu.make_async_copy(
+                source.at[:, pl.ds(i * tile, tile)], weights.at[i, index], sems.at[6 + 2 * i + index]
+            )
+            for index, source in enumerate((weight_mine, weight_other))
+        ]
+        for i in range(tiles)
+    ]
+    for copy in load_blocks + load_weights[0] + load_hidden:
+        copy.start()
+    for pair in load_weights[1:]:
+        for copy in pair:
+            copy.start()
+    for copy in load_blocks:
+        copy.wait()
+    departures = []
+    for i in range(tiles):
+        cols = slice(i * tile, (i + 1) * tile)
+        for copy in load_weights[i]:
+            copy.wait()
+        if i == 0:
+            for copy in load_hidden:
+                copy.wait()
+            head = hidden[1, 0:8, :].astype(F32)
+            line = newline[...].reshape(1, -1).astype(F32)
+            top = lax.broadcasted_iota(jnp.int32, (8, 1), 0) == 0
+            hidden[1, 0:8, :] = jnp.where(top, line, head).astype(BF16)
+        for index in range(2):
+            mixed = jnp.dot(blocks[index], weights[i, 0], preferred_element_type=F32)
+            mixed = mixed + jnp.dot(blocks[2 + index], weights[i, 1], preferred_element_type=F32)
+            out[i, index * half : (index + 1) * half, :] = (
+                hidden[index, :, cols].astype(F32) + mixed
+            ).astype(BF16)
+        departures.append(
+            pltpu.make_async_copy(out.at[i], out_hbm.at[:, pl.ds(i * tile, tile)], out_sems.at[i])
         )
-        out[index * half : (index + 1) * half, :] = (hidden + mixed).astype(BF16)
-
-
-def output(gathered, weight_mine, weight_other, crops, text, newline):
+        departures[-1].start()
+    for copy in departures:
+        copy.wait()
+
+
+def output(pieces, weight_mine, weight_other, crops, text, newline):
     section, columns = text.shape
     half = section // 2
-    tile = columns // 4
-    inner = gathered.shape[2]
+    tiles = 4
+    tile = columns // tiles
+    inner = weight_mine.shape[0]
+    whole = pl.BlockSpec(memory_space=pl.ANY)
     return pl.pallas_call(
         output_body,
-        grid=(4,),
-        in_specs=[
-            pl.BlockSpec((4, half, inner), lambda i: (0, 0, 0)),
-            pl.BlockSpec((inner, tile), lambda i: (0, i)),
-            pl.BlockSpec((inner, tile), lambda i: (0, i)),
-            pl.BlockSpec((half, tile), lambda i: (0, i)),
-            pl.BlockSpec((half, tile), lambda i: (1, i)),
-            pl.BlockSpec((tile,), lambda i: (i,)),
+        in_specs=[whole] * 8 + [pl.BlockSpec(memory_space=pltpu.VMEM)],
+        out_specs=whole,
+        out_shape=jax.ShapeDtypeStruct((section, columns), BF16),
+        scratch_shapes=[
+            pltpu.VMEM((4, half, inner), BF16),
+            pltpu.VMEM((tiles, 2, inner, tile), BF16),
+            pltpu.VMEM((2, half, columns), BF16),
+            pltpu.VMEM((tiles, section, tile), BF16),
+            pltpu.SemaphoreType.DMA((6 + 2 * tiles,)),
+            pltpu.SemaphoreType.DMA((tiles,)),
         ],
-        out_specs=pl.BlockSpec((section, tile), lambda i: (0, i)),
-        out_shape=jax.ShapeDtypeStruct((section, columns), BF16),
         name="output",
-    )(gathered, weight_mine, weight_other, crops, text, newline)
+    )(*pieces, weight_mine, weight_other, crops, text, newline)
 
 
 def per_device_halves(
@@ -512,23 +578,27 @@
     feats = crop_feats[0, 0, 0]
     feats_other = swapped(feats, "dp", 1)
     text_other = swapped(text[half:], "dp", 1)
-    edge_mine = passed_along(text[section - 8 :], "segment", 1)
-    edge_other = swapped(edge_mine, "dp", 1)
+    crops, rows, first = enter(
+        crop_dest, feats, feats_other, vision_gain, proj_weight, text, text_other, newline,
+        norm_gain, xz_weight, bc_weight, dt_weight.T,
+    )
+    later = (conv_x, out_gain, dt_bias, a_log, skip, out_weight, first, rows)
+    conv_x, out_gain, dt_bias, a_log, skip, out_weight, first, rows = lax.optimization_barrier(later)
+    first = lax.psum_scatter(first, "tensor", scatter_dimension=0, tiled=False)
+    second = gates(rows, xz_weight)
     weight_other = swapped(out_weight, "dp", 1)
-    crops, first, second = enter(
-        crop_dest, feats, feats_other, vision_gain, proj_weight, text, text_other, edge_mine,
-        edge_other, newline, norm_gain, xz_weight, bc_weight, dt_weight.T,
-    )
     own = jnp.concatenate(
         [conv_x.astype(F32), out_gain.astype(F32)[None]]
         + [jnp.broadcast_to(value[:, None], (1, 128)) for value in (dt_bias, a_log, skip)],
         0,
     )
-    own, first = lax.optimization_barrier((own, first))
     params = lax.all_gather(own, "tensor", axis=1, tiled=True)
-    first = lax.psum_scatter(first, "tensor", scatter_dimension=0, tiled=False)
+    second, params = lax.optimization_barrier((second, params))
     second = lax.psum_scatter(second, "tensor", scatter_dimension=0, tiled=False)
-    streams, maps, meta, state = scan(width, first, params, conv_bc)
+    route = [(i, i + 1) for i in range(0, 4 * segment_count, 2)]
+    route += [(i, i + 3) for i in range(1, 4 * segment_count - 4, 2)]
+    before = lax.ppermute(first[half - 8 :], ("segment", "tensor"), route)
+    streams, maps, meta, state = scan(width, first, before, params, conv_bc)
     local = inside(streams, maps, meta, params)
     partner = swapped(state, "tensor", 1).astype(F32)
     state = state.astype(F32)
@@ -555,11 +625,14 @@
         prior = jnp.where(source < my_segment, piece[128:129] * prior + piece[:128], prior)
     prior = jnp.where(late, early_decay * prior + early_state, prior)
     normed = gate(second, local, maps, meta, prior, params)
-    normed = lax.ppermute(
-        normed, ("dp", "tensor"), [(i, i if i % 4 < 2 else i ^ 4) for i in range(8)]
-    )
-    gathered = lax.all_gather(normed, "tensor", axis=0, tiled=False)
-    return output(gathered, out_weight, weight_other, crops, text, newline)[None]
+    near, far, here = (
+        lax.ppermute(
+            normed, ("dp", "tensor"), [(i, (i if i % 4 < 2 else i ^ 4) ^ bits) for i in range(8)]
+        )
+        for bits in (1, 2, 0)
+    )
+    pieces = (here, near, far, swapped(far, "tensor", 1))
+    return output(pieces, out_weight, weight_other, crops, text, newline)[None]
 
 
 def per_device(*args):

time: 157 us -> 136 us (0.87)
  waiting for transfers between devices: 71.6 us -> 44.7 us
  starting transfers between devices: 11.2 us -> 15.2 us
    all_gather x1 -> x0, waiting for transfers between devices: 28.8 us -> none  [per_device_halves(): gathered = lax.all_gather(normed, 'tensor', axis=0, tiled=False)]
    ppermute x8, waiting for transfers between devices: 7.58 us -> 21.5 us  [swapped(): lax.ppermute(block, axis, [(i, i ^ bits) for i in range(lax.axis_size(axi...]
    reduce_scatter x1, waiting for transfers between devices: 24.2 us -> 12.7 us  [per_device_halves(): first = lax.psum_scatter(first, 'tensor', scatter_dimension=0, tiled=False)]
    pallas_call x1, Pallas kernels: 22 us -> 12.4 us  [enter(): pl.pallas_call(enter_body, in_specs=[pl.BlockSpec(memory_space=pltpu.SMEM...]
    ppermute x2 -> x4, waiting for transfers between devices: 1.58 us -> 10.5 us  [the longest x3 9.18 us: per_device_halves(): lax.ppermute(normed, ('dp', 'tensor'), [(i, (i if i % 4 < 2 else i ^ 4) ^...]
    reduce_scatter x1, waiting for transfers between devices: 8.74 us -> 0.01 us  [per_device_halves(): lax.psum_scatter(second, 'tensor', scatter_dimension=0, tiled=False)]
    pallas_call x1 -> x2, Pallas kernels: 6.78 us -> 15.3 us  [the longest x1 8.67 us: gates(): pl.pallas_call(gates_body, grid=(4,), in_specs=[pl.BlockSpec((half, colum...]
    ppermute x8, starting transfers between devices: 4.74 us -> 9.69 us  [swapped(): lax.ppermute(block, axis, [(i, i ^ bits) for i in range(lax.axis_size(axi...]
  transfers between devices with their start and end apart: 13 -> 14, of which waited for: 7 -> 9; matrix products, arithmetic and copies ran while one was open for 2% -> 2% of each run, Pallas kernels for 6% -> 13%
where the time goes in v3:
time: 136 us; the launch traced here: 135 us
  waiting for transfers between devices  44.7 us (33%)
  Pallas kernels  36.8 us (27%)
  blocking collectives  15.8 us (12%)
  between operations  15.5 us (11%)
  starting transfers between devices  15.2 us (11%)
  local copies, waits for them, and re-layouts  5.27 us (4%)
  other arithmetic  1.95 us (1%)
    ppermute x8, waiting for transfers between devices, swapped(): lax.ppermute(block, axis, [(i, i ^ bits) for i in range(lax.axis_size(axi...  21.5 us
    all_gather x1, blocking collectives, per_device_halves(): params = lax.all_gather(own, 'tensor', axis=1, tiled=True)  15.8 us
    reduce_scatter x1, waiting for transfers between devices, per_device_halves(): first = lax.psum_scatter(first, 'tensor', scatter_dimension=0, tiled=False)  12.7 us
    pallas_call x1, Pallas kernels, enter(): pl.pallas_call(enter_body, in_specs=[pl.BlockSpec(memory_space=pltpu.SMEM...  12.4 us
    ppermute x8, starting transfers between devices, swapped(): lax.ppermute(block, axis, [(i, i ^ bits) for i in range(lax.axis_size(axi...  9.69 us
    ppermute x3, waiting for transfers between devices, per_device_halves(): lax.ppermute(normed, ('dp', 'tensor'), [(i, (i if i % 4 < 2 else i ^ 4) ^...  9.18 us
    pallas_call x1, Pallas kernels, gates(): pl.pallas_call(gates_body, grid=(4,), in_specs=[pl.BlockSpec((half, colum...  8.67 us
    pallas_call x1, Pallas kernels, output(): pl.pallas_call(output_body, in_specs=[whole] * 8 + [pl.BlockSpec(memory_s...  6.67 us
  transfers between devices with their start and end apart: 14, of which 9 were waited for; matrix products, arithmetic and copies ran while one was open for 2% of the time, Pallas kernels for 13%

profile of v3, /device:TPU:0, one launch (start us, length us, event | category | flops | bytes accessed | tf_op | source)
XLA Modules:
  0.0 135.3 jit_solution(14606035264308989043)
XLA Ops:
  6.5 1.4 %slice_bitcast_fusion = bf16[256,2048]{1,0:T(8,128)(2,1)S(1)} fusion(bf16[1,512,2048]{2,1,0:T(8,128)(2,1)} %param.17), kind=kLoop, calls=%fused_computation | loop fusion | bytes 2097152 | tf_op jit(solution)/shard_map/slice | solution.py:580
  7.9 0.5 collective-permute-start.1
  8.5 0.6 copy.18.table
  9.1 2.5 %collective-permute-done.feats_other = bf16[256,1280]{1,0:T(8,128)(2,1)S(1)} collective-permute-done((bf16[256,1280]{1,0:T(8,128)(2,1)S(1)}, bf16[256,1280]{1,0:T(8,128)(2,1)S(1)}, u32[]{:S(2)}, u32[]{:S(2)}) %collective-permute-start) | collective-permute-done | bytes 655392 | tf_op jit(solution)/shard_map/ppermute | solution.py:21
  11.7 0.9 copy-done.3
  12.5 0.3 copy-done.1
  12.8 12.4 %enter.1 = (bf16[512,2048]{1,0:T(8,128)(2,1)}, bf16[1024,2048]{1,0:T(8,128)(2,1)}, bf16[4,264,768]{2,1,0:T(8,128)(2,1)}) custom-call(s32[1,2,1]{2,1,0:T(2,128)} %copy.18.table, bf16[256,1280]{1,0:T(8,128)(2,1)} %bitcast.26, bf16[256,1280]{1,0:T(8,128)(2,1)} %copy-done.3, bf16[1280]{0:T(1024)(128)(2,1)} %vision_gain.1, bf16[1280,2048]{1,0:T(8,128)(2,1)} %proj.1, ...), custom_call_target="tpu_custom_call" | custom-call | tf_op jit(solution)/shard_map/enter/pallas_call | solution.py:314
  27.3 8.7 %gates.1 = bf16[4,256,512]{2,1,0:T(8,128)(2,1)} custom-call(bf16[1024,2048]{1,0:T(8,128)(2,1)} %get-tuple-element.24.rows, bf16[2048,1024]{1,0:T(8,128)(2,1)} %weight.1), custom_call_target="tpu_custom_call" | custom-call | tf_op jit(solution)/shard_map/gates/pallas_call | solution.py:351
  36.1 15.8 %all_gather.3.refs_2_.params = f32[8,512]{1,0:T(8,128)} all-gather(f32[8,128]{1,0:T(8,128)S(1)} %concatenate.7), channel_id=1, replica_groups=mesh['segment'=4,'dp'=2,'tensor'=4] {'tensor'}, dimensions={1}, use_global_device_ids=true | all-gather | bytes 20480 | tf_op jit(solution)/shard_map/all_gather | solution.py:595
  51.9 12.7 %reduce-scatter.5.cloned.1.call-done = bf16[1,264,768]{2,1,0:T(8,128)(2,1)} async-done(((bf16[4,264,768]{2,1,0:T(8,128)(2,1)}), bf16[1,264,768]{2,1,0:T(8,128)(2,1)}) %reduce-scatter.5.cloned.1.call-update) | async-done | bytes 405520 | tf_op jit(solution)/shard_map/reduce_scatter | solution.py:587
  64.6 0.7 slice_bitcast_fusion.1
  65.3 2.5 %collective-permute-start.2 = (bf16[16,768]{1,0:T(8,128)(2,1)S(1)}, bf16[16,768]{1,0:T(8,128)(2,1)S(1)}, u32[]{:S(2)}, u32[]{:S(2)}) collective-permute-start(bf16[16,768]{1,0:T(8,128)(2,1)S(1)} %slice_bitcast_fusion.1), channel_id=1, source_target_pairs={{0,1},{2,3},{8,9},{10,11},{16,17},{18,19},{24,25},{26,27},{1,8},{3... | collective-permute-start | bytes 73736 | tf_op jit(solution)/shard_map/ppermute | solution.py:600
  67.9 1.3 collective-permute-done.2.refs_1_
  69.2 0.6 copy-done.8
  69.8 3.4 %scan.1 = (bf16[256,512]{1,0:T(8,128)(2,1)}, bf16[256,256]{1,0:T(8,128)(2,1)}, f32[24,256]{1,0:T(8,128)}, bf16[144,512]{1,0:T(8,128)(2,1)}) custom-call(bf16[264,768]{1,0:T(8,128)(2,1)} %bitcast.28, bf16[16,768]{1,0:T(8,128)(2,1)} %copy-done.8, f32[8,512]{1,0:T(8,128)} %all_gather.3.refs_2_.params, bf16[4,256]{1,0:T(4,128)(2,1)} %refs_3_.1), custom_call_target="tpu_custom_call" | custom-call | tf_op jit(solution)/shard_map/scan/pallas_call | solution.py:420
  73.1 2.4 %collective-permute-start.3 = (bf16[144,512]{1,0:T(8,128)(2,1)}, bf16[144,512]{1,0:T(8,128)(2,1)S(1)}, u32[]{:S(2)}, u32[]{:S(2)}) collective-permute-start(bf16[144,512]{1,0:T(8,128)(2,1)} %get-tuple-element.36), channel_id=1, source_target_pairs={{0,1},{1,0},{2,3},{3,2},{4,5},{5,4},{6,7},{7,6},{8,9},{9,8},{10,11... | collective-permute-start | bytes 442376 | tf_op jit(solution)/shard_map/ppermute | solution.py:21
  75.6 10.6 %collective-permute-done.3 = bf16[144,512]{1,0:T(8,128)(2,1)S(1)} collective-permute-done((bf16[144,512]{1,0:T(8,128)(2,1)}, bf16[144,512]{1,0:T(8,128)(2,1)S(1)}, u32[]{:S(2)}, u32[]{:S(2)}) %collective-permute-start.3) | collective-permute-done | bytes 147488 | tf_op jit(solution)/shard_map/ppermute | solution.py:21
  86.2 1.0 convert_select_fusion.1
  87.3 4.9 %collective-permute-start.4 = (bf16[144,512]{1,0:T(8,128)(2,1)S(1)}, bf16[144,512]{1,0:T(8,128)(2,1)S(1)}, u32[]{:S(2)}, u32[]{:S(2)}) collective-permute-start(bf16[144,512]{1,0:T(8,128)(2,1)S(1)} %pad_maximum_fusion), channel_id=1, source_target_pairs={{0,24},{8,16},{16,8},{24,0},{1,25},{9,17},{17,9},{25,1},{2,26},{10... | collective-permute-start | bytes 442376 | tf_op jit(solution)/shard_map/ppermute | solution.py:21
  92.2 0.5 collective-permute-start.5
  92.7 1.2 collective-permute-start.6
  93.9 2.7 %inside.1.local = f32[256,512]{1,0:T(8,128)} custom-call(bf16[256,512]{1,0:T(8,128)(2,1)} %get-tuple-element.33.streams, bf16[256,256]{1,0:T(8,128)(2,1)} %get-tuple-element.34.maps, f32[24,256]{1,0:T(8,128)} %get-tuple-element.35.meta, f32[8,512]{1,0:T(8,128)} %all_gather.3.refs_2_.params), custom_call_target="tpu_custom_call" | custom-call | tf_op jit(solution)/shard_map/inside/pallas_call | solution.py:452
  96.7 1.0 collective-permute-done.5
  97.7 1.0 collective-permute-done.6
  98.8 0.8 add_select_fusion.prior
  99.6 2.9 %gate.1 = bf16[256,512]{1,0:T(8,128)(2,1)} custom-call(bf16[256,512]{1,0:T(8,128)(2,1)} %bitcast.29, f32[256,512]{1,0:T(8,128)} %inside.1.local, bf16[256,256]{1,0:T(8,128)(2,1)} %get-tuple-element.34.maps, f32[24,256]{1,0:T(8,128)} %get-tuple-element.35.meta, f32[128,512]{1,0:T(8,128)} %add_select_fusion.prior, f32[8,512]{1,0:T(8,128)} %all_gather.3.refs_2_.params), custom_call_target="tpu_custom_call" | custom-call | tf_op jit(solution)/shard_map/gate/pallas_call | solution.py:479
  102.5 1.6 %collective-permute-start.7 = (bf16[256,512]{1,0:T(8,128)(2,1)}, bf16[256,512]{1,0:T(8,128)(2,1)S(1)}, u32[]{:S(2)}, u32[]{:S(2)}) collective-permute-start(bf16[256,512]{1,0:T(8,128)(2,1)} %gate.1), channel_id=1, source_target_pairs={{0,0},{1,1},{2,6},{3,7},{4,4},{5,5},{6,2},{7,3},{8,8},{9,9},{10,14... | collective-permute-start | bytes 786440 | tf_op jit(solution)/shard_map/ppermute | solution.py:629
  104.1 1.4 collective-permute-start.8
  105.5 9.0 %collective-permute-done.9.far = bf16[256,512]{1,0:T(8,128)(2,1)S(1)} collective-permute-done((bf16[256,512]{1,0:T(8,128)(2,1)}, bf16[256,512]{1,0:T(8,128)(2,1)S(1)}, u32[]{:S(2)}, u32[]{:S(2)}) %collective-permute-start.9) | collective-permute-done | bytes 262176 | tf_op jit(solution)/shard_map/ppermute | solution.py:629
  114.7 6.4 %collective-permute-done.10.both = bf16[256,512]{1,0:T(8,128)(2,1)S(1)} collective-permute-done((bf16[256,512]{1,0:T(8,128)(2,1)S(1)}, bf16[256,512]{1,0:T(8,128)(2,1)S(1)}, u32[]{:S(2)}, u32[]{:S(2)}) %collective-permute-start.10) | collective-permute-done | bytes 262176 | tf_op jit(solution)/shard_map/ppermute | solution.py:21
  121.1 0.7 copy-done.7
  121.8 6.7 %output.1 = bf16[512,2048]{1,0:T(8,128)(2,1)} custom-call(bf16[256,512]{1,0:T(8,128)(2,1)} %copy-done.5, bf16[256,512]{1,0:T(8,128)(2,1)} %copy-done.6, bf16[256,512]{1,0:T(8,128)(2,1)} %copy-done.4, bf16[256,512]{1,0:T(8,128)(2,1)} %copy-done.7, bf16[512,2048]{1,0:T(8,128)(2,1)} %weight_mine, bf16[512,2048]{1,0:T(8,128)(2,1)} %collective-permute-done.11.weight_other, ...), custom_call_target="tpu_custom_call" | custom-call | tf_op jit(solution)/shard_map/output/pallas_call | solution.py:550
  (49 shorter events, 0.6 us)
Async XLA Ops:
  6.5 1.9 %copy-start.2 = (bf16[1,1,1,256,1280]{4,3,2,1,0:T(8,128)(2,1)S(1)}, bf16[1,1,1,256,1280]{4,3,2,1,0:T(8,128)(2,1)}, u32[]{:S(2)}) copy-start(bf16[1,1,1,256,1280]{4,3,2,1,0:T(8,128)(2,1)} %param.18) | copy-start | bytes 1966084
  6.5 2.0 %copy-start.10 = (s32[1,2,1]{1,2,0:T(1,128)S(1)}, s32[1,2,1]{1,2,0:T(1,128)}, u32[]{:S(2)}) copy-start(s32[1,2,1]{1,2,0:T(1,128)} %param.19) | copy-start | bytes 28
  6.5 58.0 %reduce-scatter.5.cloned.1.call-start = ((), (), s32[]{:S(2)}) async-start(), calls=%async_computation.3 | async-start | bytes 2027520 | tf_op jit(solution)/shard_map/reduce_scatter | solution.py:587
  7.9 3.7 %collective-permute-start.1 = (bf16[256,2048]{1,0:T(8,128)(2,1)S(1)}, bf16[256,2048]{1,0:T(8,128)(2,1)S(1)}, u32[]{:S(2)}, u32[]{:S(2)}) collective-permute-start(bf16[256,2048]{1,0:T(8,128)(2,1)S(1)} %slice_bitcast_fusion), channel_id=1, source_target_pairs={{0,4},{4,0},{1,5},{5,1},{2,6},{6,2},{3,7},{7,3},{8,12},{12,8},{9,1... | collective-permute-start | bytes 3145736 | tf_op jit(solution)/shard_map/ppermute | solution.py:21
  8.4 3.2 %collective-permute-start = (bf16[256,1280]{1,0:T(8,128)(2,1)S(1)}, bf16[256,1280]{1,0:T(8,128)(2,1)S(1)}, u32[]{:S(2)}, u32[]{:S(2)}) collective-permute-start(bf16[256,1280]{1,0:T(8,128)(2,1)S(1)} %bitcast.27), channel_id=1, source_target_pairs={{0,4},{4,0},{1,5},{5,1},{2,6},{6,2},{3,7},{7,3},{8,12},{12,8},{9,1... | collective-permute-start | bytes 1966088 | tf_op jit(solution)/shard_map/ppermute | solution.py:21
  11.6 0.9 copy-start.3
  11.7 1.2 copy-start.1
  25.3 74.3 %reduce-scatter.3.cloned.1.call-start = ((), (), s32[]{:S(2)}) async-start(), calls=%async_computation.2 | async-start | bytes 1310720 | tf_op jit(solution)/shard_map/reduce_scatter | solution.py:597
  27.3 8.7 %copy-start.11 = (bf16[128]{0:T(256)(128)(2,1)S(1)}, bf16[128]{0:T(256)(128)(2,1)}, u32[]{:S(2)}) copy-start(bf16[128]{0:T(256)(128)(2,1)} %param.32) | copy-start | bytes 772
  27.3 8.7 %copy-start.9 = (bf16[4,128]{1,0:T(4,128)(2,1)S(1)}, bf16[4,128]{1,0:T(4,128)(2,1)}, u32[]{:S(2)}) copy-start(bf16[4,128]{1,0:T(4,128)(2,1)} %param.27) | copy-start | bytes 3076
  27.3 48.3 %copy-start = (bf16[512,2048]{1,0:T(8,128)(2,1)S(1)}, bf16[512,2048]{1,0:T(8,128)(2,1)}, u32[]{:S(2)}) copy-start(bf16[512,2048]{1,0:T(8,128)(2,1)} %weight_mine) | copy-start | bytes 6291460
  65.3 3.9 %collective-permute-start.2 = (bf16[16,768]{1,0:T(8,128)(2,1)S(1)}, bf16[16,768]{1,0:T(8,128)(2,1)S(1)}, u32[]{:S(2)}, u32[]{:S(2)}) collective-permute-start(bf16[16,768]{1,0:T(8,128)(2,1)S(1)} %slice_bitcast_fusion.1), channel_id=1, source_target_pairs={{0,1},{2,3},{8,9},{10,11},{16,17},{18,19},{24,25},{26,27},{1,8},{3... | collective-permute-start | bytes 73736 | tf_op jit(solution)/shard_map/ppermute | solution.py:600
  69.2 0.6 copy-start.8
  73.1 13.1 %collective-permute-start.3 = (bf16[144,512]{1,0:T(8,128)(2,1)}, bf16[144,512]{1,0:T(8,128)(2,1)S(1)}, u32[]{:S(2)}, u32[]{:S(2)}) collective-permute-start(bf16[144,512]{1,0:T(8,128)(2,1)} %get-tuple-element.36), channel_id=1, source_target_pairs={{0,1},{1,0},{2,3},{3,2},{4,5},{5,4},{6,7},{7,6},{8,9},{9,8},{10,11... | collective-permute-start | bytes 442376 | tf_op jit(solution)/shard_map/ppermute | solution.py:21
  75.6 38.9 %collective-permute-start.11 = (bf16[512,2048]{1,0:T(8,128)(2,1)S(1)}, bf16[512,2048]{1,0:T(8,128)(2,1)}, u32[]{:S(2)}, u32[]{:S(2)}) collective-permute-start(bf16[512,2048]{1,0:T(8,128)(2,1)S(1)} %copy-done), channel_id=1, source_target_pairs={{0,4},{4,0},{1,5},{5,1},{2,6},{6,2},{3,7},{7,3},{8,12},{12,8},{9,1... | collective-permute-start | bytes 6291464 | tf_op jit(solution)/shard_map/ppermute | solution.py:21
  87.3 9.4 %collective-permute-start.4 = (bf16[144,512]{1,0:T(8,128)(2,1)S(1)}, bf16[144,512]{1,0:T(8,128)(2,1)S(1)}, u32[]{:S(2)}, u32[]{:S(2)}) collective-permute-start(bf16[144,512]{1,0:T(8,128)(2,1)S(1)} %pad_maximum_fusion), channel_id=1, source_target_pairs={{0,24},{8,16},{16,8},{24,0},{1,25},{9,17},{17,9},{25,1},{2,26},{10... | collective-permute-start | bytes 442376 | tf_op jit(solution)/shard_map/ppermute | solution.py:21
  92.2 5.5 %collective-permute-start.5 = (bf16[144,512]{1,0:T(8,128)(2,1)S(1)}, bf16[144,512]{1,0:T(8,128)(2,1)S(1)}, u32[]{:S(2)}, u32[]{:S(2)}) collective-permute-start(bf16[144,512]{1,0:T(8,128)(2,1)S(1)} %pad_maximum_fusion), channel_id=1, source_target_pairs={{0,16},{8,24},{16,0},{24,8},{1,17},{9,25},{17,1},{25,9},{2,18},{10... | collective-permute-start | bytes 442376 | tf_op jit(solution)/shard_map/ppermute | solution.py:21
  92.7 5.9 %collective-permute-start.6 = (bf16[144,512]{1,0:T(8,128)(2,1)S(1)}, bf16[144,512]{1,0:T(8,128)(2,1)S(1)}, u32[]{:S(2)}, u32[]{:S(2)}) collective-permute-start(bf16[144,512]{1,0:T(8,128)(2,1)S(1)} %pad_maximum_fusion), channel_id=1, source_target_pairs={{0,8},{8,0},{16,24},{24,16},{1,9},{9,1},{17,25},{25,17},{2,10},{10... | collective-permute-start | bytes 442376 | tf_op jit(solution)/shard_map/ppermute | solution.py:21
  102.5 12.0 %collective-permute-start.9 = (bf16[256,512]{1,0:T(8,128)(2,1)}, bf16[256,512]{1,0:T(8,128)(2,1)S(1)}, u32[]{:S(2)}, u32[]{:S(2)}) collective-permute-start(bf16[256,512]{1,0:T(8,128)(2,1)} %gate.1), channel_id=1, source_target_pairs={{0,2},{1,3},{2,4},{3,5},{4,6},{5,7},{6,0},{7,1},{8,10},{9,11},{10,... | collective-permute-start | bytes 786440 | tf_op jit(solution)/shard_map/ppermute | solution.py:629
  102.5 12.0 %collective-permute-start.7 = (bf16[256,512]{1,0:T(8,128)(2,1)}, bf16[256,512]{1,0:T(8,128)(2,1)S(1)}, u32[]{:S(2)}, u32[]{:S(2)}) collective-permute-start(bf16[256,512]{1,0:T(8,128)(2,1)} %gate.1), channel_id=1, source_target_pairs={{0,0},{1,1},{2,6},{3,7},{4,4},{5,5},{6,2},{7,3},{8,8},{9,9},{10,14... | collective-permute-start | bytes 786440 | tf_op jit(solution)/shard_map/ppermute | solution.py:629
  104.1 10.6 %collective-permute-start.8 = (bf16[256,512]{1,0:T(8,128)(2,1)}, bf16[256,512]{1,0:T(8,128)(2,1)S(1)}, u32[]{:S(2)}, u32[]{:S(2)}) collective-permute-start(bf16[256,512]{1,0:T(8,128)(2,1)} %gate.1), channel_id=1, source_target_pairs={{0,1},{1,0},{2,7},{3,6},{4,5},{5,4},{6,3},{7,2},{8,9},{9,8},{10,15... | collective-permute-start | bytes 786440 | tf_op jit(solution)/shard_map/ppermute | solution.py:629
  114.5 6.6 %copy-start.4 = (bf16[256,512]{1,0:T(8,128)(2,1)}, bf16[256,512]{1,0:T(8,128)(2,1)S(1)}, u32[]{:S(2)}) copy-start(bf16[256,512]{1,0:T(8,128)(2,1)S(1)} %collective-permute-done.9.far) | copy-start | bytes 786436
  114.5 6.6 %collective-permute-start.10 = (bf16[256,512]{1,0:T(8,128)(2,1)S(1)}, bf16[256,512]{1,0:T(8,128)(2,1)S(1)}, u32[]{:S(2)}, u32[]{:S(2)}) collective-permute-start(bf16[256,512]{1,0:T(8,128)(2,1)S(1)} %collective-permute-done.9.far), channel_id=1, source_target_pairs={{0,1},{1,0},{2,3},{3,2},{4,5},{5,4},{6,7},{7,6},{8,9},{9,8},{10,11... | collective-permute-start | bytes 786440 | tf_op jit(solution)/shard_map/ppermute | solution.py:21
  114.5 6.6 %copy-start.5 = (bf16[256,512]{1,0:T(8,128)(2,1)}, bf16[256,512]{1,0:T(8,128)(2,1)S(1)}, u32[]{:S(2)}) copy-start(bf16[256,512]{1,0:T(8,128)(2,1)S(1)} %collective-permute-done.7.here) | copy-start | bytes 786436
  114.7 6.4 %copy-start.6 = (bf16[256,512]{1,0:T(8,128)(2,1)}, bf16[256,512]{1,0:T(8,128)(2,1)S(1)}, u32[]{:S(2)}) copy-start(bf16[256,512]{1,0:T(8,128)(2,1)S(1)} %collective-permute-done.8.near) | copy-start | bytes 786436
  121.1 0.7 copy-start.7
Sparse Core Ops, SparseCore 0:
  25.4 39.0 reduce-scatter.4
  67.0 29.3 reduce-scatter.2

commit v4 on v3

--- a/solution.py
+++ b/solution.py
@@ -204,9 +204,10 @@
 
 
 def enter_body(
-    table, feats_mine, feats_other, vision_gain, proj, text, text_other, newline, gain, xz, bc, dt,
-    crops_out, rows_out, first_out,
-    feats, normed, proj_tiles, tails, weights, crops, rows, first, sems, out_sems,
+    table, dt_bias, a_log, skip, feats_mine, feats_other, vision_gain, proj, text, text_other,
+    newline, gain, xz, bc, dt, conv_x, out_gain,
+    crops_out, rows_out, first_out, keep_out, send_out,
+    feats, normed, proj_tiles, tails, weights, crops, rows, first, maps, sems, out_sems,
 ):
     half = tails.shape[1]
     tiles, _, tile = proj_tiles.shape
@@ -221,7 +222,7 @@
     ]
     load_tails = [
         pltpu.make_async_copy(text.at[pl.ds(half, half), :], tails.at[0], sems.at[2 + tiles]),
-        pltpu.make_async_copy(text_other, tails.at[1], sems.at[3 + tiles]),
+        pltpu.make_async_copy(text_other.at[pl.ds(half, half), :], tails.at[1], sems.at[3 + tiles]),
     ]
     load_weights = [
         pltpu.make_async_copy(
@@ -236,7 +237,7 @@
         copy.start()
     gain_row = gain[...].reshape(1, -1)
     rank = lax.axis_index("dp")
-    stays = table[0, rank, 0] == rank
+    stays = table[0, 0, rank] == rank
     load_feats[0].wait()
     load_feats[1].wait()
     for index in range(2):
@@ -284,17 +285,40 @@
         copy.start()
     for copy in load_weights:
         copy.wait()
+    chip = lax.axis_index("tensor")
+    lane = lax.broadcasted_iota(jnp.int32, (1, 128), 1)
+    own = [conv_x[...].astype(F32), out_gain[...].reshape(1, 128).astype(F32)]
+    for value in (dt_bias[0], a_log[0], skip[0]):
+        whole = jnp.full((1, 128), value, F32)
+        high = whole.astype(BF16).astype(F32)
+        middle = (whole - high).astype(BF16).astype(F32)
+        low = whole - high - middle
+        pieces = jnp.where(lane < 32, high, jnp.where(lane < 64, middle, low))
+        own.append(jnp.where(lane < 96, pieces, 0.0))
+    own = jnp.concatenate(own, 0)
+    slots = jnp.concatenate([jnp.where(chip == slot, own, 0.0) for slot in range(4)], 1)
     for part in range(4):
         main = rows[part * half : (part + 1) * half, :]
-        for i in range(3):
+        maps[part] = jnp.dot(main, weights[2], preferred_element_type=F32).astype(BF16)
+        goes = pltpu.make_async_copy(maps.at[part], send_out.at[part // 2], out_sems.at[6 + part])
+        remains = pltpu.make_async_copy(
+            maps.at[part], keep_out.at[part // 2], out_sems.at[6 + part]
+        )
+        here = chip % 2 == part % 2
+        pl.when(here)(remains.start)
+        pl.when(jnp.logical_not(here))(goes.start)
+        departures.append(goes)
+    for part in range(4):
+        main = rows[part * half : (part + 1) * half, :]
+        for i in range(2):
             first[part, 0:half, i * 256 : i * 256 + 256] = jnp.dot(
                 main, weights[i], preferred_element_type=F32
             ).astype(BF16)
         steps = contract(dt[...], main, ((1,), (1,)))
         sums = contract(ones, squares[part].astype(BF16), ((1,), (1,)))
-        first[part, half : half + 8, 0:half] = jnp.concatenate(
-            [steps[0:4], sums[0:4]], 0
-        ).astype(BF16)
+        sums = jnp.concatenate([steps[0:4], sums[0:4]], 0)
+        sums = jnp.concatenate([sums, jnp.zeros((8, 512 - half), F32)], 1)
+        first[part, half : half + 16, :] = jnp.concatenate([sums, slots], 0).astype(BF16)
         departures.append(
             pltpu.make_async_copy(first.at[part], first_out.at[part], out_sems.at[2 + part])
         )
@@ -304,7 +328,8 @@
 
 
 def enter(
-    table, feats_mine, feats_other, vision_gain, proj, text, text_other, newline, gain, xz, bc, dt
+    table, dt_bias, a_log, skip, feats_mine, feats_other, vision_gain, proj, text, text_other,
+    newline, gain, xz, bc, dt, conv_x, out_gain,
 ):
     half, vision = feats_mine.shape
     columns = text.shape[1]
@@ -313,13 +338,16 @@
     near = pl.BlockSpec(memory_space=pltpu.VMEM)
     return pl.pallas_call(
         enter_body,
-        in_specs=[pl.BlockSpec(memory_space=pltpu.SMEM), whole, whole, near, whole, whole, whole]
-        + [near, near, whole, whole, near],
-        out_specs=[whole, whole, whole],
+        in_specs=[pl.BlockSpec(memory_space=pltpu.SMEM)] * 4
+        + [whole, whole, near, whole, whole, whole]
+        + [near, near, whole, whole, near, near, near],
+        out_specs=[whole] * 5,
         out_shape=[
             jax.ShapeDtypeStruct((2 * half, columns), BF16),
             jax.ShapeDtypeStruct((4 * half, columns), BF16),
-            jax.ShapeDtypeStruct((4, half + 8, 768), BF16),
+            jax.ShapeDtypeStruct((4, half + 16, 512), BF16),
+            jax.ShapeDtypeStruct((2, half, 256), BF16),
+            jax.ShapeDtypeStruct((2, half, 256), BF16),
         ],
         scratch_shapes=[
             pltpu.VMEM((2, half, vision), BF16),
@@ -329,12 +357,16 @@
             pltpu.VMEM((3, columns, 256), BF16),
             pltpu.VMEM((2 * half, columns), BF16),
             pltpu.VMEM((4 * half, columns), BF16),
-            pltpu.VMEM((4, half + 8, 768), BF16),
+            pltpu.VMEM((4, half + 16, 512), BF16),
+            pltpu.VMEM((4, half, 256), BF16),
             pltpu.SemaphoreType.DMA((9 + tiles,)),
-            pltpu.SemaphoreType.DMA((6,)),
+            pltpu.SemaphoreType.DMA((10,)),
         ],
         name="enter",
-    )(table, feats_mine, feats_other, vision_gain, proj, text, text_other, newline, gain, xz, bc, dt)
+    )(
+        table, dt_bias, a_log, skip, feats_mine, feats_other, vision_gain, proj, text, text_other,
+        newline, gain, xz, bc, dt, conv_x, out_gain,
+    )
 
 
 def gates_body(rows, weight, out):
@@ -371,17 +403,21 @@
     return total
 
 
-def scan_body(width, first, before, params, taps_maps, streams, maps, meta, state):
-    half = first.shape[0] - 8
-    sums = first[half : half + 8, 0:half].astype(F32)
+def scan_body(
+    width, first, kept, received, before, taps_maps, streams, maps, meta, state, params
+):
+    half = first.shape[0] - 16
+    slots = first[half : half + 16, :].astype(F32)[8:16]
+    params[...] = slots
+    sums = first[half : half + 16, 0:half].astype(F32)[0:8]
     scale = lax.rsqrt(sums[4:5] / width + EPS)
     sums_before = before[8:16, half - 128 : half].astype(F32)
     scale_before = lax.rsqrt(sums_before[4:5] / width + EPS)
     head = lax.broadcasted_iota(jnp.int32, (8, 512), 1) // 128
     owner = (head == lax.broadcasted_iota(jnp.int32, (8, 512), 0)).astype(F32)
-    scalars = params[5:8, :]
-    bias = jnp.sum(owner * scalars[0:1], 1, keepdims=True) * (1.0 / 128)
-    rate = jnp.sum(owner * scalars[1:2], 1, keepdims=True) * (1.0 / 128)
+    scalars = slots[5:8]
+    bias = jnp.sum(owner * scalars[0:1], 1, keepdims=True) * (1.0 / 32)
+    rate = jnp.sum(owner * scalars[1:2], 1, keepdims=True) * (1.0 / 32)
     raw = sums * scale + bias
     step = jnp.maximum(raw, 0.0) + jnp.log1p(jnp.exp(-jnp.abs(raw)))
     decays = -jnp.exp(rate) * step
@@ -394,12 +430,12 @@
     carry = jnp.exp(final - cumulative) * step
     scale_main = columns_of(jnp.broadcast_to(scale, (8, half)))[:, 0:1]
     scale_edge = columns_of(jnp.broadcast_to(scale_before, (8, 128)))[120:128, 0:1]
-    taps_x = params[0:4, :]
+    taps_x = slots[0:4]
     edge = before[0:8, :].astype(F32) * scale_edge
-    x = silu(filtered(first[0:half, 0:512].astype(F32) * scale_main, edge[:, 0:512], taps_x))
+    x = silu(filtered(first[0:half, :].astype(F32) * scale_main, edge[:, 0:512], taps_x))
     both = silu(
         filtered(
-            first[0:half, 512:768].astype(F32) * scale_main,
+            (kept[...].astype(F32) + received[...].astype(F32)) * scale_main,
             edge[:, 512:768],
             taps_maps[...].astype(F32),
         )
@@ -415,8 +451,8 @@
     meta[16:24, :] = jnp.broadcast_to(scale, (8, half))
 
 
-def scan(width, first, before, params, taps_maps):
-    half = first.shape[0] - 8
+def scan(width, first, kept, received, before, taps_maps):
+    half = kept.shape[0]
     return pl.pallas_call(
         lambda *refs: scan_body(width, *refs),
         out_shape=[
@@ -424,9 +460,10 @@
             jax.ShapeDtypeStruct((half, 256), BF16),
             jax.ShapeDtypeStruct((24, half), F32),
             jax.ShapeDtypeStruct((144, 512), BF16),
+            jax.ShapeDtypeStruct((8, 512), F32),
         ],
         name="scan",
-    )(first, before, params, taps_maps)
+    )(first, kept, received, before, taps_maps)
 
 
 def inside_body(streams, maps, meta, params, out):
@@ -445,7 +482,8 @@
         gaps = cum_cols[:, head : head + 1] - cumulative[head : head + 1]
         weights = jnp.exp(jnp.where(lower, gaps, 0.0)) * scores * step[head : head + 1]
         y = jnp.dot(weights.astype(BF16), x, preferred_element_type=F32)
-        out[:, cols] = y + params[7:8, cols] * x.astype(F32)
+        through = jnp.sum(params[7:8, cols], 1, keepdims=True) * (1.0 / 32)
+        out[:, cols] = y + through * x.astype(F32)
 
 
 def inside(streams, maps, meta, params):
@@ -483,87 +521,6 @@
     )(second, local, maps, meta, prior, params)
 
 
-def output_body(
-    here, near, far, both, weight_mine, weight_other, crops, text, newline, out_hbm,
-    blocks, weights, hidden, out, sems, out_sems,
-):
-    half = hidden.shape[1]
-    tiles, _, _, tile = weights.shape
-    chip = lax.axis_index("tensor")
-    load_hidden = [
-        pltpu.make_async_copy(crops.at[pl.ds(0, half), :], hidden.at[0], sems.at[0]),
-        pltpu.make_async_copy(text.at[pl.ds(half, half), :], hidden.at[1], sems.at[1]),
-    ]
-    load_blocks = [
-        pltpu.make_async_copy(source, blocks.at[jnp.bitwise_xor(chip, bits)], sems.at[2 + bits])
-        for bits, source in enumerate((here, near, far, both))
-    ]
-    load_weights = [
-        [
-            pltpu.make_async_copy(
-                source.at[:, pl.ds(i * tile, tile)], weights.at[i, index], sems.at[6 + 2 * i + index]
-            )
-            for index, source in enumerate((weight_mine, weight_other))
-        ]
-        for i in range(tiles)
-    ]
-    for copy in load_blocks + load_weights[0] + load_hidden:
-        copy.start()
-    for pair in load_weights[1:]:
-        for copy in pair:
-            copy.start()
-    for copy in load_blocks:
-        copy.wait()
-    departures = []
-    for i in range(tiles):
-        cols = slice(i * tile, (i + 1) * tile)
-        for copy in load_weights[i]:
-            copy.wait()
-        if i == 0:
-            for copy in load_hidden:
-                copy.wait()
-            head = hidden[1, 0:8, :].astype(F32)
-            line = newline[...].reshape(1, -1).astype(F32)
-            top = lax.broadcasted_iota(jnp.int32, (8, 1), 0) == 0
-            hidden[1, 0:8, :] = jnp.where(top, line, head).astype(BF16)
-        for index in range(2):
-            mixed = jnp.dot(blocks[index], weights[i, 0], preferred_element_type=F32)
-            mixed = mixed + jnp.dot(blocks[2 + index], weights[i, 1], preferred_element_type=F32)
-            out[i, index * half : (index + 1) * half, :] = (
-                hidden[index, :, cols].astype(F32) + mixed
-            ).astype(BF16)
-        departures.append(
-            pltpu.make_async_copy(out.at[i], out_hbm.at[:, pl.ds(i * tile, tile)], out_sems.at[i])
-        )
-        departures[-1].start()
-    for copy in departures:
-        copy.wait()
-
-
-def output(pieces, weight_mine, weight_other, crops, text, newline):
-    section, columns = text.shape
-    half = section // 2
-    tiles = 4
-    tile = columns // tiles
-    inner = weight_mine.shape[0]
-    whole = pl.BlockSpec(memory_space=pl.ANY)
-    return pl.pallas_call(
-        output_body,
-        in_specs=[whole] * 8 + [pl.BlockSpec(memory_space=pltpu.VMEM)],
-        out_specs=whole,
-        out_shape=jax.ShapeDtypeStruct((section, columns), BF16),
-        scratch_shapes=[
-            pltpu.VMEM((4, half, inner), BF16),
-            pltpu.VMEM((tiles, 2, inner, tile), BF16),
-            pltpu.VMEM((2, half, columns), BF16),
-            pltpu.VMEM((tiles, section, tile), BF16),
-            pltpu.SemaphoreType.DMA((6 + 2 * tiles,)),
-            pltpu.SemaphoreType.DMA((tiles,)),
-        ],
-        name="output",
-    )(*pieces, weight_mine, weight_other, crops, text, newline)
-
-
 def per_device_halves(
     text_embed, crop_feats, crop_dest, vision_gain, proj_weight, newline, norm_gain, xz_weight,
     dt_weight, bc_weight, conv_x, conv_bc, dt_bias, a_log, skip, out_gain, out_weight,
@@ -577,32 +534,38 @@
     width = columns * lax.axis_size("tensor")
     feats = crop_feats[0, 0, 0]
     feats_other = swapped(feats, "dp", 1)
-    text_other = swapped(text[half:], "dp", 1)
-    crops, rows, first = enter(
-        crop_dest, feats, feats_other, vision_gain, proj_weight, text, text_other, newline,
-        norm_gain, xz_weight, bc_weight, dt_weight.T,
-    )
-    later = (conv_x, out_gain, dt_bias, a_log, skip, out_weight, first, rows)
-    conv_x, out_gain, dt_bias, a_log, skip, out_weight, first, rows = lax.optimization_barrier(later)
+    text_other = swapped(text, "dp", 1)
+    crops, rows, first, keep, send = enter(
+        crop_dest.transpose(0, 2, 1), dt_bias, a_log, skip, feats, feats_other, vision_gain,
+        proj_weight, text, text_other, newline, norm_gain, xz_weight, bc_weight, dt_weight.T,
+        conv_x, out_gain,
+    )
+    out_weight, newline, rows, first = lax.optimization_barrier((out_weight, newline, rows, first))
     first = lax.psum_scatter(first, "tensor", scatter_dimension=0, tiled=False)
+    pair = keep.astype(F32) + swapped(send, "tensor", 1).astype(F32)
+    lower = my_chip < 2
+    received = swapped(jnp.where(lower, pair[1], pair[0]).astype(BF16), "tensor", 2)
+    kept = jnp.where(lower, pair[0], pair[1]).astype(BF16)
     second = gates(rows, xz_weight)
     weight_other = swapped(out_weight, "dp", 1)
-    own = jnp.concatenate(
-        [conv_x.astype(F32), out_gain.astype(F32)[None]]
-        + [jnp.broadcast_to(value[:, None], (1, 128)) for value in (dt_bias, a_log, skip)],
-        0,
-    )
-    params = lax.all_gather(own, "tensor", axis=1, tiled=True)
-    second, params = lax.optimization_barrier((second, params))
+    weights = (
+        jnp.where(lower, out_weight, weight_other), jnp.where(lower, weight_other, out_weight)
+    )
+    late = my_chip % 2 == 1
+    head = crops[:half]
+    tail = jnp.where(jnp.arange(half)[:, None] == 0, newline[None], text[half:])
+    hidden = (jnp.where(late, tail, head), jnp.where(late, head, tail))
+    second, weights, hidden = lax.optimization_barrier((second, weights, hidden))
     second = lax.psum_scatter(second, "tensor", scatter_dimension=0, tiled=False)
     route = [(i, i + 1) for i in range(0, 4 * segment_count, 2)]
     route += [(i, i + 3) for i in range(1, 4 * segment_count - 4, 2)]
-    before = lax.ppermute(first[half - 8 :], ("segment", "tensor"), route)
-    streams, maps, meta, state = scan(width, first, before, params, conv_bc)
+    ends = (kept[half - 8 :].astype(F32) + received[half - 8 :].astype(F32)).astype(BF16)
+    before = jnp.concatenate([first[half - 8 : half + 8], jnp.pad(ends, ((0, 8), (0, 0)))], 1)
+    before = lax.ppermute(before, ("segment", "tensor"), route)
+    streams, maps, meta, state, params = scan(width, first, kept, received, before, conv_bc)
     local = inside(streams, maps, meta, params)
     partner = swapped(state, "tensor", 1).astype(F32)
     state = state.astype(F32)
-    late = my_chip % 2 == 1
     early_state = jnp.where(late, partner, state)[:128]
     late_state = jnp.where(late, state, partner)[:128]
     early_decay = jnp.where(late, partner, state)[128:129]
@@ -631,8 +594,15 @@
         )
         for bits in (1, 2, 0)
     )
-    pieces = (here, near, far, swapped(far, "tensor", 1))
-    return output(pieces, out_weight, weight_other, crops, text, newline)[None]
+    both = swapped(far, "tensor", 1)
+    out = jnp.zeros((section, columns), BF16)
+    for index, pair in enumerate(((here, far), (near, both))):
+        mixed = jnp.dot(pair[0], weights[0], preferred_element_type=F32)
+        mixed = mixed + jnp.dot(pair[1], weights[1], preferred_element_type=F32)
+        block = (hidden[index].astype(F32) + mixed).astype(BF16)
+        start = jnp.where(late, half, 0) if index == 0 else jnp.where(late, 0, half)
+        out = lax.dynamic_update_slice(out, block, (start, 0))
+    return out[None]
 
 
 def per_device(*args):

time: 136 us -> 128 us (0.941)
  blocking collectives: 15.8 us -> 0 us
  other arithmetic: 1.95 us -> 11 us
  Pallas kernels: 36.8 us -> 30.1 us
  starting transfers between devices: 15.2 us -> 20.8 us
  matrix products: 0 us -> 3.93 us
  waiting for transfers between devices: 44.7 us -> 41.1 us
    all_gather x1 -> x0, blocking collectives: 15.8 us -> none  [per_device_halves(): params = lax.all_gather(own, 'tensor', axis=1, tiled=True)]
    reduce_scatter x1, waiting for transfers between devices: 12.7 us -> 1.88 us  [per_device_halves(): first = lax.psum_scatter(first, 'tensor', scatter_dimension=0, tiled=False)]
    ppermute x8 -> x10, waiting for transfers between devices: 21.5 us -> 29.6 us  [swapped(): lax.ppermute(block, axis, [(i, i ^ bits) for i in range(lax.axis_size(axi...]
    pallas_call x1 -> x0, Pallas kernels: 6.67 us -> none  [output(): pl.pallas_call(output_body, in_specs=[whole] * 8 + [pl.BlockSpec(memory_s...]
    select_n x0 -> x2, other arithmetic: none -> 6.32 us  [the longest x1 3.89 us: per_device_halves(): jnp.where(lower, weight_other, out_weight)]
    ppermute x8 -> x10, starting transfers between devices: 9.69 us -> 14.5 us  [swapped(): lax.ppermute(block, axis, [(i, i ^ bits) for i in range(lax.axis_size(axi...]
    dot_general x0 -> x4, matrix products: none -> 3.93 us  [the longest x2 2.5 us: per_device_halves(): mixed = mixed + jnp.dot(pair[1], weights[1], preferred_element_type=F32)]
    slice x2 -> x1, local copies, waits for them, and re-layouts: 2.1 us -> 0.72 us  [per_device_halves(): first[half - 8:half + 8]]
  transfers between devices with their start and end apart: 14 -> 16, of which waited for: 9 -> 10; matrix products, arithmetic and copies ran while one was open for 2% -> 11% of each run, Pallas kernels for 13% -> 12%
where the time goes in v4:
time: 128 us
  waiting for transfers between devices  41.1 us (32%)
  Pallas kernels  30.1 us (24%)
  starting transfers between devices  20.8 us (16%)
  between operations  15.5 us (12%)
  other arithmetic  11 us (9%)
  local copies, waits for them, and re-layouts  5.12 us (4%)
  matrix products  3.93 us (3%)
    ppermute x10, waiting for transfers between devices, swapped(): lax.ppermute(block, axis, [(i, i ^ bits) for i in range(lax.axis_size(axi...  29.6 us
    ppermute x10, starting transfers between devices, swapped(): lax.ppermute(block, axis, [(i, i ^ bits) for i in range(lax.axis_size(axi...  14.5 us
    pallas_call x1, Pallas kernels, enter(): pl.pallas_call(enter_body, in_specs=[pl.BlockSpec(memory_space=pltpu.SMEM...  12.4 us
    pallas_call x1, Pallas kernels, gates(): pl.pallas_call(gates_body, grid=(4,), in_specs=[pl.BlockSpec((half, colum...  8.56 us
    ppermute x3, waiting for transfers between devices, per_device_halves(): lax.ppermute(normed, ('dp', 'tensor'), [(i, (i if i % 4 < 2 else i ^ 4) ^...  8.32 us
    unnamed x20, local copies, waits for them, and re-layouts  4.14 us
    select_n x1, other arithmetic, per_device_halves(): jnp.where(lower, weight_other, out_weight)  3.89 us
    pallas_call x1, Pallas kernels, scan(): pl.pallas_call(lambda *refs: scan_body(width, *refs), out_shape=[jax.Shap...  3.43 us
  transfers between devices with their start and end apart: 16, of which 10 were waited for; matrix products, arithmetic and copies ran while one was open for 11% of the time, Pallas kernels for 12%

profile of v4, /device:TPU:0, one launch (start us, length us, event | category | flops | bytes accessed | tf_op | source)
XLA Modules:
  0.0 127.7 jit_solution(3851541544565126577)
XLA Ops:
  9.0 2.9 %collective-permute-done.feats_other = bf16[256,1280]{1,0:T(8,128)(2,1)S(1)} collective-permute-done((bf16[256,1280]{1,0:T(8,128)(2,1)}, bf16[256,1280]{1,0:T(8,128)(2,1)S(1)}, u32[]{:S(2)}, u32[]{:S(2)}) %collective-permute-start) | collective-permute-done | bytes 655392 | tf_op jit(solution)/shard_map/ppermute | solution.py:21
  11.9 0.8 copy-done.5
  13.5 12.4 %enter.1 = (bf16[512,2048]{1,0:T(8,128)(2,1)}, bf16[1024,2048]{1,0:T(8,128)(2,1)}, bf16[4,272,512]{2,1,0:T(8,128)(2,1)}, bf16[2,256,256]{2,1,0:T(8,128)(2,1)}, bf16[2,256,256]{2,1,0:T(8,128)(2,1)}) custom-call(s32[1,1,2]{2,1,0:T(1,128)} %bitcast.56, f32[1]{0:T(128)S(6)} %copy.20.dt_bias, f32[1]{0:T(128)S(6)} %copy.21.a_log, f32[1]{0:T(128)S(6)} %copy.22.skip, ...), custom_call_target="tpu_custom_call" | custom-call | tf_op jit(solution)/shard_map/enter/pallas_call | solution.py:339
  26.4 2.8 %collective-permute-start.3 = (bf16[2,256,256]{2,1,0:T(8,128)(2,1)}, bf16[2,256,256]{2,1,0:T(8,128)(2,1)S(1)}, u32[]{:S(2)}, u32[]{:S(2)}) collective-permute-start(bf16[2,256,256]{2,1,0:T(8,128)(2,1)} %get-tuple-element.34), channel_id=1, source_target_pairs={{0,1},{1,0},{2,3},{3,2},{4,5},{5,4},{6,7},{7,6},{8,9},{9,8},{10,11... | collective-permute-start | bytes 786440 | tf_op jit(solution)/shard_map/ppermute | solution.py:21
  29.2 7.6 %collective-permute-done.3 = bf16[2,256,256]{2,1,0:T(8,128)(2,1)S(1)} collective-permute-done((bf16[2,256,256]{2,1,0:T(8,128)(2,1)}, bf16[2,256,256]{2,1,0:T(8,128)(2,1)S(1)}, u32[]{:S(2)}, u32[]{:S(2)}) %collective-permute-start.3) | collective-permute-done | bytes 262176 | tf_op jit(solution)/shard_map/ppermute | solution.py:21
  36.8 1.0 convert_add_fusion
  37.9 3.0 %collective-permute-start.4 = (bf16[256,256]{1,0:T(8,128)(2,1)S(1)}, bf16[256,256]{1,0:T(8,128)(2,1)S(1)}, u32[]{:S(2)}, u32[]{:S(2)}) collective-permute-start(bf16[256,256]{1,0:T(8,128)(2,1)S(1)} %get-tuple-element.52), channel_id=1, source_target_pairs={{0,2},{1,3},{2,0},{3,1},{4,6},{5,7},{6,4},{7,5},{8,10},{9,11},{10,... | collective-permute-start | bytes 393224 | tf_op jit(solution)/shard_map/ppermute | solution.py:21
  40.9 2.4 %broadcast_select_fusion.2 = (bf16[256,2048]{1,0:T(8,128)(2,1)S(1)}, bf16[256,2048]{1,0:T(8,128)(2,1)}) fusion(pred[]{:T(512)S(6)} %eq.34, bf16[512,2048]{1,0:T(8,128)(2,1)} %get-tuple-element.29, bf16[1,512,2048]{2,1,0:T(8,128)(2,1)S(1)} %copy-done.1, bf16[2048]{0:T(1024)(128)(2,1)S(1)} %copy-done.9, pred[256]{0:T(512)(128)(4,1)S(1)} %iota_compare_fusion.1), kind=kLoop, calls=%fused_computation.12 | loop fusion | flops 1572864 | bytes 4198657 | tf_op jit(solution)/shard_map/jit(_where)/select_n | solution.py:557
  43.4 8.6 %gates.1 = bf16[4,256,512]{2,1,0:T(8,128)(2,1)} custom-call(bf16[1024,2048]{1,0:T(8,128)(2,1)} %get-tuple-element.26.rows, bf16[2048,1024]{1,0:T(8,128)(2,1)} %weight.1), custom_call_target="tpu_custom_call" | custom-call | tf_op jit(solution)/shard_map/gates/pallas_call | solution.py:383
  51.9 3.9 %collective-permute-done.4.refs_2_ = bf16[256,256]{1,0:T(8,128)(2,1)S(1)} collective-permute-done((bf16[256,256]{1,0:T(8,128)(2,1)S(1)}, bf16[256,256]{1,0:T(8,128)(2,1)S(1)}, u32[]{:S(2)}, u32[]{:S(2)}) %collective-permute-start.4) | collective-permute-done | bytes 131104 | tf_op jit(solution)/shard_map/ppermute | solution.py:21
  55.8 3.9 %broadcast_select_fusion = (bf16[512,2048]{1,0:T(8,128)(2,1)S(1)}, bf16[512,2048]{1,0:T(8,128)(2,1)}) fusion(bf16[512,2048]{1,0:T(8,128)(2,1)} %collective-permute-done.2, bf16[512,2048]{1,0:T(8,128)(2,1)} %param.33, pred[]{:T(512)S(6)} %lt.11), kind=kLoop, calls=%fused_computation.7 | loop fusion | flops 2097152 | bytes 8388609 | tf_op jit(solution)/shard_map/jit(_where)/select_n | solution.py:552
  59.7 1.9 %reduce-scatter.5.cloned.1.call-done = bf16[1,272,512]{2,1,0:T(8,128)(2,1)} async-done(((bf16[4,272,512]{2,1,0:T(8,128)(2,1)}), bf16[1,272,512]{2,1,0:T(8,128)(2,1)}) %reduce-scatter.5.cloned.1.call-update) | async-done | bytes 278544 | tf_op jit(solution)/shard_map/reduce_scatter | solution.py:544
  62.3 3.4 %collective-permute-start.5 = (bf16[16,768]{1,0:T(8,128)(2,1)S(1)}, bf16[16,768]{1,0:T(8,128)(2,1)S(1)}, u32[]{:S(2)}, u32[]{:S(2)}) collective-permute-start(bf16[16,768]{1,0:T(8,128)(2,1)S(1)} %fusion.12), channel_id=1, source_target_pairs={{0,1},{2,3},{8,9},{10,11},{16,17},{18,19},{24,25},{26,27},{1,8},{3... | collective-permute-start | bytes 73736 | tf_op jit(solution)/shard_map/ppermute | solution.py:564
  65.7 1.3 %collective-permute-done.5.refs_3_ = bf16[16,768]{1,0:T(8,128)(2,1)S(1)} collective-permute-done((bf16[16,768]{1,0:T(8,128)(2,1)S(1)}, bf16[16,768]{1,0:T(8,128)(2,1)S(1)}, u32[]{:S(2)}, u32[]{:S(2)}) %collective-permute-start.5) | collective-permute-done | bytes 24608 | tf_op jit(solution)/shard_map/ppermute | solution.py:564
  67.7 3.4 %scan.1 = (bf16[256,512]{1,0:T(8,128)(2,1)}, bf16[256,256]{1,0:T(8,128)(2,1)}, f32[24,256]{1,0:T(8,128)}, bf16[144,512]{1,0:T(8,128)(2,1)}, f32[8,512]{1,0:T(8,128)}) custom-call(bf16[272,512]{1,0:T(8,128)(2,1)} %bitcast.48, bf16[256,256]{1,0:T(8,128)(2,1)} %bitcast.47, bf16[256,256]{1,0:T(8,128)(2,1)} %copy-done.7, bf16[16,768]{1,0:T(8,128)(2,1)} %copy-done.8, ...), custom_call_target="tpu_custom_call" | custom-call | tf_op jit(solution)/shard_map/scan/pallas_call | solution.py:456
  71.1 2.4 %collective-permute-start.6 = (bf16[144,512]{1,0:T(8,128)(2,1)}, bf16[144,512]{1,0:T(8,128)(2,1)S(1)}, u32[]{:S(2)}, u32[]{:S(2)}) collective-permute-start(bf16[144,512]{1,0:T(8,128)(2,1)} %get-tuple-element.39), channel_id=1, source_target_pairs={{0,1},{1,0},{2,3},{3,2},{4,5},{5,4},{6,7},{7,6},{8,9},{9,8},{10,11... | collective-permute-start | bytes 442376 | tf_op jit(solution)/shard_map/ppermute | solution.py:21
  73.5 11.0 %collective-permute-done.6 = bf16[144,512]{1,0:T(8,128)(2,1)S(1)} collective-permute-done((bf16[144,512]{1,0:T(8,128)(2,1)}, bf16[144,512]{1,0:T(8,128)(2,1)S(1)}, u32[]{:S(2)}, u32[]{:S(2)}) %collective-permute-start.6) | collective-permute-done | bytes 147488 | tf_op jit(solution)/shard_map/ppermute | solution.py:21
  84.5 1.0 convert_select_fusion.1
  86.2 3.5 %collective-permute-start.7 = (bf16[144,512]{1,0:T(8,128)(2,1)}, bf16[144,512]{1,0:T(8,128)(2,1)}, u32[]{:S(2)}, u32[]{:S(2)}) collective-permute-start(bf16[144,512]{1,0:T(8,128)(2,1)} %pad_maximum_fusion), channel_id=1, source_target_pairs={{0,24},{8,16},{16,8},{24,0},{1,25},{9,17},{17,9},{25,1},{2,26},{10... | collective-permute-start | bytes 442376 | tf_op jit(solution)/shard_map/ppermute | solution.py:21
  90.3 1.3 collective-permute-start.9
  91.5 2.8 %inside.1.local = f32[256,512]{1,0:T(8,128)} custom-call(bf16[256,512]{1,0:T(8,128)(2,1)} %get-tuple-element.35.streams, bf16[256,256]{1,0:T(8,128)(2,1)} %get-tuple-element.36.maps, f32[24,256]{1,0:T(8,128)} %get-tuple-element.37.meta, f32[8,512]{1,0:T(8,128)} %get-tuple-element.38.params), custom_call_target="tpu_custom_call" | custom-call | tf_op jit(solution)/shard_map/inside/pallas_call | solution.py:490
  94.3 0.9 collective-permute-done.8
  95.2 1.4 %collective-permute-done.9 = bf16[144,512]{1,0:T(8,128)(2,1)} collective-permute-done((bf16[144,512]{1,0:T(8,128)(2,1)}, bf16[144,512]{1,0:T(8,128)(2,1)}, u32[]{:S(2)}, u32[]{:S(2)}) %collective-permute-start.9) | collective-permute-done | bytes 147488 | tf_op jit(solution)/shard_map/ppermute | solution.py:21
  96.6 1.1 select_convert_fusion.2
  97.7 0.8 add_select_fusion.prior
  98.6 2.9 %gate.1 = bf16[256,512]{1,0:T(8,128)(2,1)} custom-call(bf16[256,512]{1,0:T(8,128)(2,1)} %bitcast.49, f32[256,512]{1,0:T(8,128)} %inside.1.local, bf16[256,256]{1,0:T(8,128)(2,1)} %get-tuple-element.36.maps, f32[24,256]{1,0:T(8,128)} %get-tuple-element.37.meta, f32[128,512]{1,0:T(8,128)} %add_select_fusion.prior, f32[8,512]{1,0:T(8,128)} %get-tuple-element.38.params), custom_call_target="tpu_custom_call" | custom-call | tf_op jit(solution)/shard_map/gate/pallas_call | solution.py:517
  101.5 1.6 %collective-permute-start.10 = (bf16[256,512]{1,0:T(8,128)(2,1)}, bf16[256,512]{1,0:T(8,128)(2,1)S(1)}, u32[]{:S(2)}, u32[]{:S(2)}) collective-permute-start(bf16[256,512]{1,0:T(8,128)(2,1)} %gate.1), channel_id=1, source_target_pairs={{0,0},{1,1},{2,6},{3,7},{4,4},{5,5},{6,2},{7,3},{8,8},{9,9},{10,14... | collective-permute-start | bytes 786440 | tf_op jit(solution)/shard_map/ppermute | solution.py:592
  103.1 1.3 %collective-permute-start.12 = (bf16[256,512]{1,0:T(8,128)(2,1)}, bf16[256,512]{1,0:T(8,128)(2,1)S(1)}, u32[]{:S(2)}, u32[]{:S(2)}) collective-permute-start(bf16[256,512]{1,0:T(8,128)(2,1)} %gate.1), channel_id=1, source_target_pairs={{0,1},{1,0},{2,7},{3,6},{4,5},{5,4},{6,3},{7,2},{8,9},{9,8},{10,15... | collective-permute-start | bytes 786440 | tf_op jit(solution)/shard_map/ppermute | solution.py:592
  104.4 8.3 %collective-permute-done.11 = bf16[256,512]{1,0:T(8,128)(2,1)S(1)} collective-permute-done((bf16[256,512]{1,0:T(8,128)(2,1)}, bf16[256,512]{1,0:T(8,128)(2,1)S(1)}, u32[]{:S(2)}, u32[]{:S(2)}) %collective-permute-start.11) | collective-permute-done | bytes 262176 | tf_op jit(solution)/shard_map/ppermute | solution.py:592
  113.9 1.2 copy-done
  117.1 1.9 %collective-permute-done.13 = bf16[256,512]{1,0:T(8,128)(2,1)S(1)} collective-permute-done((bf16[256,512]{1,0:T(8,128)(2,1)S(1)}, bf16[256,512]{1,0:T(8,128)(2,1)S(1)}, u32[]{:S(2)}, u32[]{:S(2)}) %collective-permute-start.13) | collective-permute-done | bytes 262176 | tf_op jit(solution)/shard_map/ppermute | solution.py:21
  119.1 1.8 %fusion.3 = bf16[1,512,2048]{2,1,0:T(8,128)(2,1)} fusion(bf16[1,512,2048]{2,1,0:T(8,128)(2,1)} %copy-done.4, s32[]{:T(128)S(6)} %select_n.173, f32[256,2048]{1,0:T(8,128)S(1)} %fusion.15, bf16[256,512]{1,0:T(8,128)(2,1)S(1)} %collective-permute-done.13, bf16[512,2048]{1,0:T(8,128)(2,1)S(1)} %get-tuple-element.41, bf16[256,2048]{1,0:T(8,128)(2,1)S(1)} %get-tuple-element.42), kind=kOutput, calls=%fused_computation.5 | convolution fusion | flops 538968064 | bytes 6553604 | tf_op jit(solution)/shard_map/dot_general | solution.py:601
  (52 shorter events, 7.6 us)
Async XLA Ops:
  6.5 55.1 %reduce-scatter.5.cloned.1.call-start = ((), (), s32[]{:S(2)}) async-start(), calls=%async_computation.3 | async-start | bytes 1392640 | tf_op jit(solution)/shard_map/reduce_scatter | solution.py:544
  6.5 5.4 %collective-permute-start.1 = (bf16[512,2048]{1,0:T(8,128)(2,1)}, bf16[512,2048]{1,0:T(8,128)(2,1)S(1)}, u32[]{:S(2)}, u32[]{:S(2)}) collective-permute-start(bf16[512,2048]{1,0:T(8,128)(2,1)} %bitcast.43), channel_id=1, source_target_pairs={{0,4},{4,0},{1,5},{5,1},{2,6},{6,2},{3,7},{7,3},{8,12},{12,8},{9,1... | collective-permute-start | bytes 6291464 | tf_op jit(solution)/shard_map/ppermute | solution.py:21
  7.0 4.9 %collective-permute-start = (bf16[256,1280]{1,0:T(8,128)(2,1)}, bf16[256,1280]{1,0:T(8,128)(2,1)S(1)}, u32[]{:S(2)}, u32[]{:S(2)}) collective-permute-start(bf16[256,1280]{1,0:T(8,128)(2,1)} %bitcast.45), channel_id=1, source_target_pairs={{0,4},{4,0},{1,5},{5,1},{2,6},{6,2},{3,7},{7,3},{8,12},{12,8},{9,1... | collective-permute-start | bytes 1966088 | tf_op jit(solution)/shard_map/ppermute | solution.py:21
  11.9 0.9 copy-start.5
  11.9 1.5 %copy-start.3 = (bf16[512,2048]{1,0:T(8,128)(2,1)}, bf16[512,2048]{1,0:T(8,128)(2,1)S(1)}, u32[]{:S(2)}) copy-start(bf16[512,2048]{1,0:T(8,128)(2,1)S(1)} %collective-permute-done.1.text_other) | copy-start | bytes 6291460
  25.9 15.0 %copy-start.1 = (bf16[1,512,2048]{2,1,0:T(8,128)(2,1)S(1)}, bf16[1,512,2048]{2,1,0:T(8,128)(2,1)}, u32[]{:S(2)}) copy-start(bf16[1,512,2048]{2,1,0:T(8,128)(2,1)} %param.17) | copy-start | bytes 6291460
  25.9 15.0 %copy-start.9 = (bf16[2048]{0:T(1024)(128)(2,1)S(1)}, bf16[2048]{0:T(1024)(128)(2,1)}, u32[]{:S(2)}) copy-start(bf16[2048]{0:T(1024)(128)(2,1)} %newline.1) | copy-start | bytes 12292
  25.9 29.9 %collective-permute-start.2 = (bf16[512,2048]{1,0:T(8,128)(2,1)}, bf16[512,2048]{1,0:T(8,128)(2,1)}, u32[]{:S(2)}, u32[]{:S(2)}) collective-permute-start(bf16[512,2048]{1,0:T(8,128)(2,1)} %param.33), channel_id=1, source_target_pairs={{0,4},{4,0},{1,5},{5,1},{2,6},{6,2},{3,7},{7,3},{8,12},{12,8},{9,1... | collective-permute-start | bytes 6291464 | tf_op jit(solution)/shard_map/ppermute | solution.py:21
  26.4 72.2 %reduce-scatter.3.cloned.1.call-start = ((), (), s32[]{:S(2)}) async-start(), calls=%async_computation.2 | async-start | bytes 1310720 | tf_op jit(solution)/shard_map/reduce_scatter | solution.py:559
  26.4 10.4 %collective-permute-start.3 = (bf16[2,256,256]{2,1,0:T(8,128)(2,1)}, bf16[2,256,256]{2,1,0:T(8,128)(2,1)S(1)}, u32[]{:S(2)}, u32[]{:S(2)}) collective-permute-start(bf16[2,256,256]{2,1,0:T(8,128)(2,1)} %get-tuple-element.34), channel_id=1, source_target_pairs={{0,1},{1,0},{2,3},{3,2},{4,5},{5,4},{6,7},{7,6},{8,9},{9,8},{10,11... | collective-permute-start | bytes 786440 | tf_op jit(solution)/shard_map/ppermute | solution.py:21
  37.9 17.9 %copy-start.6 = (bf16[1,256,256]{2,1,0:T(8,128)(2,1)}, bf16[1,256,256]{2,1,0:T(8,128)(2,1)S(1)}, u32[]{:S(2)}) copy-start(bf16[1,256,256]{2,1,0:T(8,128)(2,1)S(1)} %get-tuple-element.53) | copy-start | bytes 393220
  37.9 17.9 %collective-permute-start.4 = (bf16[256,256]{1,0:T(8,128)(2,1)S(1)}, bf16[256,256]{1,0:T(8,128)(2,1)S(1)}, u32[]{:S(2)}, u32[]{:S(2)}) collective-permute-start(bf16[256,256]{1,0:T(8,128)(2,1)S(1)} %get-tuple-element.52), channel_id=1, source_target_pairs={{0,2},{1,3},{2,0},{3,1},{4,6},{5,7},{6,4},{7,5},{8,10},{9,11},{10,... | collective-permute-start | bytes 393224 | tf_op jit(solution)/shard_map/ppermute | solution.py:21
  55.8 3.9 %copy-start.7 = (bf16[256,256]{1,0:T(8,128)(2,1)}, bf16[256,256]{1,0:T(8,128)(2,1)S(1)}, u32[]{:S(2)}) copy-start(bf16[256,256]{1,0:T(8,128)(2,1)S(1)} %collective-permute-done.4.refs_2_) | copy-start | bytes 393220
  62.3 4.7 %collective-permute-start.5 = (bf16[16,768]{1,0:T(8,128)(2,1)S(1)}, bf16[16,768]{1,0:T(8,128)(2,1)S(1)}, u32[]{:S(2)}, u32[]{:S(2)}) collective-permute-start(bf16[16,768]{1,0:T(8,128)(2,1)S(1)} %fusion.12), channel_id=1, source_target_pairs={{0,1},{2,3},{8,9},{10,11},{16,17},{18,19},{24,25},{26,27},{1,8},{3... | collective-permute-start | bytes 73736 | tf_op jit(solution)/shard_map/ppermute | solution.py:564
  67.1 0.6 copy-start.8
  71.1 13.4 %collective-permute-start.6 = (bf16[144,512]{1,0:T(8,128)(2,1)}, bf16[144,512]{1,0:T(8,128)(2,1)S(1)}, u32[]{:S(2)}, u32[]{:S(2)}) collective-permute-start(bf16[144,512]{1,0:T(8,128)(2,1)} %get-tuple-element.39), channel_id=1, source_target_pairs={{0,1},{1,0},{2,3},{3,2},{4,5},{5,4},{6,7},{7,6},{8,9},{9,8},{10,11... | collective-permute-start | bytes 442376 | tf_op jit(solution)/shard_map/ppermute | solution.py:21
  86.2 8.1 %collective-permute-start.7 = (bf16[144,512]{1,0:T(8,128)(2,1)}, bf16[144,512]{1,0:T(8,128)(2,1)}, u32[]{:S(2)}, u32[]{:S(2)}) collective-permute-start(bf16[144,512]{1,0:T(8,128)(2,1)} %pad_maximum_fusion), channel_id=1, source_target_pairs={{0,24},{8,16},{16,8},{24,0},{1,25},{9,17},{17,9},{25,1},{2,26},{10... | collective-permute-start | bytes 442376 | tf_op jit(solution)/shard_map/ppermute | solution.py:21
  89.7 5.5 %collective-permute-start.8 = (bf16[144,512]{1,0:T(8,128)(2,1)}, bf16[144,512]{1,0:T(8,128)(2,1)}, u32[]{:S(2)}, u32[]{:S(2)}) collective-permute-start(bf16[144,512]{1,0:T(8,128)(2,1)} %pad_maximum_fusion), channel_id=1, source_target_pairs={{0,16},{8,24},{16,0},{24,8},{1,17},{9,25},{17,1},{25,9},{2,18},{10... | collective-permute-start | bytes 442376 | tf_op jit(solution)/shard_map/ppermute | solution.py:21
  90.3 6.3 %collective-permute-start.9 = (bf16[144,512]{1,0:T(8,128)(2,1)}, bf16[144,512]{1,0:T(8,128)(2,1)}, u32[]{:S(2)}, u32[]{:S(2)}) collective-permute-start(bf16[144,512]{1,0:T(8,128)(2,1)} %pad_maximum_fusion), channel_id=1, source_target_pairs={{0,8},{8,0},{16,24},{24,16},{1,9},{9,1},{17,25},{25,17},{2,10},{10... | collective-permute-start | bytes 442376 | tf_op jit(solution)/shard_map/ppermute | solution.py:21
  101.5 11.2 %collective-permute-start.11 = (bf16[256,512]{1,0:T(8,128)(2,1)}, bf16[256,512]{1,0:T(8,128)(2,1)S(1)}, u32[]{:S(2)}, u32[]{:S(2)}) collective-permute-start(bf16[256,512]{1,0:T(8,128)(2,1)} %gate.1), channel_id=1, source_target_pairs={{0,2},{1,3},{2,4},{3,5},{4,6},{5,7},{6,0},{7,1},{8,10},{9,11},{10,... | collective-permute-start | bytes 786440 | tf_op jit(solution)/shard_map/ppermute | solution.py:592
  101.5 12.0 %collective-permute-start.10 = (bf16[256,512]{1,0:T(8,128)(2,1)}, bf16[256,512]{1,0:T(8,128)(2,1)S(1)}, u32[]{:S(2)}, u32[]{:S(2)}) collective-permute-start(bf16[256,512]{1,0:T(8,128)(2,1)} %gate.1), channel_id=1, source_target_pairs={{0,0},{1,1},{2,6},{3,7},{4,4},{5,5},{6,2},{7,3},{8,8},{9,9},{10,14... | collective-permute-start | bytes 786440 | tf_op jit(solution)/shard_map/ppermute | solution.py:592
  103.1 12.8 %collective-permute-start.12 = (bf16[256,512]{1,0:T(8,128)(2,1)}, bf16[256,512]{1,0:T(8,128)(2,1)S(1)}, u32[]{:S(2)}, u32[]{:S(2)}) collective-permute-start(bf16[256,512]{1,0:T(8,128)(2,1)} %gate.1), channel_id=1, source_target_pairs={{0,1},{1,0},{2,7},{3,6},{4,5},{5,4},{6,3},{7,2},{8,9},{9,8},{10,15... | collective-permute-start | bytes 786440 | tf_op jit(solution)/shard_map/ppermute | solution.py:592
  112.7 6.4 %collective-permute-start.13 = (bf16[256,512]{1,0:T(8,128)(2,1)S(1)}, bf16[256,512]{1,0:T(8,128)(2,1)S(1)}, u32[]{:S(2)}, u32[]{:S(2)}) collective-permute-start(bf16[256,512]{1,0:T(8,128)(2,1)S(1)} %collective-permute-done.11), channel_id=1, source_target_pairs={{0,1},{1,0},{2,3},{3,2},{4,5},{5,4},{6,7},{7,6},{8,9},{9,8},{10,11... | collective-permute-start | bytes 786440 | tf_op jit(solution)/shard_map/ppermute | solution.py:21
  112.7 1.2 copy-start.2
  113.4 1.7 %copy-start = (bf16[512,2048]{1,0:T(8,128)(2,1)S(1)}, bf16[512,2048]{1,0:T(8,128)(2,1)}, u32[]{:S(2)}) copy-start(bf16[512,2048]{1,0:T(8,128)(2,1)} %get-tuple-element.40) | copy-start | bytes 6291460
  115.8 1.3 %copy-start.4 = (bf16[1,512,2048]{2,1,0:T(8,128)(2,1)}, bf16[1,512,2048]{2,1,0:T(8,128)(2,1)S(1)}, u32[]{:S(2)}) copy-start(bf16[1,512,2048]{2,1,0:T(8,128)(2,1)S(1)} %fusion.5) | copy-start | bytes 6291460
Sparse Core Ops, SparseCore 0:
  26.5 35.0 reduce-scatter.4
  64.0 29.2 reduce-scatter.2

commit v5 on v4

--- a/solution.py
+++ b/solution.py
@@ -206,7 +206,7 @@
 def enter_body(
     table, dt_bias, a_log, skip, feats_mine, feats_other, vision_gain, proj, text, text_other,
     newline, gain, xz, bc, dt, conv_x, out_gain,
-    crops_out, rows_out, first_out, keep_out, send_out,
+    crops_out, rows_out, keep_x_out, send_x_out, keep_out, send_out,
     feats, normed, proj_tiles, tails, weights, crops, rows, first, maps, sems, out_sems,
 ):
     half = tails.shape[1]
@@ -297,17 +297,19 @@
         own.append(jnp.where(lane < 96, pieces, 0.0))
     own = jnp.concatenate(own, 0)
     slots = jnp.concatenate([jnp.where(chip == slot, own, 0.0) for slot in range(4)], 1)
-    for part in range(4):
-        main = rows[part * half : (part + 1) * half, :]
-        maps[part] = jnp.dot(main, weights[2], preferred_element_type=F32).astype(BF16)
-        goes = pltpu.make_async_copy(maps.at[part], send_out.at[part // 2], out_sems.at[6 + part])
-        remains = pltpu.make_async_copy(
-            maps.at[part], keep_out.at[part // 2], out_sems.at[6 + part]
-        )
+
+    def parted(source, keep, send, part, sem):
+        goes = pltpu.make_async_copy(source.at[part], send.at[part // 2], sem)
+        remains = pltpu.make_async_copy(source.at[part], keep.at[part // 2], sem)
         here = chip % 2 == part % 2
         pl.when(here)(remains.start)
         pl.when(jnp.logical_not(here))(goes.start)
         departures.append(goes)
+
+    for part in range(4):
+        main = rows[part * half : (part + 1) * half, :]
+        maps[part] = jnp.dot(main, weights[2], preferred_element_type=F32).astype(BF16)
+        parted(maps, keep_out, send_out, part, out_sems.at[6 + part])
     for part in range(4):
         main = rows[part * half : (part + 1) * half, :]
         for i in range(2):
@@ -319,10 +321,7 @@
         sums = jnp.concatenate([steps[0:4], sums[0:4]], 0)
         sums = jnp.concatenate([sums, jnp.zeros((8, 512 - half), F32)], 1)
         first[part, half : half + 16, :] = jnp.concatenate([sums, slots], 0).astype(BF16)
-        departures.append(
-            pltpu.make_async_copy(first.at[part], first_out.at[part], out_sems.at[2 + part])
-        )
-        departures[-1].start()
+        parted(first, keep_x_out, send_x_out, part, out_sems.at[2 + part])
     for copy in departures:
         copy.wait()
 
@@ -341,11 +340,12 @@
         in_specs=[pl.BlockSpec(memory_space=pltpu.SMEM)] * 4
         + [whole, whole, near, whole, whole, whole]
         + [near, near, whole, whole, near, near, near],
-        out_specs=[whole] * 5,
+        out_specs=[whole] * 6,
         out_shape=[
             jax.ShapeDtypeStruct((2 * half, columns), BF16),
             jax.ShapeDtypeStruct((4 * half, columns), BF16),
-            jax.ShapeDtypeStruct((4, half + 16, 512), BF16),
+            jax.ShapeDtypeStruct((2, half + 16, 512), BF16),
+            jax.ShapeDtypeStruct((2, half + 16, 512), BF16),
             jax.ShapeDtypeStruct((2, half, 256), BF16),
             jax.ShapeDtypeStruct((2, half, 256), BF16),
         ],
@@ -369,28 +369,60 @@
     )
 
 
-def gates_body(rows, weight, out):
-    for head in range(4):
-        out[0, :, 128 * head : 128 * head + 128] = jnp.dot(
-            rows[...],
-            weight[:, 256 * head + 128 : 256 * head + 256],
-            preferred_element_type=F32,
-        ).astype(BF16)
-
-
-def gates(rows, weight):
+def gates_body(rows_hbm, xz, keep_out, send_out, rows, weights, results, sems, out_sems):
+    half = results.shape[1]
+    chip = lax.axis_index("tensor")
+    load_weights = [
+        pltpu.make_async_copy(
+            xz.at[:, pl.ds(i * 256 + 128, 128)],
+            weights.at[i // 2, :, pl.ds(i % 2 * 128, 128)],
+            sems.at[4 + i],
+        )
+        for i in range(4)
+    ]
+    load_rows = [
+        pltpu.make_async_copy(rows_hbm.at[pl.ds(part * half, half), :], rows.at[part], sems.at[part])
+        for part in range(4)
+    ]
+    for copy in load_rows[:1] + load_weights + load_rows[1:]:
+        copy.start()
+    departures = []
+    for part in range(4):
+        load_rows[part].wait()
+        for i in range(2):
+            if part == 0:
+                load_weights[2 * i].wait()
+                load_weights[2 * i + 1].wait()
+            results[part, :, 256 * i : 256 * i + 256] = jnp.dot(
+                rows[part], weights[i], preferred_element_type=F32
+            ).astype(BF16)
+        goes = pltpu.make_async_copy(results.at[part], send_out.at[part // 2], out_sems.at[part])
+        remains = pltpu.make_async_copy(results.at[part], keep_out.at[part // 2], out_sems.at[part])
+        here = chip % 2 == part % 2
+        pl.when(here)(remains.start)
+        pl.when(jnp.logical_not(here))(goes.start)
+        departures.append(goes)
+    for copy in departures:
+        copy.wait()
+
+
+def gates(rows, xz):
     half, columns = rows.shape[0] // 4, rows.shape[1]
+    whole = pl.BlockSpec(memory_space=pl.ANY)
     return pl.pallas_call(
         gates_body,
-        grid=(4,),
-        in_specs=[
-            pl.BlockSpec((half, columns), lambda i: (i, 0)),
-            pl.BlockSpec(weight.shape, lambda i: (0, 0)),
+        in_specs=[whole, whole],
+        out_specs=[whole, whole],
+        out_shape=[jax.ShapeDtypeStruct((2, half, 512), BF16)] * 2,
+        scratch_shapes=[
+            pltpu.VMEM((4, half, columns), BF16),
+            pltpu.VMEM((2, columns, 256), BF16),
+            pltpu.VMEM((4, half, 512), BF16),
+            pltpu.SemaphoreType.DMA((8,)),
+            pltpu.SemaphoreType.DMA((4,)),
         ],
-        out_specs=pl.BlockSpec((1, half, 512), lambda i: (i, 0, 0)),
-        out_shape=jax.ShapeDtypeStruct((4, half, 512), BF16),
         name="gates",
-    )(rows, weight)
+    )(rows, xz)
 
 
 def filtered(main, edge, taps):
@@ -404,12 +436,13 @@
 
 
 def scan_body(
-    width, first, kept, received, before, taps_maps, streams, maps, meta, state, params
+    width, kept_x, received_x, kept, received, before, taps_maps, streams, maps, meta, state, params
 ):
+    first = kept_x[...].astype(F32) + received_x[...].astype(F32)
     half = first.shape[0] - 16
-    slots = first[half : half + 16, :].astype(F32)[8:16]
+    slots = first[half + 8 : half + 16]
     params[...] = slots
-    sums = first[half : half + 16, 0:half].astype(F32)[0:8]
+    sums = first[half : half + 8, 0:half]
     scale = lax.rsqrt(sums[4:5] / width + EPS)
     sums_before = before[8:16, half - 128 : half].astype(F32)
     scale_before = lax.rsqrt(sums_before[4:5] / width + EPS)
@@ -432,7 +465,7 @@
     scale_edge = columns_of(jnp.broadcast_to(scale_before, (8, 128)))[120:128, 0:1]
     taps_x = slots[0:4]
     edge = before[0:8, :].astype(F32) * scale_edge
-    x = silu(filtered(first[0:half, :].astype(F32) * scale_main, edge[:, 0:512], taps_x))
+    x = silu(filtered(first[0:half] * scale_main, edge[:, 0:512], taps_x))
     both = silu(
         filtered(
             (kept[...].astype(F32) + received[...].astype(F32)) * scale_main,
@@ -451,8 +484,8 @@
     meta[16:24, :] = jnp.broadcast_to(scale, (8, half))
 
 
-def scan(width, first, kept, received, before, taps_maps):
-    half = kept.shape[0]
+def scan(width, *operands):
+    half = operands[2].shape[0]
     return pl.pallas_call(
         lambda *refs: scan_body(width, *refs),
         out_shape=[
@@ -463,7 +496,21 @@
             jax.ShapeDtypeStruct((8, 512), F32),
         ],
         name="scan",
-    )(first, kept, received, before, taps_maps)
+    )(*operands)
+
+
+def join_body(state, partner, out):
+    late = lax.axis_index("tensor") % 2 == 1
+    mine, other = state[...].astype(F32), partner[...].astype(F32)
+    first, second = jnp.where(late, other, mine), jnp.where(late, mine, other)
+    out[0:128, :] = (second[128:129] * first[0:128] + second[0:128]).astype(BF16)
+    out[128:144, :] = (first[128:144] * second[128:144]).astype(BF16)
+
+
+def join(state, partner):
+    return pl.pallas_call(
+        join_body, out_shape=jax.ShapeDtypeStruct(state.shape, BF16), name="join"
+    )(state, partner)
 
 
 def inside_body(streams, maps, meta, params, out):
@@ -494,17 +541,31 @@
     )(streams, maps, meta, params)
 
 
-def gate_body(second, local, maps, meta, prior, params, out):
+def gate_body(kept, received, local, maps, meta, params, partner, *others_and_out):
+    *others, out = others_and_out
     half = local.shape[0]
+    section = lax.axis_index("segment")
+    late = lax.axis_index("tensor") % 2 == 1
+    prior = jnp.zeros((128, 512), F32)
+    for source in range(len(others)):
+        bits = jnp.bitwise_xor(section, source)
+        piece = others[0][...]
+        for index in range(1, len(others)):
+            piece = jnp.where(bits == index + 1, others[index][...], piece)
+        piece = piece.astype(F32)
+        prior = jnp.where(source < section, piece[128:129] * prior + piece[0:128], prior)
+    before = partner[...].astype(F32)
+    prior = jnp.where(late, before[128:129] * prior + before[0:128], prior)
     scale = columns_of(meta[16:24, :])[:, 0:1]
     entry = jnp.exp(columns_of(meta[0:8, :]))
-    across = jnp.dot(maps[:, 128:256], prior[...].astype(BF16), preferred_element_type=F32)
+    across = jnp.dot(maps[:, 128:256], prior.astype(BF16), preferred_element_type=F32)
     gated = []
     squares = jnp.zeros((half, 1), F32)
     for head in range(4):
         cols = slice(128 * head, 128 * head + 128)
         y = local[:, cols] + entry[:, head : head + 1] * across[:, cols]
-        value = y * silu(second[:, cols].astype(F32) * scale)
+        gates = kept[:, cols].astype(F32) + received[:, cols].astype(F32)
+        value = y * silu(gates * scale)
         squares = squares + jnp.sum(value * value, -1, keepdims=True)
         gated.append(value)
     norm = lax.rsqrt(squares / 512 + EPS)
@@ -513,12 +574,10 @@
         out[:, cols] = (gated[head] * norm * params[4:5, cols]).astype(BF16)
 
 
-def gate(second, local, maps, meta, prior, params):
+def gate(local, *operands):
     return pl.pallas_call(
-        gate_body,
-        out_shape=jax.ShapeDtypeStruct(local.shape, BF16),
-        name="gate",
-    )(second, local, maps, meta, prior, params)
+        gate_body, out_shape=jax.ShapeDtypeStruct(local.shape, BF16), name="gate"
+    )(*operands[:2], local, *operands[2:])
 
 
 def per_device_halves(
@@ -526,7 +585,6 @@
     dt_weight, bc_weight, conv_x, conv_bc, dt_bias, a_log, skip, out_gain, out_weight,
 ):
     my_chip = lax.axis_index("tensor")
-    my_segment = lax.axis_index("segment")
     segment_count = lax.axis_size("segment")
     text = text_embed[0]
     section, columns = text.shape
@@ -535,18 +593,31 @@
     feats = crop_feats[0, 0, 0]
     feats_other = swapped(feats, "dp", 1)
     text_other = swapped(text, "dp", 1)
-    crops, rows, first, keep, send = enter(
+    crops, rows, keep_x, send_x, keep, send = enter(
         crop_dest.transpose(0, 2, 1), dt_bias, a_log, skip, feats, feats_other, vision_gain,
         proj_weight, text, text_other, newline, norm_gain, xz_weight, bc_weight, dt_weight.T,
         conv_x, out_gain,
     )
-    out_weight, newline, rows, first = lax.optimization_barrier((out_weight, newline, rows, first))
-    first = lax.psum_scatter(first, "tensor", scatter_dimension=0, tiled=False)
-    pair = keep.astype(F32) + swapped(send, "tensor", 1).astype(F32)
+    out_weight, newline, rows = lax.optimization_barrier((out_weight, newline, rows))
     lower = my_chip < 2
-    received = swapped(jnp.where(lower, pair[1], pair[0]).astype(BF16), "tensor", 2)
-    kept = jnp.where(lower, pair[0], pair[1]).astype(BF16)
-    second = gates(rows, xz_weight)
+
+    def added(keep, arrived):
+        pair = keep.astype(F32) + arrived.astype(F32)
+        leaves = jnp.where(lower, pair[1], pair[0]).astype(BF16)
+        return leaves, jnp.where(lower, pair[0], pair[1]).astype(BF16)
+
+    keep_gates, send_gates = gates(rows, xz_weight)
+    leaves, kept = added(keep, swapped(send, "tensor", 1))
+    leaves, kept, send_x, send_gates, out_weight = lax.optimization_barrier(
+        (leaves, kept, send_x, send_gates, out_weight)
+    )
+    received = swapped(leaves, "tensor", 2)
+    leaves_x, kept_x = added(keep_x, swapped(send_x, "tensor", 1))
+    leaves_x, kept_x, send_gates, received = lax.optimization_barrier(
+        (leaves_x, kept_x, send_gates, received)
+    )
+    received_x = swapped(leaves_x, "tensor", 2)
+    arrived_gates = swapped(send_gates, "tensor", 1)
     weight_other = swapped(out_weight, "dp", 1)
     weights = (
         jnp.where(lower, out_weight, weight_other), jnp.where(lower, weight_other, out_weight)
@@ -555,39 +626,28 @@
     head = crops[:half]
     tail = jnp.where(jnp.arange(half)[:, None] == 0, newline[None], text[half:])
     hidden = (jnp.where(late, tail, head), jnp.where(late, head, tail))
-    second, weights, hidden = lax.optimization_barrier((second, weights, hidden))
-    second = lax.psum_scatter(second, "tensor", scatter_dimension=0, tiled=False)
+    kept_x, received_x, weights, hidden = lax.optimization_barrier(
+        (kept_x, received_x, weights, hidden)
+    )
     route = [(i, i + 1) for i in range(0, 4 * segment_count, 2)]
     route += [(i, i + 3) for i in range(1, 4 * segment_count - 4, 2)]
     ends = (kept[half - 8 :].astype(F32) + received[half - 8 :].astype(F32)).astype(BF16)
-    before = jnp.concatenate([first[half - 8 : half + 8], jnp.pad(ends, ((0, 8), (0, 0)))], 1)
+    before = slice(half - 8, half + 8)
+    before = (kept_x[before].astype(F32) + received_x[before].astype(F32)).astype(BF16)
+    before = jnp.concatenate([before, jnp.pad(ends, ((0, 8), (0, 0)))], 1)
     before = lax.ppermute(before, ("segment", "tensor"), route)
-    streams, maps, meta, state, params = scan(width, first, kept, received, before, conv_bc)
+    streams, maps, meta, state, params = scan(
+        width, kept_x, received_x, kept, received, before, conv_bc
+    )
+    meta, keep_gates = lax.optimization_barrier((meta, keep_gates))
     local = inside(streams, maps, meta, params)
-    partner = swapped(state, "tensor", 1).astype(F32)
-    state = state.astype(F32)
-    early_state = jnp.where(late, partner, state)[:128]
-    late_state = jnp.where(late, state, partner)[:128]
-    early_decay = jnp.where(late, partner, state)[128:129]
-    late_decay = jnp.where(late, state, partner)[128:129]
-    whole = jnp.concatenate(
-        [
-            late_decay * early_state + late_state,
-            jnp.broadcast_to(early_decay * late_decay, (16, 512)),
-        ],
-        0,
-    ).astype(BF16)
-    others = [None] + [swapped(whole, "segment", bits) for bits in range(1, segment_count)]
-    prior = jnp.zeros((128, 512), F32)
-    for source in range(segment_count - 1):
-        bits = my_segment ^ source
-        piece = others[1]
-        for index in range(2, segment_count):
-            piece = jnp.where(bits == index, others[index], piece)
-        piece = piece.astype(F32)
-        prior = jnp.where(source < my_segment, piece[128:129] * prior + piece[:128], prior)
-    prior = jnp.where(late, early_decay * prior + early_state, prior)
-    normed = gate(second, local, maps, meta, prior, params)
+    partner = swapped(state, "tensor", 1)
+    whole = join(state, partner)
+    whole, local = lax.optimization_barrier((whole, local))
+    others = [swapped(whole, "segment", bits) for bits in range(1, segment_count)]
+    leaves, kept = added(keep_gates, arrived_gates)
+    received = swapped(leaves, "tensor", 2)
+    normed = gate(local, kept, received, maps, meta, params, partner, *others)
     near, far, here = (
         lax.ppermute(
             normed, ("dp", "tensor"), [(i, (i if i % 4 < 2 else i ^ 4) ^ bits) for i in range(8)]

time: 128 us -> 120 us (0.938)
  between operations: 15.5 us -> 2.16 us
  starting transfers between devices: 20.8 us -> 26.8 us
  waiting for transfers between devices: 41.1 us -> 43.1 us
  other arithmetic: 11 us -> 9.12 us
    ppermute x10 -> x14, starting transfers between devices: 14.5 us -> 21.1 us  [swapped(): lax.ppermute(block, axis, [(i, i ^ bits) for i in range(lax.axis_size(axi...]
    reduce_scatter x2 -> x0, waiting for transfers between devices: 1.88 us -> none  [the longest x1 1.88 us: per_device_halves(): first = lax.psum_scatter(first, 'tensor', scatter_dimension=0, tiled=False)]
    select_n x2 -> x0, other arithmetic: 1.79 us -> none  [the longest x1 0.95 us: per_device_halves(): early_decay = jnp.where(late, partner, state)[128:129]]
    ppermute x10 -> x14, waiting for transfers between devices: 29.6 us -> 31.3 us  [swapped(): lax.ppermute(block, axis, [(i, i ^ bits) for i in range(lax.axis_size(axi...]
    add x1 -> x3, other arithmetic: 1.01 us -> 2.6 us  [added(): pair = keep.astype(F32) + arrived.astype(F32)]
    ppermute x1, starting transfers between devices: 3.42 us -> 1.96 us  [per_device_halves(): before = lax.ppermute(before, ('segment', 'tensor'), route)]
    ppermute x3, waiting for transfers between devices: 8.32 us -> 9.63 us  [per_device_halves(): lax.ppermute(normed, ('dp', 'tensor'), [(i, (i if i % 4 < 2 else i ^ 4) ^...]
    pallas_call x1 -> x2, Pallas kernels: 8.56 us -> 7.69 us  [the longest x1 5.98 us: gates(): pl.pallas_call(gates_body, in_specs=[whole, whole], out_specs=[whole, who...]
  transfers between devices with their start and end apart: 16 -> 18, of which waited for: 10 -> 11; matrix products, arithmetic and copies ran while one was open for 11% -> 10% of each run, Pallas kernels for 12% -> 12%
where the time goes in v5:
time: 120 us
  waiting for transfers between devices  43.1 us (36%)
  Pallas kernels  29.6 us (25%)
  starting transfers between devices  26.8 us (22%)
  other arithmetic  9.12 us (8%)
  local copies, waits for them, and re-layouts  5.07 us (4%)
  matrix products  3.94 us (3%)
  between operations  2.16 us (2%)
    ppermute x14, waiting for transfers between devices, swapped(): lax.ppermute(block, axis, [(i, i ^ bits) for i in range(lax.axis_size(axi...  31.3 us
    ppermute x14, starting transfers between devices, swapped(): lax.ppermute(block, axis, [(i, i ^ bits) for i in range(lax.axis_size(axi...  21.1 us
    pallas_call x1, Pallas kernels, enter(): pl.pallas_call(enter_body, in_specs=[pl.BlockSpec(memory_space=pltpu.SMEM...  12.4 us
    ppermute x3, waiting for transfers between devices, per_device_halves(): lax.ppermute(normed, ('dp', 'tensor'), [(i, (i if i % 4 < 2 else i ^ 4) ^...  9.63 us
    pallas_call x1, Pallas kernels, gates(): pl.pallas_call(gates_body, in_specs=[whole, whole], out_specs=[whole, who...  5.98 us
    unnamed x34, local copies, waits for them, and re-layouts  4.82 us
    ppermute x3, starting transfers between devices, per_device_halves(): lax.ppermute(normed, ('dp', 'tensor'), [(i, (i if i % 4 < 2 else i ^ 4) ^...  3.71 us
    pallas_call x1, Pallas kernels, scan(): pl.pallas_call(lambda *refs: scan_body(width, *refs), out_shape=[jax.Shap...  3.47 us
  transfers between devices with their start and end apart: 18, of which 11 were waited for; matrix products, arithmetic and copies ran while one was open for 10% of the time, Pallas kernels for 12%

profile of v5, /device:TPU:0, one launch (start us, length us, event | category | flops | bytes accessed | tf_op | source)
XLA Modules:
  0.0 119.7 jit_solution(7480636197978003549)
XLA Ops:
  2.5 2.9 %collective-permute-done.feats_other = bf16[256,1280]{1,0:T(8,128)(2,1)S(1)} collective-permute-done((bf16[256,1280]{1,0:T(8,128)(2,1)}, bf16[256,1280]{1,0:T(8,128)(2,1)S(1)}, u32[]{:S(2)}, u32[]{:S(2)}) %collective-permute-start) | collective-permute-done | bytes 655392 | tf_op jit(solution)/shard_map/ppermute | solution.py:21
  6.9 12.4 %enter.1 = (bf16[512,2048]{1,0:T(8,128)(2,1)}, bf16[1024,2048]{1,0:T(8,128)(2,1)}, bf16[2,272,512]{2,1,0:T(8,128)(2,1)}, bf16[2,272,512]{2,1,0:T(8,128)(2,1)}, b...) custom-call(s32[1,1,2]{2,1,0:T(1,128)} %bitcast.43, f32[1]{0:T(128)S(6)} %copy.20.dt_bias, f32[1]{0:T(128)S(6)} %copy.21.a_log, ...), custom_call_target="tpu_custom_call" | custom-call | tf_op jit(solution)/shard_map/enter/pallas_call | solution.py:338
  19.4 3.0 %collective-permute-start.2 = (bf16[2,256,256]{2,1,0:T(8,128)(2,1)}, bf16[2,256,256]{2,1,0:T(8,128)(2,1)S(1)}, u32[]{:S(2)}, u32[]{:S(2)}) collective-permute-start(bf16[2,256,256]{2,1,0:T(8,128)(2,1)} %get-tuple-element.42), channel_id=1, source_target_pairs={{0,1},{1,0},{2,3},{3,2},{4,5},{5,4},{6,7},{7,6},{8,9},{9,8},{10,11... | collective-permute-start | bytes 786440 | tf_op jit(solution)/shard_map/ppermute | solution.py:21
  22.4 6.0 %gates.1 = (bf16[2,256,512]{2,1,0:T(8,128)(2,1)}, bf16[2,256,512]{2,1,0:T(8,128)(2,1)}) custom-call(bf16[1024,2048]{1,0:T(8,128)(2,1)} %get-tuple-element.45.rows_hbm, bf16[2048,1024]{1,0:T(8,128)(2,1)} %xz.3), custom_call_target="tpu_custom_call" | custom-call | tf_op jit(solution)/shard_map/gates/pallas_call | solution.py:412
  29.4 1.8 %collective-permute-start.3 = (bf16[2,272,512]{2,1,0:T(8,128)(2,1)}, bf16[2,272,512]{2,1,0:T(8,128)(2,1)}, u32[]{:S(2)}, u32[]{:S(2)}) collective-permute-start(bf16[2,272,512]{2,1,0:T(8,128)(2,1)} %get-tuple-element.48), channel_id=1, source_target_pairs={{0,1},{1,0},{2,3},{3,2},{4,5},{5,4},{6,7},{7,6},{8,9},{9,8},{10,11... | collective-permute-start | bytes 1671176 | tf_op jit(solution)/shard_map/ppermute | solution.py:21
  31.2 2.5 %broadcast_select_fusion.2 = (bf16[256,2048]{1,0:T(8,128)(2,1)S(1)}, bf16[256,2048]{1,0:T(8,128)(2,1)}) fusion(pred[]{:T(512)S(6)} %eq.16, bf16[512,2048]{1,0:T(8,128)(2,1)} %get-tuple-element.55, bf16[1,512,2048]{2,1,0:T(8,128)(2,1)S(1)} %copy-done.1, bf16[2048]{0:T(1024)(128)(2,1)S(1)} %copy-done.16, pred[256]{0:T(512)(128)(4,1)S(1)} %iota_compare_fusion.1), kind=kLoop, calls=%fused_computation.14 | loop fusion | flops 1572864 | bytes 4198657 | tf_op jit(solution)/shard_map/jit(_where)/select_n | solution.py:628
  33.7 2.6 %collective-permute-start.4 = (bf16[256,256]{1,0:T(8,128)(2,1)S(1)}, bf16[256,256]{1,0:T(8,128)(2,1)S(1)}, u32[]{:S(2)}, u32[]{:S(2)}) collective-permute-start(bf16[256,256]{1,0:T(8,128)(2,1)S(1)} %get-tuple-element.50), channel_id=1, source_target_pairs={{0,2},{1,3},{2,0},{3,1},{4,6},{5,7},{6,4},{7,5},{8,10},{9,11},{10,... | collective-permute-start | bytes 393224 | tf_op jit(solution)/shard_map/ppermute | solution.py:21
  36.3 11.2 %collective-permute-done.3 = bf16[2,272,512]{2,1,0:T(8,128)(2,1)} collective-permute-done((bf16[2,272,512]{2,1,0:T(8,128)(2,1)}, bf16[2,272,512]{2,1,0:T(8,128)(2,1)}, u32[]{:S(2)}, u32[]{:S(2)}) %collective-permute-start.3) | collective-permute-done | bytes 557088 | tf_op jit(solution)/shard_map/ppermute | solution.py:21
  47.5 1.2 %convert_add_fusion = bf16[2,272,512]{2,1,0:T(8,128)(2,1)S(1)} fusion(bf16[2,272,512]{2,1,0:T(8,128)(2,1)} %collective-permute-done.3, bf16[2,272,512]{2,1,0:T(8,128)(2,1)S(1)} %copy-done.9), kind=kLoop, calls=%fused_computation.9 | loop fusion | flops 1114112 | bytes 1671168 | tf_op jit(solution)/shard_map/add | solution.py:605
  48.8 1.9 %collective-permute-start.5 = (bf16[272,512]{1,0:T(8,128)(2,1)S(1)}, bf16[272,512]{1,0:T(8,128)(2,1)S(1)}, u32[]{:S(2)}, u32[]{:S(2)}) collective-permute-start(bf16[272,512]{1,0:T(8,128)(2,1)S(1)} %get-tuple-element.52), channel_id=1, source_target_pairs={{0,2},{1,3},{2,0},{3,1},{4,6},{5,7},{6,4},{7,5},{8,10},{9,11},{10,... | collective-permute-start | bytes 835592 | tf_op jit(solution)/shard_map/ppermute | solution.py:21
  50.7 2.5 %collective-permute-start.8 = (bf16[2,256,512]{2,1,0:T(8,128)(2,1)}, bf16[2,256,512]{2,1,0:T(8,128)(2,1)}, u32[]{:S(2)}, u32[]{:S(2)}) collective-permute-start(bf16[2,256,512]{2,1,0:T(8,128)(2,1)} %get-tuple-element.64), channel_id=1, source_target_pairs={{0,1},{1,0},{2,3},{3,2},{4,5},{5,4},{6,7},{7,6},{8,9},{9,8},{10,11... | collective-permute-start | bytes 1572872 | tf_op jit(solution)/shard_map/ppermute | solution.py:21
  53.3 3.2 %broadcast_select_fusion = (bf16[512,2048]{1,0:T(8,128)(2,1)S(1)}, bf16[512,2048]{1,0:T(8,128)(2,1)}) fusion(bf16[512,2048]{1,0:T(8,128)(2,1)} %collective-permute-done.6, bf16[512,2048]{1,0:T(8,128)(2,1)S(1)} %copy-done.5, pred[]{:T(512)S(6)} %lt.11), kind=kLoop, calls=%fused_computation.7 | loop fusion | flops 2097152 | bytes 8388609 | tf_op jit(solution)/shard_map/jit(_where)/select_n | solution.py:623
  56.4 7.6 %collective-permute-done.5.refs_1_ = bf16[272,512]{1,0:T(8,128)(2,1)S(1)} collective-permute-done((bf16[272,512]{1,0:T(8,128)(2,1)S(1)}, bf16[272,512]{1,0:T(8,128)(2,1)S(1)}, u32[]{:S(2)}, u32[]{:S(2)}) %collective-permute-start.5) | collective-permute-done | bytes 278560 | tf_op jit(solution)/shard_map/ppermute | solution.py:21
  64.1 2.0 %collective-permute-start.7 = (bf16[16,768]{1,0:T(8,128)(2,1)S(1)}, bf16[16,768]{1,0:T(8,128)(2,1)S(1)}, u32[]{:S(2)}, u32[]{:S(2)}) collective-permute-start(bf16[16,768]{1,0:T(8,128)(2,1)S(1)} %fusion.13), channel_id=1, source_target_pairs={{0,1},{2,3},{8,9},{10,11},{16,17},{18,19},{24,25},{26,27},{1,8},{3... | collective-permute-start | bytes 73736 | tf_op jit(solution)/shard_map/ppermute | solution.py:638
  66.1 2.2 %collective-permute-done.7.refs_4_ = bf16[16,768]{1,0:T(8,128)(2,1)S(1)} collective-permute-done((bf16[16,768]{1,0:T(8,128)(2,1)S(1)}, bf16[16,768]{1,0:T(8,128)(2,1)S(1)}, u32[]{:S(2)}, u32[]{:S(2)}) %collective-permute-start.7) | collective-permute-done | bytes 24608 | tf_op jit(solution)/shard_map/ppermute | solution.py:638
  68.9 3.5 %scan.1 = (bf16[256,512]{1,0:T(8,128)(2,1)}, bf16[256,256]{1,0:T(8,128)(2,1)}, f32[24,256]{1,0:T(8,128)}, bf16[144,512]{1,0:T(8,128)(2,1)}, f32[8,512]{1,0:T(8,128)}) custom-call(bf16[272,512]{1,0:T(8,128)(2,1)} %copy-done.6, bf16[272,512]{1,0:T(8,128)(2,1)} %copy-done.11, bf16[256,256]{1,0:T(8,128)(2,1)} %copy-done.10, bf16[256,256]{1,0:T(8,128)(2,1)} %copy-done.14, ...), custom_call_target="tpu_custom_call" | custom-call | tf_op jit(solution)/shard_map/scan/pallas_call | solution.py:489
  72.4 2.5 %collective-permute-start.10 = (bf16[144,512]{1,0:T(8,128)(2,1)}, bf16[144,512]{1,0:T(8,128)(2,1)S(1)}, u32[]{:S(2)}, u32[]{:S(2)}) collective-permute-start(bf16[144,512]{1,0:T(8,128)(2,1)} %get-tuple-element.65.state), channel_id=1, source_target_pairs={{0,1},{1,0},{2,3},{3,2},{4,5},{5,4},{6,7},{7,6},{8,9},{9,8},{10,11... | collective-permute-start | bytes 442376 | tf_op jit(solution)/shard_map/ppermute | solution.py:21
  74.8 1.3 %convert_add_fusion.1 = bf16[2,256,512]{2,1,0:T(8,128)(2,1)S(1)} fusion(bf16[2,256,512]{2,1,0:T(8,128)(2,1)} %collective-permute-done.8, bf16[2,256,512]{2,1,0:T(8,128)(2,1)} %get-tuple-element.63), kind=kLoop, calls=%fused_computation.13 | loop fusion | flops 1048576 | bytes 1572864 | tf_op jit(solution)/shard_map/add | solution.py:605
  76.9 2.7 %collective-permute-start.9 = (bf16[256,512]{1,0:T(8,128)(2,1)S(1)}, bf16[256,512]{1,0:T(8,128)(2,1)}, u32[]{:S(2)}, u32[]{:S(2)}) collective-permute-start(bf16[256,512]{1,0:T(8,128)(2,1)S(1)} %get-tuple-element.81), channel_id=1, source_target_pairs={{0,2},{1,3},{2,0},{3,1},{4,6},{5,7},{6,4},{7,5},{8,10},{9,11},{10,... | collective-permute-start | bytes 786440 | tf_op jit(solution)/shard_map/ppermute | solution.py:21
  79.7 2.7 %inside.1.local = f32[256,512]{1,0:T(8,128)} custom-call(bf16[256,512]{1,0:T(8,128)(2,1)} %get-tuple-element.66.streams, bf16[256,256]{1,0:T(8,128)(2,1)} %get-tuple-element.67.maps, f32[24,256]{1,0:T(8,128)} %get-tuple-element.68.meta, f32[8,512]{1,0:T(8,128)} %get-tuple-element.69.params), custom_call_target="tpu_custom_call" | custom-call | tf_op jit(solution)/shard_map/inside/pallas_call | solution.py:537
  83.1 1.7 %join.1 = bf16[144,512]{1,0:T(8,128)(2,1)} custom-call(bf16[144,512]{1,0:T(8,128)(2,1)} %get-tuple-element.65.state, bf16[144,512]{1,0:T(8,128)(2,1)} %copy-done.8), custom_call_target="tpu_custom_call" | custom-call | tf_op jit(solution)/shard_map/join/pallas_call | solution.py:511
  84.8 1.5 %collective-permute-start.11 = (bf16[144,512]{1,0:T(8,128)(2,1)}, bf16[144,512]{1,0:T(8,128)(2,1)S(1)}, u32[]{:S(2)}, u32[]{:S(2)}) collective-permute-start(bf16[144,512]{1,0:T(8,128)(2,1)} %join.1), channel_id=1, source_target_pairs={{0,8},{8,0},{16,24},{24,16},{1,9},{9,1},{17,25},{25,17},{2,10},{10... | collective-permute-start | bytes 442376 | tf_op jit(solution)/shard_map/ppermute | solution.py:21
  86.3 1.5 %collective-permute-start.12 = (bf16[144,512]{1,0:T(8,128)(2,1)}, bf16[144,512]{1,0:T(8,128)(2,1)}, u32[]{:S(2)}, u32[]{:S(2)}) collective-permute-start(bf16[144,512]{1,0:T(8,128)(2,1)} %join.1), channel_id=1, source_target_pairs={{0,16},{8,24},{16,0},{24,8},{1,17},{9,25},{17,1},{25,9},{2,18},{10... | collective-permute-start | bytes 442376 | tf_op jit(solution)/shard_map/ppermute | solution.py:21
  88.3 2.3 %collective-permute-done.9.received = bf16[256,512]{1,0:T(8,128)(2,1)} collective-permute-done((bf16[256,512]{1,0:T(8,128)(2,1)S(1)}, bf16[256,512]{1,0:T(8,128)(2,1)}, u32[]{:S(2)}, u32[]{:S(2)}) %collective-permute-start.9) | collective-permute-done | bytes 262176 | tf_op jit(solution)/shard_map/ppermute | solution.py:21
  91.7 1.5 %collective-permute-done.12.others_and_out_1_ = bf16[144,512]{1,0:T(8,128)(2,1)} collective-permute-done((bf16[144,512]{1,0:T(8,128)(2,1)}, bf16[144,512]{1,0:T(8,128)(2,1)}, u32[]{:S(2)}, u32[]{:S(2)}) %collective-permute-start.12) | collective-permute-done | bytes 147488 | tf_op jit(solution)/shard_map/ppermute | solution.py:21
  93.2 1.2 %collective-permute-done.13.others_and_out_2_ = bf16[144,512]{1,0:T(8,128)(2,1)} collective-permute-done((bf16[144,512]{1,0:T(8,128)(2,1)}, bf16[144,512]{1,0:T(8,128)(2,1)}, u32[]{:S(2)}, u32[]{:S(2)}) %collective-permute-start.13) | collective-permute-done | bytes 147488 | tf_op jit(solution)/shard_map/ppermute | solution.py:21
  94.4 3.2 %gate.1 = bf16[256,512]{1,0:T(8,128)(2,1)} custom-call(bf16[256,512]{1,0:T(8,128)(2,1)} %get-tuple-element.82.kept, bf16[256,512]{1,0:T(8,128)(2,1)} %collective-permute-done.9.received, f32[256,512]{1,0:T(8,128)} %inside.1.local, bf16[256,256]{1,0:T(8,128)(2,1)} %get-tuple-element.67.maps, f32[24,256]{1,0:T(8,128)} %get-tuple-element.68.meta, ...), custom_call_target="tpu_custom_call" | custom-call | tf_op jit(solution)/shard_map/gate/pallas_call | solution.py:578
  97.9 1.6 %collective-permute-start.14 = (bf16[256,512]{1,0:T(8,128)(2,1)}, bf16[256,512]{1,0:T(8,128)(2,1)S(1)}, u32[]{:S(2)}, u32[]{:S(2)}) collective-permute-start(bf16[256,512]{1,0:T(8,128)(2,1)} %gate.1), channel_id=1, source_target_pairs={{0,0},{1,1},{2,6},{3,7},{4,4},{5,5},{6,2},{7,3},{8,8},{9,9},{10,14... | collective-permute-start | bytes 786440 | tf_op jit(solution)/shard_map/ppermute | solution.py:652
  99.5 1.9 %collective-permute-start.16 = (bf16[256,512]{1,0:T(8,128)(2,1)}, bf16[256,512]{1,0:T(8,128)(2,1)S(1)}, u32[]{:S(2)}, u32[]{:S(2)}) collective-permute-start(bf16[256,512]{1,0:T(8,128)(2,1)} %gate.1), channel_id=1, source_target_pairs={{0,1},{1,0},{2,7},{3,6},{4,5},{5,4},{6,3},{7,2},{8,9},{9,8},{10,15... | collective-permute-start | bytes 786440 | tf_op jit(solution)/shard_map/ppermute | solution.py:652
  101.3 9.6 %collective-permute-done.15 = bf16[256,512]{1,0:T(8,128)(2,1)S(1)} collective-permute-done((bf16[256,512]{1,0:T(8,128)(2,1)}, bf16[256,512]{1,0:T(8,128)(2,1)S(1)}, u32[]{:S(2)}, u32[]{:S(2)}) %collective-permute-start.15) | collective-permute-done | bytes 262176 | tf_op jit(solution)/shard_map/ppermute | solution.py:652
  115.4 2.5 %collective-permute-done.17 = bf16[256,512]{1,0:T(8,128)(2,1)S(1)} collective-permute-done((bf16[256,512]{1,0:T(8,128)(2,1)S(1)}, bf16[256,512]{1,0:T(8,128)(2,1)S(1)}, u32[]{:S(2)}, u32[]{:S(2)}) %collective-permute-start.17) | collective-permute-done | bytes 262176 | tf_op jit(solution)/shard_map/ppermute | solution.py:21
  117.9 1.8 %fusion.3 = bf16[1,512,2048]{2,1,0:T(8,128)(2,1)} fusion(bf16[1,512,2048]{2,1,0:T(8,128)(2,1)} %copy-done.4, s32[]{:T(128)S(6)} %select_n.104, f32[256,2048]{1,0:T(8,128)S(1)} %fusion.15, bf16[256,512]{1,0:T(8,128)(2,1)S(1)} %collective-permute-done.17, bf16[512,2048]{1,0:T(8,128)(2,1)S(1)} %get-tuple-element.73, bf16[256,2048]{1,0:T(8,128)(2,1)S(1)} %get-tuple-element.74), kind=kOutput, calls=%fused_computation.5 | convolution fusion | flops 538968064 | bytes 6553604 | tf_op jit(solution)/shard_map/dot_general | solution.py:661
  (61 shorter events, 11.3 us)
Async XLA Ops:
  0.0 5.4 %collective-permute-start.1 = (bf16[512,2048]{1,0:T(8,128)(2,1)}, bf16[512,2048]{1,0:T(8,128)(2,1)S(1)}, u32[]{:S(2)}, u32[]{:S(2)}) collective-permute-start(bf16[512,2048]{1,0:T(8,128)(2,1)} %bitcast.38), channel_id=1, source_target_pairs={{0,4},{4,0},{1,5},{5,1},{2,6},{6,2},{3,7},{7,3},{8,12},{12,8},{9,1... | collective-permute-start | bytes 6291464 | tf_op jit(solution)/shard_map/ppermute | solution.py:21
  0.5 4.9 %collective-permute-start = (bf16[256,1280]{1,0:T(8,128)(2,1)}, bf16[256,1280]{1,0:T(8,128)(2,1)S(1)}, u32[]{:S(2)}, u32[]{:S(2)}) collective-permute-start(bf16[256,1280]{1,0:T(8,128)(2,1)} %bitcast.40), channel_id=1, source_target_pairs={{0,4},{4,0},{1,5},{5,1},{2,6},{6,2},{3,7},{7,3},{8,12},{12,8},{9,1... | collective-permute-start | bytes 1966088 | tf_op jit(solution)/shard_map/ppermute | solution.py:21
  5.4 1.5 %copy-start.3 = (bf16[512,2048]{1,0:T(8,128)(2,1)}, bf16[512,2048]{1,0:T(8,128)(2,1)S(1)}, u32[]{:S(2)}) copy-start(bf16[512,2048]{1,0:T(8,128)(2,1)S(1)} %collective-permute-done.1.text_other) | copy-start | bytes 6291460
  19.4 9.8 %collective-permute-start.2 = (bf16[2,256,256]{2,1,0:T(8,128)(2,1)}, bf16[2,256,256]{2,1,0:T(8,128)(2,1)S(1)}, u32[]{:S(2)}, u32[]{:S(2)}) collective-permute-start(bf16[2,256,256]{2,1,0:T(8,128)(2,1)} %get-tuple-element.42), channel_id=1, source_target_pairs={{0,1},{1,0},{2,3},{3,2},{4,5},{5,4},{6,7},{7,6},{8,9},{9,8},{10,11... | collective-permute-start | bytes 786440 | tf_op jit(solution)/shard_map/ppermute | solution.py:21
  22.4 6.8 %copy-start.12 = (bf16[2,256,256]{2,1,0:T(8,128)(2,1)S(1)}, bf16[2,256,256]{2,1,0:T(8,128)(2,1)}, u32[]{:S(2)}) copy-start(bf16[2,256,256]{2,1,0:T(8,128)(2,1)} %get-tuple-element.41) | copy-start | bytes 786436
  22.4 8.8 %copy-start.1 = (bf16[1,512,2048]{2,1,0:T(8,128)(2,1)S(1)}, bf16[1,512,2048]{2,1,0:T(8,128)(2,1)}, u32[]{:S(2)}) copy-start(bf16[1,512,2048]{2,1,0:T(8,128)(2,1)} %param.17) | copy-start | bytes 6291460
  22.4 8.8 %copy-start.16 = (bf16[2048]{0:T(1024)(128)(2,1)S(1)}, bf16[2048]{0:T(1024)(128)(2,1)}, u32[]{:S(2)}) copy-start(bf16[2048]{0:T(1024)(128)(2,1)} %newline.1) | copy-start | bytes 12292
  29.3 23.9 %copy-start.10 = (bf16[256,256]{1,0:T(8,128)(2,1)}, bf16[256,256]{1,0:T(8,128)(2,1)S(1)}, u32[]{:S(2)}) copy-start(bf16[256,256]{1,0:T(8,128)(2,1)S(1)} %get-tuple-element.59.refs_2_) | copy-start | bytes 393220
  29.3 23.9 %collective-permute-start.6 = (bf16[512,2048]{1,0:T(8,128)(2,1)}, bf16[512,2048]{1,0:T(8,128)(2,1)}, u32[]{:S(2)}, u32[]{:S(2)}) collective-permute-start(bf16[512,2048]{1,0:T(8,128)(2,1)} %param.33), channel_id=1, source_target_pairs={{0,4},{4,0},{1,5},{5,1},{2,6},{6,2},{3,7},{7,3},{8,12},{12,8},{9,1... | collective-permute-start | bytes 6291464 | tf_op jit(solution)/shard_map/ppermute | solution.py:21
  29.4 18.2 %collective-permute-start.3 = (bf16[2,272,512]{2,1,0:T(8,128)(2,1)}, bf16[2,272,512]{2,1,0:T(8,128)(2,1)}, u32[]{:S(2)}, u32[]{:S(2)}) collective-permute-start(bf16[2,272,512]{2,1,0:T(8,128)(2,1)} %get-tuple-element.48), channel_id=1, source_target_pairs={{0,1},{1,0},{2,3},{3,2},{4,5},{5,4},{6,7},{7,6},{8,9},{9,8},{10,11... | collective-permute-start | bytes 1671176 | tf_op jit(solution)/shard_map/ppermute | solution.py:21
  31.2 16.3 %copy-start.9 = (bf16[2,272,512]{2,1,0:T(8,128)(2,1)S(1)}, bf16[2,272,512]{2,1,0:T(8,128)(2,1)}, u32[]{:S(2)}) copy-start(bf16[2,272,512]{2,1,0:T(8,128)(2,1)} %get-tuple-element.40) | copy-start | bytes 1671172
  33.7 19.5 %copy-start.5 = (bf16[512,2048]{1,0:T(8,128)(2,1)S(1)}, bf16[512,2048]{1,0:T(8,128)(2,1)}, u32[]{:S(2)}) copy-start(bf16[512,2048]{1,0:T(8,128)(2,1)} %param.33) | copy-start | bytes 6291460
  33.7 15.1 %collective-permute-start.4 = (bf16[256,256]{1,0:T(8,128)(2,1)S(1)}, bf16[256,256]{1,0:T(8,128)(2,1)S(1)}, u32[]{:S(2)}, u32[]{:S(2)}) collective-permute-start(bf16[256,256]{1,0:T(8,128)(2,1)S(1)} %get-tuple-element.50), channel_id=1, source_target_pairs={{0,2},{1,3},{2,0},{3,1},{4,6},{5,7},{6,4},{7,5},{8,10},{9,11},{10,... | collective-permute-start | bytes 393224 | tf_op jit(solution)/shard_map/ppermute | solution.py:21
  48.8 15.3 %copy-start.6 = (bf16[272,512]{1,0:T(8,128)(2,1)}, bf16[272,512]{1,0:T(8,128)(2,1)S(1)}, u32[]{:S(2)}) copy-start(bf16[272,512]{1,0:T(8,128)(2,1)S(1)} %get-tuple-element.57.refs_0_) | copy-start | bytes 835588
  48.8 7.6 %copy-start.14 = (bf16[256,256]{1,0:T(8,128)(2,1)}, bf16[256,256]{1,0:T(8,128)(2,1)S(1)}, u32[]{:S(2)}) copy-start(bf16[256,256]{1,0:T(8,128)(2,1)S(1)} %collective-permute-done.4.refs_3_) | copy-start | bytes 393220
  48.8 15.3 %collective-permute-start.5 = (bf16[272,512]{1,0:T(8,128)(2,1)S(1)}, bf16[272,512]{1,0:T(8,128)(2,1)S(1)}, u32[]{:S(2)}, u32[]{:S(2)}) collective-permute-start(bf16[272,512]{1,0:T(8,128)(2,1)S(1)} %get-tuple-element.52), channel_id=1, source_target_pairs={{0,2},{1,3},{2,0},{3,1},{4,6},{5,7},{6,4},{7,5},{8,10},{9,11},{10,... | collective-permute-start | bytes 835592 | tf_op jit(solution)/shard_map/ppermute | solution.py:21
  50.7 24.1 %collective-permute-start.8 = (bf16[2,256,512]{2,1,0:T(8,128)(2,1)}, bf16[2,256,512]{2,1,0:T(8,128)(2,1)}, u32[]{:S(2)}, u32[]{:S(2)}) collective-permute-start(bf16[2,256,512]{2,1,0:T(8,128)(2,1)} %get-tuple-element.64), channel_id=1, source_target_pairs={{0,1},{1,0},{2,3},{3,2},{4,5},{5,4},{6,7},{7,6},{8,9},{9,8},{10,11... | collective-permute-start | bytes 1572872 | tf_op jit(solution)/shard_map/ppermute | solution.py:21
  64.1 4.2 %copy-start.11 = (bf16[272,512]{1,0:T(8,128)(2,1)}, bf16[272,512]{1,0:T(8,128)(2,1)S(1)}, u32[]{:S(2)}) copy-start(bf16[272,512]{1,0:T(8,128)(2,1)S(1)} %collective-permute-done.5.refs_1_) | copy-start | bytes 835588
  64.1 4.2 %collective-permute-start.7 = (bf16[16,768]{1,0:T(8,128)(2,1)S(1)}, bf16[16,768]{1,0:T(8,128)(2,1)S(1)}, u32[]{:S(2)}, u32[]{:S(2)}) collective-permute-start(bf16[16,768]{1,0:T(8,128)(2,1)S(1)} %fusion.13), channel_id=1, source_target_pairs={{0,1},{2,3},{8,9},{10,11},{16,17},{18,19},{24,25},{26,27},{1,8},{3... | collective-permute-start | bytes 73736 | tf_op jit(solution)/shard_map/ppermute | solution.py:638
  72.4 10.1 %collective-permute-start.10 = (bf16[144,512]{1,0:T(8,128)(2,1)}, bf16[144,512]{1,0:T(8,128)(2,1)S(1)}, u32[]{:S(2)}, u32[]{:S(2)}) collective-permute-start(bf16[144,512]{1,0:T(8,128)(2,1)} %get-tuple-element.65.state), channel_id=1, source_target_pairs={{0,1},{1,0},{2,3},{3,2},{4,5},{5,4},{6,7},{7,6},{8,9},{9,8},{10,11... | collective-permute-start | bytes 442376 | tf_op jit(solution)/shard_map/ppermute | solution.py:21
  76.9 13.7 %collective-permute-start.9 = (bf16[256,512]{1,0:T(8,128)(2,1)S(1)}, bf16[256,512]{1,0:T(8,128)(2,1)}, u32[]{:S(2)}, u32[]{:S(2)}) collective-permute-start(bf16[256,512]{1,0:T(8,128)(2,1)S(1)} %get-tuple-element.81), channel_id=1, source_target_pairs={{0,2},{1,3},{2,0},{3,1},{4,6},{5,7},{6,4},{7,5},{8,10},{9,11},{10,... | collective-permute-start | bytes 786440 | tf_op jit(solution)/shard_map/ppermute | solution.py:21
  84.8 6.9 %collective-permute-start.11 = (bf16[144,512]{1,0:T(8,128)(2,1)}, bf16[144,512]{1,0:T(8,128)(2,1)S(1)}, u32[]{:S(2)}, u32[]{:S(2)}) collective-permute-start(bf16[144,512]{1,0:T(8,128)(2,1)} %join.1), channel_id=1, source_target_pairs={{0,8},{8,0},{16,24},{24,16},{1,9},{9,1},{17,25},{25,17},{2,10},{10... | collective-permute-start | bytes 442376 | tf_op jit(solution)/shard_map/ppermute | solution.py:21
  86.3 6.9 %collective-permute-start.12 = (bf16[144,512]{1,0:T(8,128)(2,1)}, bf16[144,512]{1,0:T(8,128)(2,1)}, u32[]{:S(2)}, u32[]{:S(2)}) collective-permute-start(bf16[144,512]{1,0:T(8,128)(2,1)} %join.1), channel_id=1, source_target_pairs={{0,16},{8,24},{16,0},{24,8},{1,17},{9,25},{17,1},{25,9},{2,18},{10... | collective-permute-start | bytes 442376 | tf_op jit(solution)/shard_map/ppermute | solution.py:21
  87.8 6.6 %collective-permute-start.13 = (bf16[144,512]{1,0:T(8,128)(2,1)}, bf16[144,512]{1,0:T(8,128)(2,1)}, u32[]{:S(2)}, u32[]{:S(2)}) collective-permute-start(bf16[144,512]{1,0:T(8,128)(2,1)} %join.1), channel_id=1, source_target_pairs={{0,24},{8,16},{16,8},{24,0},{1,25},{9,17},{17,9},{25,1},{2,26},{10... | collective-permute-start | bytes 442376 | tf_op jit(solution)/shard_map/ppermute | solution.py:21
  91.7 2.7 %copy-start.13 = (bf16[144,512]{1,0:T(8,128)(2,1)}, bf16[144,512]{1,0:T(8,128)(2,1)S(1)}, u32[]{:S(2)}) copy-start(bf16[144,512]{1,0:T(8,128)(2,1)S(1)} %collective-permute-done.11.others_and_out_0_) | copy-start | bytes 442372
  97.6 13.3 %collective-permute-start.15 = (bf16[256,512]{1,0:T(8,128)(2,1)}, bf16[256,512]{1,0:T(8,128)(2,1)S(1)}, u32[]{:S(2)}, u32[]{:S(2)}) collective-permute-start(bf16[256,512]{1,0:T(8,128)(2,1)} %gate.1), channel_id=1, source_target_pairs={{0,2},{1,3},{2,4},{3,5},{4,6},{5,7},{6,0},{7,1},{8,10},{9,11},{10,... | collective-permute-start | bytes 786440 | tf_op jit(solution)/shard_map/ppermute | solution.py:652
  97.9 13.8 %collective-permute-start.14 = (bf16[256,512]{1,0:T(8,128)(2,1)}, bf16[256,512]{1,0:T(8,128)(2,1)S(1)}, u32[]{:S(2)}, u32[]{:S(2)}) collective-permute-start(bf16[256,512]{1,0:T(8,128)(2,1)} %gate.1), channel_id=1, source_target_pairs={{0,0},{1,1},{2,6},{3,7},{4,4},{5,5},{6,2},{7,3},{8,8},{9,9},{10,14... | collective-permute-start | bytes 786440 | tf_op jit(solution)/shard_map/ppermute | solution.py:652
  99.5 14.6 %collective-permute-start.16 = (bf16[256,512]{1,0:T(8,128)(2,1)}, bf16[256,512]{1,0:T(8,128)(2,1)S(1)}, u32[]{:S(2)}, u32[]{:S(2)}) collective-permute-start(bf16[256,512]{1,0:T(8,128)(2,1)} %gate.1), channel_id=1, source_target_pairs={{0,1},{1,0},{2,7},{3,6},{4,5},{5,4},{6,3},{7,2},{8,9},{9,8},{10,15... | collective-permute-start | bytes 786440 | tf_op jit(solution)/shard_map/ppermute | solution.py:652
  111.0 7.0 %collective-permute-start.17 = (bf16[256,512]{1,0:T(8,128)(2,1)S(1)}, bf16[256,512]{1,0:T(8,128)(2,1)S(1)}, u32[]{:S(2)}, u32[]{:S(2)}) collective-permute-start(bf16[256,512]{1,0:T(8,128)(2,1)S(1)} %collective-permute-done.15), channel_id=1, source_target_pairs={{0,1},{1,0},{2,3},{3,2},{4,5},{5,4},{6,7},{7,6},{8,9},{9,8},{10,11... | collective-permute-start | bytes 786440 | tf_op jit(solution)/shard_map/ppermute | solution.py:21
  111.0 1.2 %copy-start.2 = (bf16[256,2048]{1,0:T(8,128)(2,1)S(1)}, bf16[256,2048]{1,0:T(8,128)(2,1)}, u32[]{:S(2)}) copy-start(bf16[256,2048]{1,0:T(8,128)(2,1)} %get-tuple-element.56) | copy-start | bytes 3145732
  111.7 1.7 %copy-start = (bf16[512,2048]{1,0:T(8,128)(2,1)S(1)}, bf16[512,2048]{1,0:T(8,128)(2,1)}, u32[]{:S(2)}) copy-start(bf16[512,2048]{1,0:T(8,128)(2,1)} %get-tuple-element.72) | copy-start | bytes 6291460
  114.1 1.3 %copy-start.4 = (bf16[1,512,2048]{2,1,0:T(8,128)(2,1)}, bf16[1,512,2048]{2,1,0:T(8,128)(2,1)S(1)}, u32[]{:S(2)}) copy-start(bf16[1,512,2048]{2,1,0:T(8,128)(2,1)S(1)} %fusion.5) | copy-start | bytes 6291460
  (3 other events, 2.1 us)

commit v6 on v5

--- a/solution.py
+++ b/solution.py
@@ -436,7 +436,7 @@
 
 
 def scan_body(
-    width, kept_x, received_x, kept, received, before, taps_maps, streams, maps, meta, state, params
+    width, kept_x, received_x, kept, received, before, taps_maps, streams, maps, meta, cols, state, params
 ):
     first = kept_x[...].astype(F32) + received_x[...].astype(F32)
     half = first.shape[0] - 16
@@ -461,8 +461,15 @@
     cumulative = contract(decays, upper, ((1,), (0,)), HIGHEST)
     final = cumulative[:, half - 1 : half]
     carry = jnp.exp(final - cumulative) * step
-    scale_main = columns_of(jnp.broadcast_to(scale, (8, half)))[:, 0:1]
-    scale_edge = columns_of(jnp.broadcast_to(scale_before, (8, 128)))[120:128, 0:1]
+    wide = jnp.concatenate([scale_before, jnp.zeros((1, half - 128), F32)], 1)
+    columns = columns_of(
+        jnp.concatenate(
+            [cumulative, carry] + [jnp.broadcast_to(row, (8, half)) for row in (scale, wide)], 0
+        )
+    )
+    cols[...] = columns
+    scale_main = columns[:, 16:17]
+    scale_edge = columns[120:128, 24:25]
     taps_x = slots[0:4]
     edge = before[0:8, :].astype(F32) * scale_edge
     x = silu(filtered(first[0:half] * scale_main, edge[:, 0:512], taps_x))
@@ -473,7 +480,9 @@
             taps_maps[...].astype(F32),
         )
     ).astype(BF16)
-    carried = contract(columns_of(carry), owner, ((1,), (0,)), HIGHEST)
+    carried = jnp.concatenate(
+        [jnp.broadcast_to(columns[:, 8 + h : 9 + h], (half, 128)) for h in range(4)], 1
+    )
     state[0:128, :] = contract(both[:, 0:128], (x * carried).astype(BF16), ((0,), (0,))).astype(BF16)
     total = jnp.sum(jnp.exp(final) * owner, 0, keepdims=True)
     state[128:144, :] = jnp.broadcast_to(total, (16, 512)).astype(BF16)
@@ -481,7 +490,6 @@
     maps[...] = both
     meta[0:8, :] = cumulative
     meta[8:16, :] = step
-    meta[16:24, :] = jnp.broadcast_to(scale, (8, half))
 
 
 def scan(width, *operands):
@@ -491,7 +499,8 @@
         out_shape=[
             jax.ShapeDtypeStruct((half, 512), BF16),
             jax.ShapeDtypeStruct((half, 256), BF16),
-            jax.ShapeDtypeStruct((24, half), F32),
+            jax.ShapeDtypeStruct((16, half), F32),
+            jax.ShapeDtypeStruct((half, 32), F32),
             jax.ShapeDtypeStruct((144, 512), BF16),
             jax.ShapeDtypeStruct((8, 512), F32),
         ],
@@ -499,49 +508,43 @@
     )(*operands)
 
 
-def join_body(state, partner, out):
+def join(state, partner):
     late = lax.axis_index("tensor") % 2 == 1
-    mine, other = state[...].astype(F32), partner[...].astype(F32)
-    first, second = jnp.where(late, other, mine), jnp.where(late, mine, other)
-    out[0:128, :] = (second[128:129] * first[0:128] + second[0:128]).astype(BF16)
-    out[128:144, :] = (first[128:144] * second[128:144]).astype(BF16)
-
-
-def join(state, partner):
-    return pl.pallas_call(
-        join_body, out_shape=jax.ShapeDtypeStruct(state.shape, BF16), name="join"
-    )(state, partner)
-
-
-def inside_body(streams, maps, meta, params, out):
+    first = jnp.where(late, partner, state).astype(F32)
+    second = jnp.where(late, state, partner).astype(F32)
+    decay = lax.broadcasted_iota(jnp.int32, state.shape, 0) >= 128
+    return jnp.where(decay, first * second, second[128:129] * first + second).astype(BF16)
+
+
+def inside_body(streams, maps, meta, cols, params, out):
     half = streams.shape[0]
     cumulative = meta[0:8, :]
     step = meta[8:16, :]
-    cum_cols = columns_of(cumulative)
+    cum_cols = cols[:, 0:8]
     scores = contract(maps[:, 128:256], maps[:, 0:128], ((1,), (1,)))
     lower = lax.broadcasted_iota(jnp.int32, (half, half), 0) >= lax.broadcasted_iota(
         jnp.int32, (half, half), 1
     )
     scores = jnp.where(lower, scores, 0.0)
     for head in range(4):
-        cols = slice(128 * head, 128 * head + 128)
-        x = streams[:, cols]
+        lanes = slice(128 * head, 128 * head + 128)
+        x = streams[:, lanes]
         gaps = cum_cols[:, head : head + 1] - cumulative[head : head + 1]
         weights = jnp.exp(jnp.where(lower, gaps, 0.0)) * scores * step[head : head + 1]
         y = jnp.dot(weights.astype(BF16), x, preferred_element_type=F32)
-        through = jnp.sum(params[7:8, cols], 1, keepdims=True) * (1.0 / 32)
-        out[:, cols] = y + through * x.astype(F32)
-
-
-def inside(streams, maps, meta, params):
+        through = jnp.sum(params[7:8, lanes], 1, keepdims=True) * (1.0 / 32)
+        out[:, lanes] = y + through * x.astype(F32)
+
+
+def inside(streams, maps, meta, cols, params):
     return pl.pallas_call(
         inside_body,
         out_shape=jax.ShapeDtypeStruct(streams.shape, F32),
         name="inside",
-    )(streams, maps, meta, params)
-
-
-def gate_body(kept, received, local, maps, meta, params, partner, *others_and_out):
+    )(streams, maps, meta, cols, params)
+
+
+def gate_body(kept, received, local, maps, cols, params, partner, *others_and_out):
     *others, out = others_and_out
     half = local.shape[0]
     section = lax.axis_index("segment")
@@ -556,22 +559,22 @@
         prior = jnp.where(source < section, piece[128:129] * prior + piece[0:128], prior)
     before = partner[...].astype(F32)
     prior = jnp.where(late, before[128:129] * prior + before[0:128], prior)
-    scale = columns_of(meta[16:24, :])[:, 0:1]
-    entry = jnp.exp(columns_of(meta[0:8, :]))
+    scale = cols[:, 16:17]
+    entry = jnp.exp(cols[:, 0:8])
     across = jnp.dot(maps[:, 128:256], prior.astype(BF16), preferred_element_type=F32)
     gated = []
     squares = jnp.zeros((half, 1), F32)
     for head in range(4):
-        cols = slice(128 * head, 128 * head + 128)
-        y = local[:, cols] + entry[:, head : head + 1] * across[:, cols]
-        gates = kept[:, cols].astype(F32) + received[:, cols].astype(F32)
+        lanes = slice(128 * head, 128 * head + 128)
+        y = local[:, lanes] + entry[:, head : head + 1] * across[:, lanes]
+        gates = kept[:, lanes].astype(F32) + received[:, lanes].astype(F32)
         value = y * silu(gates * scale)
         squares = squares + jnp.sum(value * value, -1, keepdims=True)
         gated.append(value)
     norm = lax.rsqrt(squares / 512 + EPS)
     for head in range(4):
-        cols = slice(128 * head, 128 * head + 128)
-        out[:, cols] = (gated[head] * norm * params[4:5, cols]).astype(BF16)
+        lanes = slice(128 * head, 128 * head + 128)
+        out[:, lanes] = (gated[head] * norm * params[4:5, lanes]).astype(BF16)
 
 
 def gate(local, *operands):
@@ -636,18 +639,18 @@
     before = (kept_x[before].astype(F32) + received_x[before].astype(F32)).astype(BF16)
     before = jnp.concatenate([before, jnp.pad(ends, ((0, 8), (0, 0)))], 1)
     before = lax.ppermute(before, ("segment", "tensor"), route)
-    streams, maps, meta, state, params = scan(
+    streams, maps, meta, as_columns, state, params = scan(
         width, kept_x, received_x, kept, received, before, conv_bc
     )
     meta, keep_gates = lax.optimization_barrier((meta, keep_gates))
-    local = inside(streams, maps, meta, params)
+    local = inside(streams, maps, meta, as_columns, params)
     partner = swapped(state, "tensor", 1)
     whole = join(state, partner)
     whole, local = lax.optimization_barrier((whole, local))
     others = [swapped(whole, "segment", bits) for bits in range(1, segment_count)]
     leaves, kept = added(keep_gates, arrived_gates)
     received = swapped(leaves, "tensor", 2)
-    normed = gate(local, kept, received, maps, meta, params, partner, *others)
+    normed = gate(local, kept, received, maps, as_columns, params, partner, *others)
     near, far, here = (
         lax.ppermute(
             normed, ("dp", "tensor"), [(i, (i if i % 4 < 2 else i ^ 4) ^ bits) for i in range(8)]

time: 120 us -> 119 us (level)
  Pallas kernels: 29.6 us -> 27.4 us
    pallas_call x1 -> x0, Pallas kernels: 1.71 us -> none  [join(): pl.pallas_call(join_body, out_shape=jax.ShapeDtypeStruct(state.shape, BF1...]
    unnamed x34 -> x36, local copies, waits for them, and re-layouts: 4.82 us -> 4.18 us
  transfers between devices with their start and end apart: 18 -> 18, of which waited for: 11 -> 9; matrix products, arithmetic and copies ran while one was open for 10% -> 10% of each run, Pallas kernels for 12% -> 10%
where the time goes in v6:
time: 119 us
  waiting for transfers between devices  43.7 us (37%)
  starting transfers between devices  27.6 us (23%)
  Pallas kernels  27.4 us (23%)
  other arithmetic  9.35 us (8%)
  local copies, waits for them, and re-layouts  4.43 us (4%)
  matrix products  3.93 us (3%)
  between operations  2.19 us (2%)
    ppermute x14, waiting for transfers between devices, swapped(): lax.ppermute(block, axis, [(i, i ^ bits) for i in range(lax.axis_size(axi...  31.6 us
    ppermute x14, starting transfers between devices, swapped(): lax.ppermute(block, axis, [(i, i ^ bits) for i in range(lax.axis_size(axi...  21.1 us
    pallas_call x1, Pallas kernels, enter(): pl.pallas_call(enter_body, in_specs=[pl.BlockSpec(memory_space=pltpu.SMEM...  12.5 us
    ppermute x3, waiting for transfers between devices, per_device_halves(): lax.ppermute(normed, ('dp', 'tensor'), [(i, (i if i % 4 < 2 else i ^ 4) ^...  9.9 us
    pallas_call x1, Pallas kernels, gates(): pl.pallas_call(gates_body, in_specs=[whole, whole], out_specs=[whole, who...  5.97 us
    ppermute x3, starting transfers between devices, per_device_halves(): lax.ppermute(normed, ('dp', 'tensor'), [(i, (i if i % 4 < 2 else i ^ 4) ^...  4.47 us
    unnamed x36, local copies, waits for them, and re-layouts  4.18 us
    pallas_call x1, Pallas kernels, scan(): pl.pallas_call(lambda *refs: scan_body(width, *refs), out_shape=[jax.Shap...  3.6 us
  transfers between devices with their start and end apart: 18, of which 9 were waited for; matrix products, arithmetic and copies ran while one was open for 10% of the time, Pallas kernels for 10%

profile of v6, /device:TPU:0, one launch (start us, length us, event | category | flops | bytes accessed | tf_op | source)
XLA Modules:
  0.0 118.6 jit_solution(3833446706250095764)
XLA Ops:
  2.5 2.9 %collective-permute-done.feats_other = bf16[256,1280]{1,0:T(8,128)(2,1)S(1)} collective-permute-done((bf16[256,1280]{1,0:T(8,128)(2,1)}, bf16[256,1280]{1,0:T(8,128)(2,1)S(1)}, u32[]{:S(2)}, u32[]{:S(2)}) %collective-permute-start) | collective-permute-done | bytes 655392 | tf_op jit(solution)/shard_map/ppermute | solution.py:21
  6.9 12.5 %enter.1 = (bf16[512,2048]{1,0:T(8,128)(2,1)}, bf16[1024,2048]{1,0:T(8,128)(2,1)}, bf16[2,272,512]{2,1,0:T(8,128)(2,1)}, bf16[2,272,512]{2,1,0:T(8,128)(2,1)}, b...) custom-call(s32[1,1,2]{2,1,0:T(1,128)} %bitcast.45, f32[1]{0:T(128)S(6)} %copy.20.dt_bias, f32[1]{0:T(128)S(6)} %copy.21.a_log, ...), custom_call_target="tpu_custom_call" | custom-call | tf_op jit(solution)/shard_map/enter/pallas_call | solution.py:338
  19.4 3.0 %collective-permute-start.2 = (bf16[2,256,256]{2,1,0:T(8,128)(2,1)}, bf16[2,256,256]{2,1,0:T(8,128)(2,1)S(1)}, u32[]{:S(2)}, u32[]{:S(2)}) collective-permute-start(bf16[2,256,256]{2,1,0:T(8,128)(2,1)} %get-tuple-element.43), channel_id=1, source_target_pairs={{0,1},{1,0},{2,3},{3,2},{4,5},{5,4},{6,7},{7,6},{8,9},{9,8},{10,11... | collective-permute-start | bytes 786440 | tf_op jit(solution)/shard_map/ppermute | solution.py:21
  22.4 6.0 %gates.1 = (bf16[2,256,512]{2,1,0:T(8,128)(2,1)}, bf16[2,256,512]{2,1,0:T(8,128)(2,1)}) custom-call(bf16[1024,2048]{1,0:T(8,128)(2,1)} %get-tuple-element.46.rows_hbm, bf16[2048,1024]{1,0:T(8,128)(2,1)} %xz.3), custom_call_target="tpu_custom_call" | custom-call | tf_op jit(solution)/shard_map/gates/pallas_call | solution.py:412
  29.4 1.8 %collective-permute-start.3 = (bf16[2,272,512]{2,1,0:T(8,128)(2,1)}, bf16[2,272,512]{2,1,0:T(8,128)(2,1)}, u32[]{:S(2)}, u32[]{:S(2)}) collective-permute-start(bf16[2,272,512]{2,1,0:T(8,128)(2,1)} %get-tuple-element.49), channel_id=1, source_target_pairs={{0,1},{1,0},{2,3},{3,2},{4,5},{5,4},{6,7},{7,6},{8,9},{9,8},{10,11... | collective-permute-start | bytes 1671176 | tf_op jit(solution)/shard_map/ppermute | solution.py:21
  31.2 2.5 %broadcast_select_fusion.2 = (bf16[256,2048]{1,0:T(8,128)(2,1)S(1)}, bf16[256,2048]{1,0:T(8,128)(2,1)}) fusion(pred[]{:T(512)S(6)} %eq.18, bf16[512,2048]{1,0:T(8,128)(2,1)} %get-tuple-element.56, bf16[1,512,2048]{2,1,0:T(8,128)(2,1)S(1)} %copy-done.1, bf16[2048]{0:T(1024)(128)(2,1)S(1)} %copy-done.17, pred[256]{0:T(512)(128)(4,1)S(1)} %iota_compare_fusion.2), kind=kLoop, calls=%fused_computation.14 | loop fusion | flops 1572864 | bytes 4198657 | tf_op jit(solution)/shard_map/jit(_where)/select_n | solution.py:631
  33.7 2.6 %collective-permute-start.4 = (bf16[256,256]{1,0:T(8,128)(2,1)S(1)}, bf16[256,256]{1,0:T(8,128)(2,1)S(1)}, u32[]{:S(2)}, u32[]{:S(2)}) collective-permute-start(bf16[256,256]{1,0:T(8,128)(2,1)S(1)} %get-tuple-element.51), channel_id=1, source_target_pairs={{0,2},{1,3},{2,0},{3,1},{4,6},{5,7},{6,4},{7,5},{8,10},{9,11},{10,... | collective-permute-start | bytes 393224 | tf_op jit(solution)/shard_map/ppermute | solution.py:21
  36.3 11.2 %collective-permute-done.3 = bf16[2,272,512]{2,1,0:T(8,128)(2,1)} collective-permute-done((bf16[2,272,512]{2,1,0:T(8,128)(2,1)}, bf16[2,272,512]{2,1,0:T(8,128)(2,1)}, u32[]{:S(2)}, u32[]{:S(2)}) %collective-permute-start.3) | collective-permute-done | bytes 557088 | tf_op jit(solution)/shard_map/ppermute | solution.py:21
  47.5 1.2 %convert_add_fusion = bf16[2,272,512]{2,1,0:T(8,128)(2,1)S(1)} fusion(bf16[2,272,512]{2,1,0:T(8,128)(2,1)} %collective-permute-done.3, bf16[2,272,512]{2,1,0:T(8,128)(2,1)S(1)} %copy-done.10), kind=kLoop, calls=%fused_computation.9 | loop fusion | flops 1114112 | bytes 1671168 | tf_op jit(solution)/shard_map/add | solution.py:608
  48.8 1.9 %collective-permute-start.5 = (bf16[272,512]{1,0:T(8,128)(2,1)S(1)}, bf16[272,512]{1,0:T(8,128)(2,1)S(1)}, u32[]{:S(2)}, u32[]{:S(2)}) collective-permute-start(bf16[272,512]{1,0:T(8,128)(2,1)S(1)} %get-tuple-element.53), channel_id=1, source_target_pairs={{0,2},{1,3},{2,0},{3,1},{4,6},{5,7},{6,4},{7,5},{8,10},{9,11},{10,... | collective-permute-start | bytes 835592 | tf_op jit(solution)/shard_map/ppermute | solution.py:21
  50.7 2.5 %collective-permute-start.8 = (bf16[2,256,512]{2,1,0:T(8,128)(2,1)}, bf16[2,256,512]{2,1,0:T(8,128)(2,1)}, u32[]{:S(2)}, u32[]{:S(2)}) collective-permute-start(bf16[2,256,512]{2,1,0:T(8,128)(2,1)} %get-tuple-element.65), channel_id=1, source_target_pairs={{0,1},{1,0},{2,3},{3,2},{4,5},{5,4},{6,7},{7,6},{8,9},{9,8},{10,11... | collective-permute-start | bytes 1572872 | tf_op jit(solution)/shard_map/ppermute | solution.py:21
  53.3 3.2 %broadcast_select_fusion = (bf16[512,2048]{1,0:T(8,128)(2,1)S(1)}, bf16[512,2048]{1,0:T(8,128)(2,1)}) fusion(bf16[512,2048]{1,0:T(8,128)(2,1)} %collective-permute-done.6, bf16[512,2048]{1,0:T(8,128)(2,1)S(1)} %copy-done.5, pred[]{:T(512)S(6)} %lt.13), kind=kLoop, calls=%fused_computation.7 | loop fusion | flops 2097152 | bytes 8388609 | tf_op jit(solution)/shard_map/jit(_where)/select_n | solution.py:626
  56.4 7.6 %collective-permute-done.5.refs_1_ = bf16[272,512]{1,0:T(8,128)(2,1)S(1)} collective-permute-done((bf16[272,512]{1,0:T(8,128)(2,1)S(1)}, bf16[272,512]{1,0:T(8,128)(2,1)S(1)}, u32[]{:S(2)}, u32[]{:S(2)}) %collective-permute-start.5) | collective-permute-done | bytes 278560 | tf_op jit(solution)/shard_map/ppermute | solution.py:21
  64.1 2.0 %collective-permute-start.7 = (bf16[16,768]{1,0:T(8,128)(2,1)S(1)}, bf16[16,768]{1,0:T(8,128)(2,1)S(1)}, u32[]{:S(2)}, u32[]{:S(2)}) collective-permute-start(bf16[16,768]{1,0:T(8,128)(2,1)S(1)} %fusion.16), channel_id=1, source_target_pairs={{0,1},{2,3},{8,9},{10,11},{16,17},{18,19},{24,25},{26,27},{1,8},{3... | collective-permute-start | bytes 73736 | tf_op jit(solution)/shard_map/ppermute | solution.py:641
  66.1 2.2 %collective-permute-done.7.refs_4_ = bf16[16,768]{1,0:T(8,128)(2,1)S(1)} collective-permute-done((bf16[16,768]{1,0:T(8,128)(2,1)S(1)}, bf16[16,768]{1,0:T(8,128)(2,1)S(1)}, u32[]{:S(2)}, u32[]{:S(2)}) %collective-permute-start.7) | collective-permute-done | bytes 24608 | tf_op jit(solution)/shard_map/ppermute | solution.py:641
  68.9 3.6 %scan.1 = (bf16[256,512]{1,0:T(8,128)(2,1)}, bf16[256,256]{1,0:T(8,128)(2,1)}, f32[16,256]{1,0:T(8,128)}, f32[256,32]{1,0:T(8,128)}, bf16[144,512]{1,0:T(8,128)(2,1)}, /*index=5*/f32[8,512]{1,0:T(8,128)}) custom-call(bf16[272,512]{1,0:T(8,128)(2,1)} %copy-done.7, bf16[272,512]{1,0:T(8,128)(2,1)} %copy-done.12, bf16[256,256]{1,0:T(8,128)(2,1)} %copy-done.11, ...), custom_call_target="tpu_custom_call" | custom-call | tf_op jit(solution)/shard_map/scan/pallas_call | solution.py:497
  72.5 2.5 %collective-permute-start.10 = (bf16[144,512]{1,0:T(8,128)(2,1)}, bf16[144,512]{1,0:T(8,128)(2,1)S(1)}, u32[]{:S(2)}, u32[]{:S(2)}) collective-permute-start(bf16[144,512]{1,0:T(8,128)(2,1)} %get-tuple-element.66), channel_id=1, source_target_pairs={{0,1},{1,0},{2,3},{3,2},{4,5},{5,4},{6,7},{7,6},{8,9},{9,8},{10,11... | collective-permute-start | bytes 442376 | tf_op jit(solution)/shard_map/ppermute | solution.py:21
  75.0 1.3 %convert_add_fusion.1 = bf16[2,256,512]{2,1,0:T(8,128)(2,1)S(1)} fusion(bf16[2,256,512]{2,1,0:T(8,128)(2,1)} %collective-permute-done.8, bf16[2,256,512]{2,1,0:T(8,128)(2,1)} %get-tuple-element.64), kind=kLoop, calls=%fused_computation.13 | loop fusion | flops 1048576 | bytes 1572864 | tf_op jit(solution)/shard_map/add | solution.py:608
  76.3 0.8 fusion.12
  77.2 2.7 %collective-permute-start.9 = (bf16[256,512]{1,0:T(8,128)(2,1)}, bf16[256,512]{1,0:T(8,128)(2,1)}, u32[]{:S(2)}, u32[]{:S(2)}) collective-permute-start(bf16[256,512]{1,0:T(8,128)(2,1)} %get-tuple-element.83), channel_id=1, source_target_pairs={{0,2},{1,3},{2,0},{3,1},{4,6},{5,7},{6,4},{7,5},{8,10},{9,11},{10,... | collective-permute-start | bytes 786440 | tf_op jit(solution)/shard_map/ppermute | solution.py:21
  79.9 2.4 %inside.1.local = f32[256,512]{1,0:T(8,128)} custom-call(bf16[256,512]{1,0:T(8,128)(2,1)} %get-tuple-element.67.streams, bf16[256,256]{1,0:T(8,128)(2,1)} %get-tuple-element.68.maps, f32[16,256]{1,0:T(8,128)} %get-tuple-element.69.meta, f32[256,32]{1,0:T(8,128)} %get-tuple-element.70.cols, f32[8,512]{1,0:T(8,128)} %get-tuple-element.71.params), custom_call_target="tpu_custom_call" | custom-call | tf_op jit(solution)/shard_map/inside/pallas_call | solution.py:540
  82.4 1.5 %collective-permute-start.11 = (bf16[144,512]{1,0:T(8,128)(2,1)S(1)}, bf16[144,512]{1,0:T(8,128)(2,1)S(1)}, u32[]{:S(2)}, u32[]{:S(2)}) collective-permute-start(bf16[144,512]{1,0:T(8,128)(2,1)S(1)} %fusion.7), channel_id=1, source_target_pairs={{0,8},{8,0},{16,24},{24,16},{1,9},{9,1},{17,25},{25,17},{2,10},{10... | collective-permute-start | bytes 442376 | tf_op jit(solution)/shard_map/ppermute | solution.py:21
  84.0 1.5 %collective-permute-start.12 = (bf16[144,512]{1,0:T(8,128)(2,1)S(1)}, bf16[144,512]{1,0:T(8,128)(2,1)}, u32[]{:S(2)}, u32[]{:S(2)}) collective-permute-start(bf16[144,512]{1,0:T(8,128)(2,1)S(1)} %fusion.7), channel_id=1, source_target_pairs={{0,16},{8,24},{16,0},{24,8},{1,17},{9,25},{17,1},{25,9},{2,18},{10... | collective-permute-start | bytes 442376 | tf_op jit(solution)/shard_map/ppermute | solution.py:21
  86.0 5.1 %collective-permute-done.9.received = bf16[256,512]{1,0:T(8,128)(2,1)} collective-permute-done((bf16[256,512]{1,0:T(8,128)(2,1)}, bf16[256,512]{1,0:T(8,128)(2,1)}, u32[]{:S(2)}, u32[]{:S(2)}) %collective-permute-start.9) | collective-permute-done | bytes 262176 | tf_op jit(solution)/shard_map/ppermute | solution.py:21
  91.1 0.9 collective-permute-done.13.others_and_out_2_
  92.0 3.0 %gate.1 = bf16[256,512]{1,0:T(8,128)(2,1)} custom-call(bf16[256,512]{1,0:T(8,128)(2,1)} %get-tuple-element.84.kept, bf16[256,512]{1,0:T(8,128)(2,1)} %collective-permute-done.9.received, f32[256,512]{1,0:T(8,128)} %inside.1.local, bf16[256,256]{1,0:T(8,128)(2,1)} %get-tuple-element.68.maps, f32[256,32]{1,0:T(8,128)} %get-tuple-element.70.cols, ...), custom_call_target="tpu_custom_call" | custom-call | tf_op jit(solution)/shard_map/gate/pallas_call | solution.py:581
  95.2 1.6 %collective-permute-start.14 = (bf16[256,512]{1,0:T(8,128)(2,1)}, bf16[256,512]{1,0:T(8,128)(2,1)S(1)}, u32[]{:S(2)}, u32[]{:S(2)}) collective-permute-start(bf16[256,512]{1,0:T(8,128)(2,1)} %gate.1), channel_id=1, source_target_pairs={{0,0},{1,1},{2,6},{3,7},{4,4},{5,5},{6,2},{7,3},{8,8},{9,9},{10,14... | collective-permute-start | bytes 786440 | tf_op jit(solution)/shard_map/ppermute | solution.py:655
  96.8 2.7 %collective-permute-start.16 = (bf16[256,512]{1,0:T(8,128)(2,1)}, bf16[256,512]{1,0:T(8,128)(2,1)S(1)}, u32[]{:S(2)}, u32[]{:S(2)}) collective-permute-start(bf16[256,512]{1,0:T(8,128)(2,1)} %gate.1), channel_id=1, source_target_pairs={{0,1},{1,0},{2,7},{3,6},{4,5},{5,4},{6,3},{7,2},{8,9},{9,8},{10,15... | collective-permute-start | bytes 786440 | tf_op jit(solution)/shard_map/ppermute | solution.py:655
  99.5 9.9 %collective-permute-done.15 = bf16[256,512]{1,0:T(8,128)(2,1)S(1)} collective-permute-done((bf16[256,512]{1,0:T(8,128)(2,1)}, bf16[256,512]{1,0:T(8,128)(2,1)S(1)}, u32[]{:S(2)}, u32[]{:S(2)}) %collective-permute-start.15) | collective-permute-done | bytes 262176 | tf_op jit(solution)/shard_map/ppermute | solution.py:655
  110.6 1.2 copy-done
  113.8 3.0 %collective-permute-done.17 = bf16[256,512]{1,0:T(8,128)(2,1)S(1)} collective-permute-done((bf16[256,512]{1,0:T(8,128)(2,1)S(1)}, bf16[256,512]{1,0:T(8,128)(2,1)S(1)}, u32[]{:S(2)}, u32[]{:S(2)}) %collective-permute-start.17) | collective-permute-done | bytes 262176 | tf_op jit(solution)/shard_map/ppermute | solution.py:21
  116.8 1.8 %fusion.3 = bf16[1,512,2048]{2,1,0:T(8,128)(2,1)} fusion(bf16[1,512,2048]{2,1,0:T(8,128)(2,1)} %copy-done.4, s32[]{:T(128)S(6)} %select_n.126, f32[256,2048]{1,0:T(8,128)S(1)} %fusion.18, bf16[256,512]{1,0:T(8,128)(2,1)S(1)} %collective-permute-done.17, bf16[512,2048]{1,0:T(8,128)(2,1)S(1)} %get-tuple-element.75, bf16[256,2048]{1,0:T(8,128)(2,1)S(1)} %get-tuple-element.76), kind=kOutput, calls=%fused_computation.5 | convolution fusion | flops 538968064 | bytes 6553604 | tf_op jit(solution)/shard_map/dot_general | solution.py:664
  (66 shorter events, 7.8 us)
Async XLA Ops:
  0.0 5.4 %collective-permute-start.1 = (bf16[512,2048]{1,0:T(8,128)(2,1)}, bf16[512,2048]{1,0:T(8,128)(2,1)S(1)}, u32[]{:S(2)}, u32[]{:S(2)}) collective-permute-start(bf16[512,2048]{1,0:T(8,128)(2,1)} %bitcast.39), channel_id=1, source_target_pairs={{0,4},{4,0},{1,5},{5,1},{2,6},{6,2},{3,7},{7,3},{8,12},{12,8},{9,1... | collective-permute-start | bytes 6291464 | tf_op jit(solution)/shard_map/ppermute | solution.py:21
  0.5 4.9 %collective-permute-start = (bf16[256,1280]{1,0:T(8,128)(2,1)}, bf16[256,1280]{1,0:T(8,128)(2,1)S(1)}, u32[]{:S(2)}, u32[]{:S(2)}) collective-permute-start(bf16[256,1280]{1,0:T(8,128)(2,1)} %bitcast.41), channel_id=1, source_target_pairs={{0,4},{4,0},{1,5},{5,1},{2,6},{6,2},{3,7},{7,3},{8,12},{12,8},{9,1... | collective-permute-start | bytes 1966088 | tf_op jit(solution)/shard_map/ppermute | solution.py:21
  5.4 1.5 %copy-start.3 = (bf16[512,2048]{1,0:T(8,128)(2,1)}, bf16[512,2048]{1,0:T(8,128)(2,1)S(1)}, u32[]{:S(2)}) copy-start(bf16[512,2048]{1,0:T(8,128)(2,1)S(1)} %collective-permute-done.1.text_other) | copy-start | bytes 6291460
  19.4 9.8 %collective-permute-start.2 = (bf16[2,256,256]{2,1,0:T(8,128)(2,1)}, bf16[2,256,256]{2,1,0:T(8,128)(2,1)S(1)}, u32[]{:S(2)}, u32[]{:S(2)}) collective-permute-start(bf16[2,256,256]{2,1,0:T(8,128)(2,1)} %get-tuple-element.43), channel_id=1, source_target_pairs={{0,1},{1,0},{2,3},{3,2},{4,5},{5,4},{6,7},{7,6},{8,9},{9,8},{10,11... | collective-permute-start | bytes 786440 | tf_op jit(solution)/shard_map/ppermute | solution.py:21
  22.4 6.8 %copy-start.13 = (bf16[2,256,256]{2,1,0:T(8,128)(2,1)S(1)}, bf16[2,256,256]{2,1,0:T(8,128)(2,1)}, u32[]{:S(2)}) copy-start(bf16[2,256,256]{2,1,0:T(8,128)(2,1)} %get-tuple-element.42) | copy-start | bytes 786436
  22.4 8.8 %copy-start.1 = (bf16[1,512,2048]{2,1,0:T(8,128)(2,1)S(1)}, bf16[1,512,2048]{2,1,0:T(8,128)(2,1)}, u32[]{:S(2)}) copy-start(bf16[1,512,2048]{2,1,0:T(8,128)(2,1)} %param.17) | copy-start | bytes 6291460
  22.4 8.8 %copy-start.17 = (bf16[2048]{0:T(1024)(128)(2,1)S(1)}, bf16[2048]{0:T(1024)(128)(2,1)}, u32[]{:S(2)}) copy-start(bf16[2048]{0:T(1024)(128)(2,1)} %newline.1) | copy-start | bytes 12292
  29.3 23.9 %copy-start.11 = (bf16[256,256]{1,0:T(8,128)(2,1)}, bf16[256,256]{1,0:T(8,128)(2,1)S(1)}, u32[]{:S(2)}) copy-start(bf16[256,256]{1,0:T(8,128)(2,1)S(1)} %get-tuple-element.60.refs_2_) | copy-start | bytes 393220
  29.3 23.9 %collective-permute-start.6 = (bf16[512,2048]{1,0:T(8,128)(2,1)}, bf16[512,2048]{1,0:T(8,128)(2,1)}, u32[]{:S(2)}, u32[]{:S(2)}) collective-permute-start(bf16[512,2048]{1,0:T(8,128)(2,1)} %param.33), channel_id=1, source_target_pairs={{0,4},{4,0},{1,5},{5,1},{2,6},{6,2},{3,7},{7,3},{8,12},{12,8},{9,1... | collective-permute-start | bytes 6291464 | tf_op jit(solution)/shard_map/ppermute | solution.py:21
  29.4 18.2 %collective-permute-start.3 = (bf16[2,272,512]{2,1,0:T(8,128)(2,1)}, bf16[2,272,512]{2,1,0:T(8,128)(2,1)}, u32[]{:S(2)}, u32[]{:S(2)}) collective-permute-start(bf16[2,272,512]{2,1,0:T(8,128)(2,1)} %get-tuple-element.49), channel_id=1, source_target_pairs={{0,1},{1,0},{2,3},{3,2},{4,5},{5,4},{6,7},{7,6},{8,9},{9,8},{10,11... | collective-permute-start | bytes 1671176 | tf_op jit(solution)/shard_map/ppermute | solution.py:21
  31.2 16.3 %copy-start.10 = (bf16[2,272,512]{2,1,0:T(8,128)(2,1)S(1)}, bf16[2,272,512]{2,1,0:T(8,128)(2,1)}, u32[]{:S(2)}) copy-start(bf16[2,272,512]{2,1,0:T(8,128)(2,1)} %get-tuple-element.41) | copy-start | bytes 1671172
  33.7 19.5 %copy-start.5 = (bf16[512,2048]{1,0:T(8,128)(2,1)S(1)}, bf16[512,2048]{1,0:T(8,128)(2,1)}, u32[]{:S(2)}) copy-start(bf16[512,2048]{1,0:T(8,128)(2,1)} %param.33) | copy-start | bytes 6291460
  33.7 15.1 %collective-permute-start.4 = (bf16[256,256]{1,0:T(8,128)(2,1)S(1)}, bf16[256,256]{1,0:T(8,128)(2,1)S(1)}, u32[]{:S(2)}, u32[]{:S(2)}) collective-permute-start(bf16[256,256]{1,0:T(8,128)(2,1)S(1)} %get-tuple-element.51), channel_id=1, source_target_pairs={{0,2},{1,3},{2,0},{3,1},{4,6},{5,7},{6,4},{7,5},{8,10},{9,11},{10,... | collective-permute-start | bytes 393224 | tf_op jit(solution)/shard_map/ppermute | solution.py:21
  48.8 15.3 %copy-start.7 = (bf16[272,512]{1,0:T(8,128)(2,1)}, bf16[272,512]{1,0:T(8,128)(2,1)S(1)}, u32[]{:S(2)}) copy-start(bf16[272,512]{1,0:T(8,128)(2,1)S(1)} %get-tuple-element.58.refs_0_) | copy-start | bytes 835588
  48.8 7.6 %copy-start.15 = (bf16[256,256]{1,0:T(8,128)(2,1)}, bf16[256,256]{1,0:T(8,128)(2,1)S(1)}, u32[]{:S(2)}) copy-start(bf16[256,256]{1,0:T(8,128)(2,1)S(1)} %collective-permute-done.4.refs_3_) | copy-start | bytes 393220
  48.8 15.3 %collective-permute-start.5 = (bf16[272,512]{1,0:T(8,128)(2,1)S(1)}, bf16[272,512]{1,0:T(8,128)(2,1)S(1)}, u32[]{:S(2)}, u32[]{:S(2)}) collective-permute-start(bf16[272,512]{1,0:T(8,128)(2,1)S(1)} %get-tuple-element.53), channel_id=1, source_target_pairs={{0,2},{1,3},{2,0},{3,1},{4,6},{5,7},{6,4},{7,5},{8,10},{9,11},{10,... | collective-permute-start | bytes 835592 | tf_op jit(solution)/shard_map/ppermute | solution.py:21
  50.7 24.2 %collective-permute-start.8 = (bf16[2,256,512]{2,1,0:T(8,128)(2,1)}, bf16[2,256,512]{2,1,0:T(8,128)(2,1)}, u32[]{:S(2)}, u32[]{:S(2)}) collective-permute-start(bf16[2,256,512]{2,1,0:T(8,128)(2,1)} %get-tuple-element.65), channel_id=1, source_target_pairs={{0,1},{1,0},{2,3},{3,2},{4,5},{5,4},{6,7},{7,6},{8,9},{9,8},{10,11... | collective-permute-start | bytes 1572872 | tf_op jit(solution)/shard_map/ppermute | solution.py:21
  64.1 4.2 %copy-start.12 = (bf16[272,512]{1,0:T(8,128)(2,1)}, bf16[272,512]{1,0:T(8,128)(2,1)S(1)}, u32[]{:S(2)}) copy-start(bf16[272,512]{1,0:T(8,128)(2,1)S(1)} %collective-permute-done.5.refs_1_) | copy-start | bytes 835588
  64.1 4.2 %collective-permute-start.7 = (bf16[16,768]{1,0:T(8,128)(2,1)S(1)}, bf16[16,768]{1,0:T(8,128)(2,1)S(1)}, u32[]{:S(2)}, u32[]{:S(2)}) collective-permute-start(bf16[16,768]{1,0:T(8,128)(2,1)S(1)} %fusion.16), channel_id=1, source_target_pairs={{0,1},{2,3},{8,9},{10,11},{16,17},{18,19},{24,25},{26,27},{1,8},{3... | collective-permute-start | bytes 73736 | tf_op jit(solution)/shard_map/ppermute | solution.py:641
  72.5 9.8 %copy-start.9 = (bf16[144,512]{1,0:T(8,128)(2,1)S(1)}, bf16[144,512]{1,0:T(8,128)(2,1)}, u32[]{:S(2)}) copy-start(bf16[144,512]{1,0:T(8,128)(2,1)} %get-tuple-element.66) | copy-start | bytes 442372
  72.5 9.8 %collective-permute-start.10 = (bf16[144,512]{1,0:T(8,128)(2,1)}, bf16[144,512]{1,0:T(8,128)(2,1)S(1)}, u32[]{:S(2)}, u32[]{:S(2)}) collective-permute-start(bf16[144,512]{1,0:T(8,128)(2,1)} %get-tuple-element.66), channel_id=1, source_target_pairs={{0,1},{1,0},{2,3},{3,2},{4,5},{5,4},{6,7},{7,6},{8,9},{9,8},{10,11... | collective-permute-start | bytes 442376 | tf_op jit(solution)/shard_map/ppermute | solution.py:21
  77.2 13.9 %collective-permute-start.9 = (bf16[256,512]{1,0:T(8,128)(2,1)}, bf16[256,512]{1,0:T(8,128)(2,1)}, u32[]{:S(2)}, u32[]{:S(2)}) collective-permute-start(bf16[256,512]{1,0:T(8,128)(2,1)} %get-tuple-element.83), channel_id=1, source_target_pairs={{0,2},{1,3},{2,0},{3,1},{4,6},{5,7},{6,4},{7,5},{8,10},{9,11},{10,... | collective-permute-start | bytes 786440 | tf_op jit(solution)/shard_map/ppermute | solution.py:21
  82.3 9.7 %copy-start.6 = (bf16[144,512]{1,0:T(8,128)(2,1)}, bf16[144,512]{1,0:T(8,128)(2,1)S(1)}, u32[]{:S(2)}) copy-start(bf16[144,512]{1,0:T(8,128)(2,1)S(1)} %collective-permute-done.10.partner) | copy-start | bytes 442372
  82.4 8.6 %collective-permute-start.11 = (bf16[144,512]{1,0:T(8,128)(2,1)S(1)}, bf16[144,512]{1,0:T(8,128)(2,1)S(1)}, u32[]{:S(2)}, u32[]{:S(2)}) collective-permute-start(bf16[144,512]{1,0:T(8,128)(2,1)S(1)} %fusion.7), channel_id=1, source_target_pairs={{0,8},{8,0},{16,24},{24,16},{1,9},{9,1},{17,25},{25,17},{2,10},{10... | collective-permute-start | bytes 442376 | tf_op jit(solution)/shard_map/ppermute | solution.py:21
  84.0 7.1 %collective-permute-start.12 = (bf16[144,512]{1,0:T(8,128)(2,1)S(1)}, bf16[144,512]{1,0:T(8,128)(2,1)}, u32[]{:S(2)}, u32[]{:S(2)}) collective-permute-start(bf16[144,512]{1,0:T(8,128)(2,1)S(1)} %fusion.7), channel_id=1, source_target_pairs={{0,16},{8,24},{16,0},{24,8},{1,17},{9,25},{17,1},{25,9},{2,18},{10... | collective-permute-start | bytes 442376 | tf_op jit(solution)/shard_map/ppermute | solution.py:21
  85.5 6.5 %collective-permute-start.13 = (bf16[144,512]{1,0:T(8,128)(2,1)S(1)}, bf16[144,512]{1,0:T(8,128)(2,1)}, u32[]{:S(2)}, u32[]{:S(2)}) collective-permute-start(bf16[144,512]{1,0:T(8,128)(2,1)S(1)} %fusion.7), channel_id=1, source_target_pairs={{0,24},{8,16},{16,8},{24,0},{1,25},{9,17},{17,9},{25,1},{2,26},{10... | collective-permute-start | bytes 442376 | tf_op jit(solution)/shard_map/ppermute | solution.py:21
  95.0 14.4 %collective-permute-start.15 = (bf16[256,512]{1,0:T(8,128)(2,1)}, bf16[256,512]{1,0:T(8,128)(2,1)S(1)}, u32[]{:S(2)}, u32[]{:S(2)}) collective-permute-start(bf16[256,512]{1,0:T(8,128)(2,1)} %gate.1), channel_id=1, source_target_pairs={{0,2},{1,3},{2,4},{3,5},{4,6},{5,7},{6,0},{7,1},{8,10},{9,11},{10,... | collective-permute-start | bytes 786440 | tf_op jit(solution)/shard_map/ppermute | solution.py:655
  95.2 14.9 %collective-permute-start.14 = (bf16[256,512]{1,0:T(8,128)(2,1)}, bf16[256,512]{1,0:T(8,128)(2,1)S(1)}, u32[]{:S(2)}, u32[]{:S(2)}) collective-permute-start(bf16[256,512]{1,0:T(8,128)(2,1)} %gate.1), channel_id=1, source_target_pairs={{0,0},{1,1},{2,6},{3,7},{4,4},{5,5},{6,2},{7,3},{8,8},{9,9},{10,14... | collective-permute-start | bytes 786440 | tf_op jit(solution)/shard_map/ppermute | solution.py:655
  96.8 15.7 %collective-permute-start.16 = (bf16[256,512]{1,0:T(8,128)(2,1)}, bf16[256,512]{1,0:T(8,128)(2,1)S(1)}, u32[]{:S(2)}, u32[]{:S(2)}) collective-permute-start(bf16[256,512]{1,0:T(8,128)(2,1)} %gate.1), channel_id=1, source_target_pairs={{0,1},{1,0},{2,7},{3,6},{4,5},{5,4},{6,3},{7,2},{8,9},{9,8},{10,15... | collective-permute-start | bytes 786440 | tf_op jit(solution)/shard_map/ppermute | solution.py:655
  109.4 7.4 %collective-permute-start.17 = (bf16[256,512]{1,0:T(8,128)(2,1)S(1)}, bf16[256,512]{1,0:T(8,128)(2,1)S(1)}, u32[]{:S(2)}, u32[]{:S(2)}) collective-permute-start(bf16[256,512]{1,0:T(8,128)(2,1)S(1)} %collective-permute-done.15), channel_id=1, source_target_pairs={{0,1},{1,0},{2,3},{3,2},{4,5},{5,4},{6,7},{7,6},{8,9},{9,8},{10,11... | collective-permute-start | bytes 786440 | tf_op jit(solution)/shard_map/ppermute | solution.py:21
  110.1 1.7 %copy-start = (bf16[512,2048]{1,0:T(8,128)(2,1)S(1)}, bf16[512,2048]{1,0:T(8,128)(2,1)}, u32[]{:S(2)}) copy-start(bf16[512,2048]{1,0:T(8,128)(2,1)} %get-tuple-element.74) | copy-start | bytes 6291460
  112.5 1.3 %copy-start.4 = (bf16[1,512,2048]{2,1,0:T(8,128)(2,1)}, bf16[1,512,2048]{2,1,0:T(8,128)(2,1)S(1)}, u32[]{:S(2)}) copy-start(bf16[1,512,2048]{2,1,0:T(8,128)(2,1)S(1)} %fusion.5) | copy-start | bytes 6291460
  (4 other events, 3.6 us)

commit v7 on v6

--- a/solution.py
+++ b/solution.py
@@ -222,7 +222,7 @@
     ]
     load_tails = [
         pltpu.make_async_copy(text.at[pl.ds(half, half), :], tails.at[0], sems.at[2 + tiles]),
-        pltpu.make_async_copy(text_other.at[pl.ds(half, half), :], tails.at[1], sems.at[3 + tiles]),
+        pltpu.make_async_copy(text_other, tails.at[1], sems.at[3 + tiles]),
     ]
     load_weights = [
         pltpu.make_async_copy(
@@ -595,7 +595,7 @@
     width = columns * lax.axis_size("tensor")
     feats = crop_feats[0, 0, 0]
     feats_other = swapped(feats, "dp", 1)
-    text_other = swapped(text, "dp", 1)
+    text_other = swapped(text[half:], "dp", 1)
     crops, rows, keep_x, send_x, keep, send = enter(
         crop_dest.transpose(0, 2, 1), dt_bias, a_log, skip, feats, feats_other, vision_gain,
         proj_weight, text, text_other, newline, norm_gain, xz_weight, bc_weight, dt_weight.T,
@@ -611,13 +611,11 @@
 
     keep_gates, send_gates = gates(rows, xz_weight)
     leaves, kept = added(keep, swapped(send, "tensor", 1))
-    leaves, kept, send_x, send_gates, out_weight = lax.optimization_barrier(
-        (leaves, kept, send_x, send_gates, out_weight)
-    )
+    leaves, kept, send_gates = lax.optimization_barrier((leaves, kept, send_gates))
     received = swapped(leaves, "tensor", 2)
     leaves_x, kept_x = added(keep_x, swapped(send_x, "tensor", 1))
-    leaves_x, kept_x, send_gates, received = lax.optimization_barrier(
-        (leaves_x, kept_x, send_gates, received)
+    leaves_x, kept_x, send_gates, received, out_weight, newline = lax.optimization_barrier(
+        (leaves_x, kept_x, send_gates, received, out_weight, newline)
     )
     received_x = swapped(leaves_x, "tensor", 2)
     arrived_gates = swapped(send_gates, "tensor", 1)

time: 119 us -> 118 us (level)
  waiting for transfers between devices: 43.7 us -> 39.1 us
  local copies, waits for them, and re-layouts: 4.43 us -> 6.87 us
  other arithmetic: 9.35 us -> 11.1 us
    ppermute x14, waiting for transfers between devices: 31.6 us -> 27.2 us  [swapped(): lax.ppermute(block, axis, [(i, i ^ bits) for i in range(lax.axis_size(axi...]
    slice x0 -> x1, local copies, waits for them, and re-layouts: none -> 1.36 us  [per_device_halves(): text_other = swapped(text[half:], 'dp', 1)]
    unnamed x36 -> x38, local copies, waits for them, and re-layouts: 4.18 us -> 5.27 us
  transfers between devices with their start and end apart: 18 -> 18, of which waited for: 9 -> 9; matrix products, arithmetic and copies ran while one was open for 10% -> 11% of each run, Pallas kernels for 10% -> 10%
where the time goes in v7:
time: 118 us; the launch traced here: 117 us
  waiting for transfers between devices  39.1 us (33%)
  Pallas kernels  27.4 us (23%)
  starting transfers between devices  26.9 us (23%)
  other arithmetic  11.1 us (9%)
  local copies, waits for them, and re-layouts  6.87 us (6%)
  matrix products  3.93 us (3%)
  between operations  2.18 us (2%)
    ppermute x14, waiting for transfers between devices, swapped(): lax.ppermute(block, axis, [(i, i ^ bits) for i in range(lax.axis_size(axi...  27.2 us
    ppermute x14, starting transfers between devices, swapped(): lax.ppermute(block, axis, [(i, i ^ bits) for i in range(lax.axis_size(axi...  20.4 us
    pallas_call x1, Pallas kernels, enter(): pl.pallas_call(enter_body, in_specs=[pl.BlockSpec(memory_space=pltpu.SMEM...  12.4 us
    ppermute x3, waiting for transfers between devices, per_device_halves(): lax.ppermute(normed, ('dp', 'tensor'), [(i, (i if i % 4 < 2 else i ^ 4) ^...  10.4 us
    pallas_call x1, Pallas kernels, gates(): pl.pallas_call(gates_body, in_specs=[whole, whole], out_specs=[whole, who...  5.93 us
    unnamed x38, local copies, waits for them, and re-layouts  5.27 us
    ppermute x3, starting transfers between devices, per_device_halves(): lax.ppermute(normed, ('dp', 'tensor'), [(i, (i if i % 4 < 2 else i ^ 4) ^...  4.48 us
    pallas_call x1, Pallas kernels, scan(): pl.pallas_call(lambda *refs: scan_body(width, *refs), out_shape=[jax.Shap...  3.61 us
  transfers between devices with their start and end apart: 18, of which 9 were waited for; matrix products, arithmetic and copies ran while one was open for 11% of the time, Pallas kernels for 10%

profile of v7, /device:TPU:0, one launch (start us, length us, event | category | flops | bytes accessed | tf_op | source)
XLA Modules:
  0.0 117.4 jit_solution(7299220350565140028)
XLA Ops:
  0.0 1.4 %slice_bitcast_fusion = bf16[256,2048]{1,0:T(8,128)(2,1)S(1)} fusion(bf16[1,512,2048]{2,1,0:T(8,128)(2,1)} %param.17), kind=kLoop, calls=%fused_computation.13 | loop fusion | bytes 2097152 | tf_op jit(solution)/shard_map/slice | solution.py:598
  3.9 1.2 %collective-permute-done.feats_other = bf16[256,1280]{1,0:T(8,128)(2,1)S(1)} collective-permute-done((bf16[256,1280]{1,0:T(8,128)(2,1)S(1)}, bf16[256,1280]{1,0:T(8,128)(2,1)S(1)}, u32[]{:S(2)}, u32[]{:S(2)}) %collective-permute-start) | collective-permute-done | bytes 655392 | tf_op jit(solution)/shard_map/ppermute | solution.py:21
  6.3 12.4 %enter.1 = (bf16[512,2048]{1,0:T(8,128)(2,1)}, bf16[1024,2048]{1,0:T(8,128)(2,1)}, bf16[2,272,512]{2,1,0:T(8,128)(2,1)}, bf16[2,272,512]{2,1,0:T(8,128)(2,1)}, b...) custom-call(s32[1,1,2]{2,1,0:T(1,128)} %bitcast.44, f32[1]{0:T(128)S(6)} %copy.20.dt_bias, f32[1]{0:T(128)S(6)} %copy.21.a_log, ...), custom_call_target="tpu_custom_call" | custom-call | tf_op jit(solution)/shard_map/enter/pallas_call | solution.py:338
  18.8 3.0 %collective-permute-start.3 = (bf16[2,256,256]{2,1,0:T(8,128)(2,1)}, bf16[2,256,256]{2,1,0:T(8,128)(2,1)S(1)}, u32[]{:S(2)}, u32[]{:S(2)}) collective-permute-start(bf16[2,256,256]{2,1,0:T(8,128)(2,1)} %get-tuple-element.44), channel_id=1, source_target_pairs={{0,1},{1,0},{2,3},{3,2},{4,5},{5,4},{6,7},{7,6},{8,9},{9,8},{10,11... | collective-permute-start | bytes 786440 | tf_op jit(solution)/shard_map/ppermute | solution.py:21
  21.8 5.9 %gates.1 = (bf16[2,256,512]{2,1,0:T(8,128)(2,1)}, bf16[2,256,512]{2,1,0:T(8,128)(2,1)}) custom-call(bf16[1024,2048]{1,0:T(8,128)(2,1)} %get-tuple-element.46.rows_hbm, bf16[2048,1024]{1,0:T(8,128)(2,1)} %xz.3), custom_call_target="tpu_custom_call" | custom-call | tf_op jit(solution)/shard_map/gates/pallas_call | solution.py:412
  27.8 1.3 %collective-permute-done.3 = bf16[2,256,256]{2,1,0:T(8,128)(2,1)S(1)} collective-permute-done((bf16[2,256,256]{2,1,0:T(8,128)(2,1)}, bf16[2,256,256]{2,1,0:T(8,128)(2,1)S(1)}, u32[]{:S(2)}, u32[]{:S(2)}) %collective-permute-start.3) | collective-permute-done | bytes 262176 | tf_op jit(solution)/shard_map/ppermute | solution.py:21
  29.7 1.0 convert_add_fusion.2
  30.8 3.1 %collective-permute-start.4 = (bf16[256,256]{1,0:T(8,128)(2,1)S(1)}, bf16[256,256]{1,0:T(8,128)(2,1)S(1)}, u32[]{:S(2)}, u32[]{:S(2)}) collective-permute-start(bf16[256,256]{1,0:T(8,128)(2,1)S(1)} %get-tuple-element.49), channel_id=1, source_target_pairs={{0,2},{1,3},{2,0},{3,1},{4,6},{5,7},{6,4},{7,5},{8,10},{9,11},{10,... | collective-permute-start | bytes 393224 | tf_op jit(solution)/shard_map/ppermute | solution.py:21
  33.9 9.5 %collective-permute-done.2 = bf16[2,272,512]{2,1,0:T(8,128)(2,1)} collective-permute-done((bf16[2,272,512]{2,1,0:T(8,128)(2,1)}, bf16[2,272,512]{2,1,0:T(8,128)(2,1)}, u32[]{:S(2)}, u32[]{:S(2)}) %collective-permute-start.2) | collective-permute-done | bytes 557088 | tf_op jit(solution)/shard_map/ppermute | solution.py:21
  43.4 1.2 %convert_add_fusion = bf16[2,272,512]{2,1,0:T(8,128)(2,1)S(1)} fusion(bf16[2,272,512]{2,1,0:T(8,128)(2,1)} %collective-permute-done.2, bf16[2,272,512]{2,1,0:T(8,128)(2,1)S(1)} %copy-done.11), kind=kLoop, calls=%fused_computation.9 | loop fusion | flops 1114112 | bytes 1671168 | tf_op jit(solution)/shard_map/add | solution.py:608
  45.4 1.9 %collective-permute-start.5 = (bf16[272,512]{1,0:T(8,128)(2,1)}, bf16[272,512]{1,0:T(8,128)(2,1)S(1)}, u32[]{:S(2)}, u32[]{:S(2)}) collective-permute-start(bf16[272,512]{1,0:T(8,128)(2,1)} %get-tuple-element.53), channel_id=1, source_target_pairs={{0,2},{1,3},{2,0},{3,1},{4,6},{5,7},{6,4},{7,5},{8,10},{9,11},{10,... | collective-permute-start | bytes 835592 | tf_op jit(solution)/shard_map/ppermute | solution.py:21
  47.3 2.5 %collective-permute-start.8 = (bf16[2,256,512]{2,1,0:T(8,128)(2,1)}, bf16[2,256,512]{2,1,0:T(8,128)(2,1)}, u32[]{:S(2)}, u32[]{:S(2)}) collective-permute-start(bf16[2,256,512]{2,1,0:T(8,128)(2,1)} %get-tuple-element.65), channel_id=1, source_target_pairs={{0,1},{1,0},{2,3},{3,2},{4,5},{5,4},{6,7},{7,6},{8,9},{9,8},{10,11... | collective-permute-start | bytes 1572872 | tf_op jit(solution)/shard_map/ppermute | solution.py:21
  49.9 2.6 %broadcast_select_fusion.3 = (bf16[256,2048]{1,0:T(8,128)(2,1)S(1)}, bf16[256,2048]{1,0:T(8,128)(2,1)}) fusion(pred[]{:T(512)S(6)} %eq.18, bf16[512,2048]{1,0:T(8,128)(2,1)} %get-tuple-element.56, bf16[2048]{0:T(1024)(128)(2,1)} %newline.1, pred[256]{0:T(512)(128)(4,1)S(1)} %iota_compare_fusion.2, bf16[1,512,2048]{2,1,0:T(8,128)(2,1)S(1)} %copy-done.1), kind=kLoop, calls=%fused_computation.15 | loop fusion | flops 1572864 | bytes 4198657 | tf_op jit(solution)/shard_map/jit(_where)/select_n | solution.py:629
  52.4 3.2 %broadcast_select_fusion = (bf16[512,2048]{1,0:T(8,128)(2,1)S(1)}, bf16[512,2048]{1,0:T(8,128)(2,1)}) fusion(bf16[512,2048]{1,0:T(8,128)(2,1)} %collective-permute-done.6, bf16[512,2048]{1,0:T(8,128)(2,1)S(1)} %copy-done.4, pred[]{:T(512)S(6)} %lt.13), kind=kLoop, calls=%fused_computation.7 | loop fusion | flops 2097152 | bytes 8388609 | tf_op jit(solution)/shard_map/jit(_where)/select_n | solution.py:624
  55.6 6.1 %collective-permute-done.5.refs_1_ = bf16[272,512]{1,0:T(8,128)(2,1)S(1)} collective-permute-done((bf16[272,512]{1,0:T(8,128)(2,1)}, bf16[272,512]{1,0:T(8,128)(2,1)S(1)}, u32[]{:S(2)}, u32[]{:S(2)}) %collective-permute-start.5) | collective-permute-done | bytes 278560 | tf_op jit(solution)/shard_map/ppermute | solution.py:21
  62.4 2.0 %collective-permute-start.7 = (bf16[16,768]{1,0:T(8,128)(2,1)S(1)}, bf16[16,768]{1,0:T(8,128)(2,1)S(1)}, u32[]{:S(2)}, u32[]{:S(2)}) collective-permute-start(bf16[16,768]{1,0:T(8,128)(2,1)S(1)} %fusion.16), channel_id=1, source_target_pairs={{0,1},{2,3},{8,9},{10,11},{16,17},{18,19},{24,25},{26,27},{1,8},{3... | collective-permute-start | bytes 73736 | tf_op jit(solution)/shard_map/ppermute | solution.py:639
  64.5 1.4 %collective-permute-done.7.refs_4_ = bf16[16,768]{1,0:T(8,128)(2,1)S(1)} collective-permute-done((bf16[16,768]{1,0:T(8,128)(2,1)S(1)}, bf16[16,768]{1,0:T(8,128)(2,1)S(1)}, u32[]{:S(2)}, u32[]{:S(2)}) %collective-permute-start.7) | collective-permute-done | bytes 24608 | tf_op jit(solution)/shard_map/ppermute | solution.py:639
  66.5 3.6 %scan.1 = (bf16[256,512]{1,0:T(8,128)(2,1)}, bf16[256,256]{1,0:T(8,128)(2,1)}, f32[16,256]{1,0:T(8,128)}, f32[256,32]{1,0:T(8,128)}, bf16[144,512]{1,0:T(8,128)(2,1)}, /*index=5*/f32[8,512]{1,0:T(8,128)}) custom-call(bf16[272,512]{1,0:T(8,128)(2,1)} %copy-done.6, bf16[272,512]{1,0:T(8,128)(2,1)} %copy-done.13, bf16[256,256]{1,0:T(8,128)(2,1)} %copy-done.12, ...), custom_call_target="tpu_custom_call" | custom-call | tf_op jit(solution)/shard_map/scan/pallas_call | solution.py:497
  70.1 3.0 %collective-permute-start.10 = (bf16[144,512]{1,0:T(8,128)(2,1)}, bf16[144,512]{1,0:T(8,128)(2,1)S(1)}, u32[]{:S(2)}, u32[]{:S(2)}) collective-permute-start(bf16[144,512]{1,0:T(8,128)(2,1)} %get-tuple-element.66), channel_id=1, source_target_pairs={{0,1},{1,0},{2,3},{3,2},{4,5},{5,4},{6,7},{7,6},{8,9},{9,8},{10,11... | collective-permute-start | bytes 442376 | tf_op jit(solution)/shard_map/ppermute | solution.py:21
  73.1 1.3 %convert_add_fusion.1 = bf16[2,256,512]{2,1,0:T(8,128)(2,1)S(1)} fusion(bf16[2,256,512]{2,1,0:T(8,128)(2,1)} %collective-permute-done.8, bf16[2,256,512]{2,1,0:T(8,128)(2,1)} %get-tuple-element.64), kind=kLoop, calls=%fused_computation.12 | loop fusion | flops 1048576 | bytes 1572864 | tf_op jit(solution)/shard_map/add | solution.py:608
  75.3 2.5 %collective-permute-start.9 = (bf16[256,512]{1,0:T(8,128)(2,1)}, bf16[256,512]{1,0:T(8,128)(2,1)}, u32[]{:S(2)}, u32[]{:S(2)}) collective-permute-start(bf16[256,512]{1,0:T(8,128)(2,1)} %get-tuple-element.83), channel_id=1, source_target_pairs={{0,2},{1,3},{2,0},{3,1},{4,6},{5,7},{6,4},{7,5},{8,10},{9,11},{10,... | collective-permute-start | bytes 786440 | tf_op jit(solution)/shard_map/ppermute | solution.py:21
  77.8 2.4 %inside.1.local = f32[256,512]{1,0:T(8,128)} custom-call(bf16[256,512]{1,0:T(8,128)(2,1)} %get-tuple-element.67.streams, bf16[256,256]{1,0:T(8,128)(2,1)} %get-tuple-element.68.maps, f32[16,256]{1,0:T(8,128)} %get-tuple-element.69.meta, f32[256,32]{1,0:T(8,128)} %get-tuple-element.70.cols, f32[8,512]{1,0:T(8,128)} %get-tuple-element.71.params), custom_call_target="tpu_custom_call" | custom-call | tf_op jit(solution)/shard_map/inside/pallas_call | solution.py:540
  80.4 1.6 %collective-permute-start.11 = (bf16[144,512]{1,0:T(8,128)(2,1)S(1)}, bf16[144,512]{1,0:T(8,128)(2,1)S(1)}, u32[]{:S(2)}, u32[]{:S(2)}) collective-permute-start(bf16[144,512]{1,0:T(8,128)(2,1)S(1)} %fusion.7), channel_id=1, source_target_pairs={{0,8},{8,0},{16,24},{24,16},{1,9},{9,1},{17,25},{25,17},{2,10},{10... | collective-permute-start | bytes 442376 | tf_op jit(solution)/shard_map/ppermute | solution.py:21
  82.0 1.5 %collective-permute-start.12 = (bf16[144,512]{1,0:T(8,128)(2,1)S(1)}, bf16[144,512]{1,0:T(8,128)(2,1)}, u32[]{:S(2)}, u32[]{:S(2)}) collective-permute-start(bf16[144,512]{1,0:T(8,128)(2,1)S(1)} %fusion.7), channel_id=1, source_target_pairs={{0,16},{8,24},{16,0},{24,8},{1,17},{9,25},{17,1},{25,9},{2,18},{10... | collective-permute-start | bytes 442376 | tf_op jit(solution)/shard_map/ppermute | solution.py:21
  84.0 5.1 %collective-permute-done.9.received = bf16[256,512]{1,0:T(8,128)(2,1)} collective-permute-done((bf16[256,512]{1,0:T(8,128)(2,1)}, bf16[256,512]{1,0:T(8,128)(2,1)}, u32[]{:S(2)}, u32[]{:S(2)}) %collective-permute-start.9) | collective-permute-done | bytes 262176 | tf_op jit(solution)/shard_map/ppermute | solution.py:21
  89.8 3.0 %gate.1 = bf16[256,512]{1,0:T(8,128)(2,1)} custom-call(bf16[256,512]{1,0:T(8,128)(2,1)} %get-tuple-element.84.kept, bf16[256,512]{1,0:T(8,128)(2,1)} %collective-permute-done.9.received, f32[256,512]{1,0:T(8,128)} %inside.1.local, bf16[256,256]{1,0:T(8,128)(2,1)} %get-tuple-element.68.maps, f32[256,32]{1,0:T(8,128)} %get-tuple-element.70.cols, ...), custom_call_target="tpu_custom_call" | custom-call | tf_op jit(solution)/shard_map/gate/pallas_call | solution.py:581
  93.4 1.6 %collective-permute-start.14 = (bf16[256,512]{1,0:T(8,128)(2,1)}, bf16[256,512]{1,0:T(8,128)(2,1)S(1)}, u32[]{:S(2)}, u32[]{:S(2)}) collective-permute-start(bf16[256,512]{1,0:T(8,128)(2,1)} %gate.1), channel_id=1, source_target_pairs={{0,0},{1,1},{2,6},{3,7},{4,4},{5,5},{6,2},{7,3},{8,8},{9,9},{10,14... | collective-permute-start | bytes 786440 | tf_op jit(solution)/shard_map/ppermute | solution.py:653
  95.0 2.3 %collective-permute-start.16 = (bf16[256,512]{1,0:T(8,128)(2,1)}, bf16[256,512]{1,0:T(8,128)(2,1)S(1)}, u32[]{:S(2)}, u32[]{:S(2)}) collective-permute-start(bf16[256,512]{1,0:T(8,128)(2,1)} %gate.1), channel_id=1, source_target_pairs={{0,1},{1,0},{2,7},{3,6},{4,5},{5,4},{6,3},{7,2},{8,9},{9,8},{10,15... | collective-permute-start | bytes 786440 | tf_op jit(solution)/shard_map/ppermute | solution.py:653
  97.3 10.4 %collective-permute-done.15 = bf16[256,512]{1,0:T(8,128)(2,1)S(1)} collective-permute-done((bf16[256,512]{1,0:T(8,128)(2,1)}, bf16[256,512]{1,0:T(8,128)(2,1)S(1)}, u32[]{:S(2)}, u32[]{:S(2)}) %collective-permute-start.15) | collective-permute-done | bytes 262176 | tf_op jit(solution)/shard_map/ppermute | solution.py:653
  108.9 1.2 copy-done
  112.2 3.5 %collective-permute-done.17 = bf16[256,512]{1,0:T(8,128)(2,1)S(1)} collective-permute-done((bf16[256,512]{1,0:T(8,128)(2,1)S(1)}, bf16[256,512]{1,0:T(8,128)(2,1)S(1)}, u32[]{:S(2)}, u32[]{:S(2)}) %collective-permute-start.17) | collective-permute-done | bytes 262176 | tf_op jit(solution)/shard_map/ppermute | solution.py:21
  115.7 1.8 %fusion.3 = bf16[1,512,2048]{2,1,0:T(8,128)(2,1)} fusion(bf16[1,512,2048]{2,1,0:T(8,128)(2,1)} %copy-done.3, s32[]{:T(128)S(6)} %select_n.126, f32[256,2048]{1,0:T(8,128)S(1)} %fusion.18, bf16[256,512]{1,0:T(8,128)(2,1)S(1)} %collective-permute-done.17, bf16[512,2048]{1,0:T(8,128)(2,1)S(1)} %get-tuple-element.75, bf16[256,2048]{1,0:T(8,128)(2,1)S(1)} %get-tuple-element.76), kind=kOutput, calls=%fused_computation.5 | convolution fusion | flops 538968064 | bytes 6553604 | tf_op jit(solution)/shard_map/dot_general | solution.py:662
  (69 shorter events, 10.7 us)
Async XLA Ops:
  0.0 1.9 %copy-start.8 = (bf16[1,1,1,256,1280]{4,3,2,1,0:T(8,128)(2,1)S(1)}, bf16[1,1,1,256,1280]{4,3,2,1,0:T(8,128)(2,1)}, u32[]{:S(2)}) copy-start(bf16[1,1,1,256,1280]{4,3,2,1,0:T(8,128)(2,1)} %param.18) | copy-start | bytes 1966084
  1.4 3.7 %collective-permute-start.1 = (bf16[256,2048]{1,0:T(8,128)(2,1)S(1)}, bf16[256,2048]{1,0:T(8,128)(2,1)S(1)}, u32[]{:S(2)}, u32[]{:S(2)}) collective-permute-start(bf16[256,2048]{1,0:T(8,128)(2,1)S(1)} %slice_bitcast_fusion), channel_id=1, source_target_pairs={{0,4},{4,0},{1,5},{5,1},{2,6},{6,2},{3,7},{7,3},{8,12},{12,8},{9,1... | collective-permute-start | bytes 3145736 | tf_op jit(solution)/shard_map/ppermute | solution.py:21
  1.9 3.2 %collective-permute-start = (bf16[256,1280]{1,0:T(8,128)(2,1)S(1)}, bf16[256,1280]{1,0:T(8,128)(2,1)S(1)}, u32[]{:S(2)}, u32[]{:S(2)}) collective-permute-start(bf16[256,1280]{1,0:T(8,128)(2,1)S(1)} %bitcast.41), channel_id=1, source_target_pairs={{0,4},{4,0},{1,5},{5,1},{2,6},{6,2},{3,7},{7,3},{8,12},{12,8},{9,1... | collective-permute-start | bytes 1966088 | tf_op jit(solution)/shard_map/ppermute | solution.py:21
  5.1 1.2 %copy-start.7 = (bf16[256,2048]{1,0:T(8,128)(2,1)}, bf16[256,2048]{1,0:T(8,128)(2,1)S(1)}, u32[]{:S(2)}) copy-start(bf16[256,2048]{1,0:T(8,128)(2,1)S(1)} %collective-permute-done.1.text_other) | copy-start | bytes 3145732
  18.8 10.3 %collective-permute-start.3 = (bf16[2,256,256]{2,1,0:T(8,128)(2,1)}, bf16[2,256,256]{2,1,0:T(8,128)(2,1)S(1)}, u32[]{:S(2)}, u32[]{:S(2)}) collective-permute-start(bf16[2,256,256]{2,1,0:T(8,128)(2,1)} %get-tuple-element.44), channel_id=1, source_target_pairs={{0,1},{1,0},{2,3},{3,2},{4,5},{5,4},{6,7},{7,6},{8,9},{9,8},{10,11... | collective-permute-start | bytes 786440 | tf_op jit(solution)/shard_map/ppermute | solution.py:21
  21.8 21.7 %collective-permute-start.2 = (bf16[2,272,512]{2,1,0:T(8,128)(2,1)}, bf16[2,272,512]{2,1,0:T(8,128)(2,1)}, u32[]{:S(2)}, u32[]{:S(2)}) collective-permute-start(bf16[2,272,512]{2,1,0:T(8,128)(2,1)} %get-tuple-element.42), channel_id=1, source_target_pairs={{0,1},{1,0},{2,3},{3,2},{4,5},{5,4},{6,7},{7,6},{8,9},{9,8},{10,11... | collective-permute-start | bytes 1671176 | tf_op jit(solution)/shard_map/ppermute | solution.py:21
  21.8 7.9 %copy-start.14 = (bf16[2,256,256]{2,1,0:T(8,128)(2,1)S(1)}, bf16[2,256,256]{2,1,0:T(8,128)(2,1)}, u32[]{:S(2)}) copy-start(bf16[2,256,256]{2,1,0:T(8,128)(2,1)} %get-tuple-element.43) | copy-start | bytes 786436
  21.8 21.6 %copy-start.11 = (bf16[2,272,512]{2,1,0:T(8,128)(2,1)S(1)}, bf16[2,272,512]{2,1,0:T(8,128)(2,1)}, u32[]{:S(2)}) copy-start(bf16[2,272,512]{2,1,0:T(8,128)(2,1)} %get-tuple-element.41) | copy-start | bytes 1671172
  27.8 22.1 %copy-start.1 = (bf16[1,512,2048]{2,1,0:T(8,128)(2,1)S(1)}, bf16[1,512,2048]{2,1,0:T(8,128)(2,1)}, u32[]{:S(2)}) copy-start(bf16[1,512,2048]{2,1,0:T(8,128)(2,1)} %param.17) | copy-start | bytes 6291460
  30.8 21.6 %copy-start.12 = (bf16[256,256]{1,0:T(8,128)(2,1)}, bf16[256,256]{1,0:T(8,128)(2,1)S(1)}, u32[]{:S(2)}) copy-start(bf16[256,256]{1,0:T(8,128)(2,1)S(1)} %get-tuple-element.60.refs_2_) | copy-start | bytes 393220
  30.8 14.6 %collective-permute-start.4 = (bf16[256,256]{1,0:T(8,128)(2,1)S(1)}, bf16[256,256]{1,0:T(8,128)(2,1)S(1)}, u32[]{:S(2)}, u32[]{:S(2)}) collective-permute-start(bf16[256,256]{1,0:T(8,128)(2,1)S(1)} %get-tuple-element.49), channel_id=1, source_target_pairs={{0,2},{1,3},{2,0},{3,1},{4,6},{5,7},{6,4},{7,5},{8,10},{9,11},{10,... | collective-permute-start | bytes 393224 | tf_op jit(solution)/shard_map/ppermute | solution.py:21
  45.4 16.3 %copy-start.6 = (bf16[272,512]{1,0:T(8,128)(2,1)}, bf16[272,512]{1,0:T(8,128)(2,1)S(1)}, u32[]{:S(2)}) copy-start(bf16[272,512]{1,0:T(8,128)(2,1)S(1)} %get-tuple-element.58.refs_0_) | copy-start | bytes 835588
  45.4 4.4 %copy-start.17 = (bf16[256,256]{1,0:T(8,128)(2,1)}, bf16[256,256]{1,0:T(8,128)(2,1)S(1)}, u32[]{:S(2)}) copy-start(bf16[256,256]{1,0:T(8,128)(2,1)S(1)} %collective-permute-done.4.refs_3_) | copy-start | bytes 393220
  45.4 7.0 %collective-permute-start.6 = (bf16[512,2048]{1,0:T(8,128)(2,1)}, bf16[512,2048]{1,0:T(8,128)(2,1)}, u32[]{:S(2)}, u32[]{:S(2)}) collective-permute-start(bf16[512,2048]{1,0:T(8,128)(2,1)} %param.33), channel_id=1, source_target_pairs={{0,4},{4,0},{1,5},{5,1},{2,6},{6,2},{3,7},{7,3},{8,12},{12,8},{9,1... | collective-permute-start | bytes 6291464 | tf_op jit(solution)/shard_map/ppermute | solution.py:21
  45.4 16.2 %collective-permute-start.5 = (bf16[272,512]{1,0:T(8,128)(2,1)}, bf16[272,512]{1,0:T(8,128)(2,1)S(1)}, u32[]{:S(2)}, u32[]{:S(2)}) collective-permute-start(bf16[272,512]{1,0:T(8,128)(2,1)} %get-tuple-element.53), channel_id=1, source_target_pairs={{0,2},{1,3},{2,0},{3,1},{4,6},{5,7},{6,4},{7,5},{8,10},{9,11},{10,... | collective-permute-start | bytes 835592 | tf_op jit(solution)/shard_map/ppermute | solution.py:21
  47.3 25.8 %collective-permute-start.8 = (bf16[2,256,512]{2,1,0:T(8,128)(2,1)}, bf16[2,256,512]{2,1,0:T(8,128)(2,1)}, u32[]{:S(2)}, u32[]{:S(2)}) collective-permute-start(bf16[2,256,512]{2,1,0:T(8,128)(2,1)} %get-tuple-element.65), channel_id=1, source_target_pairs={{0,1},{1,0},{2,3},{3,2},{4,5},{5,4},{6,7},{7,6},{8,9},{9,8},{10,11... | collective-permute-start | bytes 1572872 | tf_op jit(solution)/shard_map/ppermute | solution.py:21
  49.8 2.6 %copy-start.4 = (bf16[512,2048]{1,0:T(8,128)(2,1)S(1)}, bf16[512,2048]{1,0:T(8,128)(2,1)}, u32[]{:S(2)}) copy-start(bf16[512,2048]{1,0:T(8,128)(2,1)} %param.33) | copy-start | bytes 6291460
  62.4 3.5 %collective-permute-start.7 = (bf16[16,768]{1,0:T(8,128)(2,1)S(1)}, bf16[16,768]{1,0:T(8,128)(2,1)S(1)}, u32[]{:S(2)}, u32[]{:S(2)}) collective-permute-start(bf16[16,768]{1,0:T(8,128)(2,1)S(1)} %fusion.16), channel_id=1, source_target_pairs={{0,1},{2,3},{8,9},{10,11},{16,17},{18,19},{24,25},{26,27},{1,8},{3... | collective-permute-start | bytes 73736 | tf_op jit(solution)/shard_map/ppermute | solution.py:639
  70.1 10.1 %copy-start.10 = (bf16[144,512]{1,0:T(8,128)(2,1)S(1)}, bf16[144,512]{1,0:T(8,128)(2,1)}, u32[]{:S(2)}) copy-start(bf16[144,512]{1,0:T(8,128)(2,1)} %get-tuple-element.66) | copy-start | bytes 442372
  70.1 10.1 %collective-permute-start.10 = (bf16[144,512]{1,0:T(8,128)(2,1)}, bf16[144,512]{1,0:T(8,128)(2,1)S(1)}, u32[]{:S(2)}, u32[]{:S(2)}) collective-permute-start(bf16[144,512]{1,0:T(8,128)(2,1)} %get-tuple-element.66), channel_id=1, source_target_pairs={{0,1},{1,0},{2,3},{3,2},{4,5},{5,4},{6,7},{7,6},{8,9},{9,8},{10,11... | collective-permute-start | bytes 442376 | tf_op jit(solution)/shard_map/ppermute | solution.py:21
  75.3 13.8 %collective-permute-start.9 = (bf16[256,512]{1,0:T(8,128)(2,1)}, bf16[256,512]{1,0:T(8,128)(2,1)}, u32[]{:S(2)}, u32[]{:S(2)}) collective-permute-start(bf16[256,512]{1,0:T(8,128)(2,1)} %get-tuple-element.83), channel_id=1, source_target_pairs={{0,2},{1,3},{2,0},{3,1},{4,6},{5,7},{6,4},{7,5},{8,10},{9,11},{10,... | collective-permute-start | bytes 786440 | tf_op jit(solution)/shard_map/ppermute | solution.py:21
  80.2 9.5 %copy-start.5 = (bf16[144,512]{1,0:T(8,128)(2,1)}, bf16[144,512]{1,0:T(8,128)(2,1)S(1)}, u32[]{:S(2)}) copy-start(bf16[144,512]{1,0:T(8,128)(2,1)S(1)} %collective-permute-done.10.partner) | copy-start | bytes 442372
  80.4 8.7 %collective-permute-start.11 = (bf16[144,512]{1,0:T(8,128)(2,1)S(1)}, bf16[144,512]{1,0:T(8,128)(2,1)S(1)}, u32[]{:S(2)}, u32[]{:S(2)}) collective-permute-start(bf16[144,512]{1,0:T(8,128)(2,1)S(1)} %fusion.7), channel_id=1, source_target_pairs={{0,8},{8,0},{16,24},{24,16},{1,9},{9,1},{17,25},{25,17},{2,10},{10... | collective-permute-start | bytes 442376 | tf_op jit(solution)/shard_map/ppermute | solution.py:21
  82.0 7.2 %collective-permute-start.12 = (bf16[144,512]{1,0:T(8,128)(2,1)S(1)}, bf16[144,512]{1,0:T(8,128)(2,1)}, u32[]{:S(2)}, u32[]{:S(2)}) collective-permute-start(bf16[144,512]{1,0:T(8,128)(2,1)S(1)} %fusion.7), channel_id=1, source_target_pairs={{0,16},{8,24},{16,0},{24,8},{1,17},{9,25},{17,1},{25,9},{2,18},{10... | collective-permute-start | bytes 442376 | tf_op jit(solution)/shard_map/ppermute | solution.py:21
  83.5 6.3 %collective-permute-start.13 = (bf16[144,512]{1,0:T(8,128)(2,1)S(1)}, bf16[144,512]{1,0:T(8,128)(2,1)}, u32[]{:S(2)}, u32[]{:S(2)}) collective-permute-start(bf16[144,512]{1,0:T(8,128)(2,1)S(1)} %fusion.7), channel_id=1, source_target_pairs={{0,24},{8,16},{16,8},{24,0},{1,25},{9,17},{17,9},{25,1},{2,26},{10... | collective-permute-start | bytes 442376 | tf_op jit(solution)/shard_map/ppermute | solution.py:21
  92.8 14.9 %collective-permute-start.15 = (bf16[256,512]{1,0:T(8,128)(2,1)}, bf16[256,512]{1,0:T(8,128)(2,1)S(1)}, u32[]{:S(2)}, u32[]{:S(2)}) collective-permute-start(bf16[256,512]{1,0:T(8,128)(2,1)} %gate.1), channel_id=1, source_target_pairs={{0,2},{1,3},{2,4},{3,5},{4,6},{5,7},{6,0},{7,1},{8,10},{9,11},{10,... | collective-permute-start | bytes 786440 | tf_op jit(solution)/shard_map/ppermute | solution.py:653
  93.4 15.1 %collective-permute-start.14 = (bf16[256,512]{1,0:T(8,128)(2,1)}, bf16[256,512]{1,0:T(8,128)(2,1)S(1)}, u32[]{:S(2)}, u32[]{:S(2)}) collective-permute-start(bf16[256,512]{1,0:T(8,128)(2,1)} %gate.1), channel_id=1, source_target_pairs={{0,0},{1,1},{2,6},{3,7},{4,4},{5,5},{6,2},{7,3},{8,8},{9,9},{10,14... | collective-permute-start | bytes 786440 | tf_op jit(solution)/shard_map/ppermute | solution.py:653
  95.0 15.9 %collective-permute-start.16 = (bf16[256,512]{1,0:T(8,128)(2,1)}, bf16[256,512]{1,0:T(8,128)(2,1)S(1)}, u32[]{:S(2)}, u32[]{:S(2)}) collective-permute-start(bf16[256,512]{1,0:T(8,128)(2,1)} %gate.1), channel_id=1, source_target_pairs={{0,1},{1,0},{2,7},{3,6},{4,5},{5,4},{6,3},{7,2},{8,9},{9,8},{10,15... | collective-permute-start | bytes 786440 | tf_op jit(solution)/shard_map/ppermute | solution.py:653
  107.7 8.0 %collective-permute-start.17 = (bf16[256,512]{1,0:T(8,128)(2,1)S(1)}, bf16[256,512]{1,0:T(8,128)(2,1)S(1)}, u32[]{:S(2)}, u32[]{:S(2)}) collective-permute-start(bf16[256,512]{1,0:T(8,128)(2,1)S(1)} %collective-permute-done.15), channel_id=1, source_target_pairs={{0,1},{1,0},{2,3},{3,2},{4,5},{5,4},{6,7},{7,6},{8,9},{9,8},{10,11... | collective-permute-start | bytes 786440 | tf_op jit(solution)/shard_map/ppermute | solution.py:21
  107.7 1.2 %copy-start.2 = (bf16[256,2048]{1,0:T(8,128)(2,1)S(1)}, bf16[256,2048]{1,0:T(8,128)(2,1)}, u32[]{:S(2)}) copy-start(bf16[256,2048]{1,0:T(8,128)(2,1)} %get-tuple-element.57) | copy-start | bytes 3145732
  108.4 1.7 %copy-start = (bf16[512,2048]{1,0:T(8,128)(2,1)S(1)}, bf16[512,2048]{1,0:T(8,128)(2,1)}, u32[]{:S(2)}) copy-start(bf16[512,2048]{1,0:T(8,128)(2,1)} %get-tuple-element.74) | copy-start | bytes 6291460
  110.8 1.3 %copy-start.3 = (bf16[1,512,2048]{2,1,0:T(8,128)(2,1)}, bf16[1,512,2048]{2,1,0:T(8,128)(2,1)S(1)}, u32[]{:S(2)}) copy-start(bf16[1,512,2048]{2,1,0:T(8,128)(2,1)S(1)} %fusion.5) | copy-start | bytes 6291460
  (5 other events, 3.5 us)

commit v8 on v7

--- a/solution.py
+++ b/solution.py
@@ -485,7 +485,7 @@
     )
     state[0:128, :] = contract(both[:, 0:128], (x * carried).astype(BF16), ((0,), (0,))).astype(BF16)
     total = jnp.sum(jnp.exp(final) * owner, 0, keepdims=True)
-    state[128:144, :] = jnp.broadcast_to(total, (16, 512)).astype(BF16)
+    state[128:136, :] = jnp.broadcast_to(total, (8, 512)).astype(BF16)
     streams[...] = x.astype(BF16)
     maps[...] = both
     meta[0:8, :] = cumulative
@@ -501,7 +501,7 @@
             jax.ShapeDtypeStruct((half, 256), BF16),
             jax.ShapeDtypeStruct((16, half), F32),
             jax.ShapeDtypeStruct((half, 32), F32),
-            jax.ShapeDtypeStruct((144, 512), BF16),
+            jax.ShapeDtypeStruct((136, 512), BF16),
             jax.ShapeDtypeStruct((8, 512), F32),
         ],
         name="scan",
@@ -644,7 +644,6 @@
     local = inside(streams, maps, meta, as_columns, params)
     partner = swapped(state, "tensor", 1)
     whole = join(state, partner)
-    whole, local = lax.optimization_barrier((whole, local))
     others = [swapped(whole, "segment", bits) for bits in range(1, segment_count)]
     leaves, kept = added(keep_gates, arrived_gates)
     received = swapped(leaves, "tensor", 2)

time: 118 us -> 116 us (0.983)
  waiting for transfers between devices: 39.1 us -> 36.6 us
  starting transfers between devices: 26.9 us -> 28.8 us
    ppermute x14, starting transfers between devices: 20.4 us -> 22.7 us  [swapped(): lax.ppermute(block, axis, [(i, i ^ bits) for i in range(lax.axis_size(axi...]
    ppermute x14, waiting for transfers between devices: 27.2 us -> 25.5 us  [swapped(): lax.ppermute(block, axis, [(i, i ^ bits) for i in range(lax.axis_size(axi...]
    unnamed x38 -> x34, local copies, waits for them, and re-layouts: 5.27 us -> 4.54 us
where the time goes in v8:
time: 116 us
  waiting for transfers between devices  36.6 us (32%)
  starting transfers between devices  28.8 us (25%)
  Pallas kernels  27.3 us (24%)
  other arithmetic  10.7 us (9%)
  local copies, waits for them, and re-layouts  6.15 us (5%)
  matrix products  3.93 us (3%)
  between operations  2.17 us (2%)
    ppermute x14, waiting for transfers between devices, swapped(): lax.ppermute(block, axis, [(i, i ^ bits) for i in range(lax.axis_size(axi...  25.5 us
    ppermute x14, starting transfers between devices, swapped(): lax.ppermute(block, axis, [(i, i ^ bits) for i in range(lax.axis_size(axi...  22.7 us
    pallas_call x1, Pallas kernels, enter(): pl.pallas_call(enter_body, in_specs=[pl.BlockSpec(memory_space=pltpu.SMEM...  12.4 us
    ppermute x3, waiting for transfers between devices, per_device_halves(): lax.ppermute(normed, ('dp', 'tensor'), [(i, (i if i % 4 < 2 else i ^ 4) ^...  9.66 us
    pallas_call x1, Pallas kernels, gates(): pl.pallas_call(gates_body, in_specs=[whole, whole], out_specs=[whole, who...  5.91 us
    unnamed x34, local copies, waits for them, and re-layouts  4.54 us
    ppermute x3, starting transfers between devices, per_device_halves(): lax.ppermute(normed, ('dp', 'tensor'), [(i, (i if i % 4 < 2 else i ^ 4) ^...  4.01 us
    pallas_call x1, Pallas kernels, scan(): pl.pallas_call(lambda *refs: scan_body(width, *refs), out_shape=[jax.Shap...  3.62 us
  transfers between devices with their start and end apart: 18, of which 9 were waited for; matrix products, arithmetic and copies ran while one was open for 11% of the time, Pallas kernels for 10%

profile of v8, /device:TPU:0, one launch (start us, length us, event | category | flops | bytes accessed | tf_op | source)
XLA Modules:
  0.0 115.6 jit_solution(7653203485883983144)
XLA Ops:
  0.0 1.4 %slice_bitcast_fusion = bf16[256,2048]{1,0:T(8,128)(2,1)S(1)} fusion(bf16[1,512,2048]{2,1,0:T(8,128)(2,1)} %param.17), kind=kLoop, calls=%fused_computation.13 | loop fusion | bytes 2097152 | tf_op jit(solution)/shard_map/slice | solution.py:598
  3.9 1.2 %collective-permute-done.feats_other = bf16[256,1280]{1,0:T(8,128)(2,1)S(1)} collective-permute-done((bf16[256,1280]{1,0:T(8,128)(2,1)S(1)}, bf16[256,1280]{1,0:T(8,128)(2,1)S(1)}, u32[]{:S(2)}, u32[]{:S(2)}) %collective-permute-start) | collective-permute-done | bytes 655392 | tf_op jit(solution)/shard_map/ppermute | solution.py:21
  6.3 12.4 %enter.1 = (bf16[512,2048]{1,0:T(8,128)(2,1)}, bf16[1024,2048]{1,0:T(8,128)(2,1)}, bf16[2,272,512]{2,1,0:T(8,128)(2,1)}, bf16[2,272,512]{2,1,0:T(8,128)(2,1)}, b...) custom-call(s32[1,1,2]{2,1,0:T(1,128)} %bitcast.44, f32[1]{0:T(128)S(6)} %copy.20.dt_bias, f32[1]{0:T(128)S(6)} %copy.21.a_log, ...), custom_call_target="tpu_custom_call" | custom-call | tf_op jit(solution)/shard_map/enter/pallas_call | solution.py:338
  18.8 3.0 %collective-permute-start.3 = (bf16[2,256,256]{2,1,0:T(8,128)(2,1)}, bf16[2,256,256]{2,1,0:T(8,128)(2,1)S(1)}, u32[]{:S(2)}, u32[]{:S(2)}) collective-permute-start(bf16[2,256,256]{2,1,0:T(8,128)(2,1)} %get-tuple-element.42), channel_id=1, source_target_pairs={{0,1},{1,0},{2,3},{3,2},{4,5},{5,4},{6,7},{7,6},{8,9},{9,8},{10,11... | collective-permute-start | bytes 786440 | tf_op jit(solution)/shard_map/ppermute | solution.py:21
  21.9 5.9 %gates.1 = (bf16[2,256,512]{2,1,0:T(8,128)(2,1)}, bf16[2,256,512]{2,1,0:T(8,128)(2,1)}) custom-call(bf16[1024,2048]{1,0:T(8,128)(2,1)} %get-tuple-element.44.rows_hbm, bf16[2048,1024]{1,0:T(8,128)(2,1)} %xz.3), custom_call_target="tpu_custom_call" | custom-call | tf_op jit(solution)/shard_map/gates/pallas_call | solution.py:412
  27.8 1.3 %collective-permute-done.3 = bf16[2,256,256]{2,1,0:T(8,128)(2,1)S(1)} collective-permute-done((bf16[2,256,256]{2,1,0:T(8,128)(2,1)}, bf16[2,256,256]{2,1,0:T(8,128)(2,1)S(1)}, u32[]{:S(2)}, u32[]{:S(2)}) %collective-permute-start.3) | collective-permute-done | bytes 262176 | tf_op jit(solution)/shard_map/ppermute | solution.py:21
  29.2 3.1 %collective-permute-start.4 = (bf16[256,256]{1,0:T(8,128)(2,1)S(1)}, bf16[256,256]{1,0:T(8,128)(2,1)S(1)}, u32[]{:S(2)}, u32[]{:S(2)}) collective-permute-start(bf16[256,256]{1,0:T(8,128)(2,1)S(1)} %get-tuple-element.47), channel_id=1, source_target_pairs={{0,2},{1,3},{2,0},{3,1},{4,6},{5,7},{6,4},{7,5},{8,10},{9,11},{10,... | collective-permute-start | bytes 393224 | tf_op jit(solution)/shard_map/ppermute | solution.py:21
  32.3 11.1 %collective-permute-done.2 = bf16[2,272,512]{2,1,0:T(8,128)(2,1)} collective-permute-done((bf16[2,272,512]{2,1,0:T(8,128)(2,1)}, bf16[2,272,512]{2,1,0:T(8,128)(2,1)}, u32[]{:S(2)}, u32[]{:S(2)}) %collective-permute-start.2) | collective-permute-done | bytes 557088 | tf_op jit(solution)/shard_map/ppermute | solution.py:21
  43.5 1.2 %convert_add_fusion = bf16[2,272,512]{2,1,0:T(8,128)(2,1)S(1)} fusion(bf16[2,272,512]{2,1,0:T(8,128)(2,1)} %collective-permute-done.2, bf16[2,272,512]{2,1,0:T(8,128)(2,1)S(1)} %copy-done.10), kind=kLoop, calls=%fused_computation.9 | loop fusion | flops 1114112 | bytes 1671168 | tf_op jit(solution)/shard_map/add | solution.py:608
  45.5 1.9 %collective-permute-start.5 = (bf16[272,512]{1,0:T(8,128)(2,1)}, bf16[272,512]{1,0:T(8,128)(2,1)S(1)}, u32[]{:S(2)}, u32[]{:S(2)}) collective-permute-start(bf16[272,512]{1,0:T(8,128)(2,1)} %get-tuple-element.51), channel_id=1, source_target_pairs={{0,2},{1,3},{2,0},{3,1},{4,6},{5,7},{6,4},{7,5},{8,10},{9,11},{10,... | collective-permute-start | bytes 835592 | tf_op jit(solution)/shard_map/ppermute | solution.py:21
  47.4 2.5 %collective-permute-start.8 = (bf16[2,256,512]{2,1,0:T(8,128)(2,1)}, bf16[2,256,512]{2,1,0:T(8,128)(2,1)}, u32[]{:S(2)}, u32[]{:S(2)}) collective-permute-start(bf16[2,256,512]{2,1,0:T(8,128)(2,1)} %get-tuple-element.63), channel_id=1, source_target_pairs={{0,1},{1,0},{2,3},{3,2},{4,5},{5,4},{6,7},{7,6},{8,9},{9,8},{10,11... | collective-permute-start | bytes 1572872 | tf_op jit(solution)/shard_map/ppermute | solution.py:21
  49.9 2.6 %broadcast_select_fusion.3 = (bf16[256,2048]{1,0:T(8,128)(2,1)S(1)}, bf16[256,2048]{1,0:T(8,128)(2,1)}) fusion(pred[]{:T(512)S(6)} %eq.18, bf16[512,2048]{1,0:T(8,128)(2,1)} %get-tuple-element.54, bf16[2048]{0:T(1024)(128)(2,1)} %newline.1, pred[256]{0:T(512)(128)(4,1)S(1)} %iota_compare_fusion.2, bf16[1,512,2048]{2,1,0:T(8,128)(2,1)S(1)} %copy-done.1), kind=kLoop, calls=%fused_computation.15 | loop fusion | flops 1572864 | bytes 4198657 | tf_op jit(solution)/shard_map/jit(_where)/select_n | solution.py:629
  52.5 3.2 %broadcast_select_fusion = (bf16[512,2048]{1,0:T(8,128)(2,1)S(1)}, bf16[512,2048]{1,0:T(8,128)(2,1)}) fusion(bf16[512,2048]{1,0:T(8,128)(2,1)} %collective-permute-done.6, bf16[512,2048]{1,0:T(8,128)(2,1)S(1)} %copy-done.4, pred[]{:T(512)S(6)} %lt.13), kind=kLoop, calls=%fused_computation.7 | loop fusion | flops 2097152 | bytes 8388609 | tf_op jit(solution)/shard_map/jit(_where)/select_n | solution.py:624
  55.7 6.0 %collective-permute-done.5.refs_1_ = bf16[272,512]{1,0:T(8,128)(2,1)S(1)} collective-permute-done((bf16[272,512]{1,0:T(8,128)(2,1)}, bf16[272,512]{1,0:T(8,128)(2,1)S(1)}, u32[]{:S(2)}, u32[]{:S(2)}) %collective-permute-start.5) | collective-permute-done | bytes 278560 | tf_op jit(solution)/shard_map/ppermute | solution.py:21
  62.4 2.0 %collective-permute-start.7 = (bf16[16,768]{1,0:T(8,128)(2,1)S(1)}, bf16[16,768]{1,0:T(8,128)(2,1)S(1)}, u32[]{:S(2)}, u32[]{:S(2)}) collective-permute-start(bf16[16,768]{1,0:T(8,128)(2,1)S(1)} %fusion.16), channel_id=1, source_target_pairs={{0,1},{2,3},{8,9},{10,11},{16,17},{18,19},{24,25},{26,27},{1,8},{3... | collective-permute-start | bytes 73736 | tf_op jit(solution)/shard_map/ppermute | solution.py:639
  64.5 1.4 %collective-permute-done.7.refs_4_ = bf16[16,768]{1,0:T(8,128)(2,1)S(1)} collective-permute-done((bf16[16,768]{1,0:T(8,128)(2,1)S(1)}, bf16[16,768]{1,0:T(8,128)(2,1)S(1)}, u32[]{:S(2)}, u32[]{:S(2)}) %collective-permute-start.7) | collective-permute-done | bytes 24608 | tf_op jit(solution)/shard_map/ppermute | solution.py:639
  66.5 3.6 %scan.1 = (bf16[256,512]{1,0:T(8,128)(2,1)}, bf16[256,256]{1,0:T(8,128)(2,1)}, f32[16,256]{1,0:T(8,128)}, f32[256,32]{1,0:T(8,128)}, bf16[136,512]{1,0:T(8,128)(2,1)}, /*index=5*/f32[8,512]{1,0:T(8,128)}) custom-call(bf16[272,512]{1,0:T(8,128)(2,1)} %copy-done.6, bf16[272,512]{1,0:T(8,128)(2,1)} %copy-done.13, bf16[256,256]{1,0:T(8,128)(2,1)} %copy-done.12, ...), custom_call_target="tpu_custom_call" | custom-call | tf_op jit(solution)/shard_map/scan/pallas_call | solution.py:497
  70.1 3.0 %collective-permute-start.10 = (bf16[136,512]{1,0:T(8,128)(2,1)}, bf16[136,512]{1,0:T(8,128)(2,1)S(1)}, u32[]{:S(2)}, u32[]{:S(2)}) collective-permute-start(bf16[136,512]{1,0:T(8,128)(2,1)} %get-tuple-element.69), channel_id=1, source_target_pairs={{0,1},{1,0},{2,3},{3,2},{4,5},{5,4},{6,7},{7,6},{8,9},{9,8},{10,11... | collective-permute-start | bytes 417800 | tf_op jit(solution)/shard_map/ppermute | solution.py:21
  73.1 1.3 %convert_add_fusion.1 = bf16[2,256,512]{2,1,0:T(8,128)(2,1)S(1)} fusion(bf16[2,256,512]{2,1,0:T(8,128)(2,1)} %collective-permute-done.8, bf16[2,256,512]{2,1,0:T(8,128)(2,1)} %get-tuple-element.62), kind=kLoop, calls=%fused_computation.12 | loop fusion | flops 1048576 | bytes 1572864 | tf_op jit(solution)/shard_map/add | solution.py:608
  75.2 2.5 %collective-permute-start.9 = (bf16[256,512]{1,0:T(8,128)(2,1)S(1)}, bf16[256,512]{1,0:T(8,128)(2,1)}, u32[]{:S(2)}, u32[]{:S(2)}) collective-permute-start(bf16[256,512]{1,0:T(8,128)(2,1)S(1)} %get-tuple-element.79), channel_id=1, source_target_pairs={{0,2},{1,3},{2,0},{3,1},{4,6},{5,7},{6,4},{7,5},{8,10},{9,11},{10,... | collective-permute-start | bytes 786440 | tf_op jit(solution)/shard_map/ppermute | solution.py:21
  78.6 3.4 %collective-permute-start.11 = (bf16[136,512]{1,0:T(8,128)(2,1)}, bf16[136,512]{1,0:T(8,128)(2,1)}, u32[]{:S(2)}, u32[]{:S(2)}) collective-permute-start(bf16[136,512]{1,0:T(8,128)(2,1)} %fusion.7), channel_id=1, source_target_pairs={{0,8},{8,0},{16,24},{24,16},{1,9},{9,1},{17,25},{25,17},{2,10},{10... | collective-permute-start | bytes 417800 | tf_op jit(solution)/shard_map/ppermute | solution.py:21
  82.0 1.5 %collective-permute-start.12 = (bf16[136,512]{1,0:T(8,128)(2,1)}, bf16[136,512]{1,0:T(8,128)(2,1)}, u32[]{:S(2)}, u32[]{:S(2)}) collective-permute-start(bf16[136,512]{1,0:T(8,128)(2,1)} %fusion.7), channel_id=1, source_target_pairs={{0,16},{8,24},{16,0},{24,8},{1,17},{9,25},{17,1},{25,9},{2,18},{10... | collective-permute-start | bytes 417800 | tf_op jit(solution)/shard_map/ppermute | solution.py:21
  83.5 1.0 collective-permute-start.13
  84.5 2.4 %inside.1.local = f32[256,512]{1,0:T(8,128)} custom-call(bf16[256,512]{1,0:T(8,128)(2,1)} %get-tuple-element.64.streams, bf16[256,256]{1,0:T(8,128)(2,1)} %get-tuple-element.65.maps, f32[16,256]{1,0:T(8,128)} %get-tuple-element.66.meta, f32[256,32]{1,0:T(8,128)} %get-tuple-element.67.cols, f32[8,512]{1,0:T(8,128)} %get-tuple-element.68.params), custom_call_target="tpu_custom_call" | custom-call | tf_op jit(solution)/shard_map/inside/pallas_call | solution.py:540
  86.9 2.0 %collective-permute-done.9.received = bf16[256,512]{1,0:T(8,128)(2,1)} collective-permute-done((bf16[256,512]{1,0:T(8,128)(2,1)S(1)}, bf16[256,512]{1,0:T(8,128)(2,1)}, u32[]{:S(2)}, u32[]{:S(2)}) %collective-permute-start.9) | collective-permute-done | bytes 262176 | tf_op jit(solution)/shard_map/ppermute | solution.py:21
  89.8 3.0 %gate.1 = bf16[256,512]{1,0:T(8,128)(2,1)} custom-call(bf16[256,512]{1,0:T(8,128)(2,1)} %get-tuple-element.80.kept, bf16[256,512]{1,0:T(8,128)(2,1)} %collective-permute-done.9.received, f32[256,512]{1,0:T(8,128)} %inside.1.local, bf16[256,256]{1,0:T(8,128)(2,1)} %get-tuple-element.65.maps, f32[256,32]{1,0:T(8,128)} %get-tuple-element.67.cols, ...), custom_call_target="tpu_custom_call" | custom-call | tf_op jit(solution)/shard_map/gate/pallas_call | solution.py:581
  92.8 1.6 %collective-permute-start.14 = (bf16[256,512]{1,0:T(8,128)(2,1)}, bf16[256,512]{1,0:T(8,128)(2,1)S(1)}, u32[]{:S(2)}, u32[]{:S(2)}) collective-permute-start(bf16[256,512]{1,0:T(8,128)(2,1)} %gate.1), channel_id=1, source_target_pairs={{0,0},{1,1},{2,6},{3,7},{4,4},{5,5},{6,2},{7,3},{8,8},{9,9},{10,14... | collective-permute-start | bytes 786440 | tf_op jit(solution)/shard_map/ppermute | solution.py:652
  94.4 2.3 %collective-permute-start.16 = (bf16[256,512]{1,0:T(8,128)(2,1)}, bf16[256,512]{1,0:T(8,128)(2,1)S(1)}, u32[]{:S(2)}, u32[]{:S(2)}) collective-permute-start(bf16[256,512]{1,0:T(8,128)(2,1)} %gate.1), channel_id=1, source_target_pairs={{0,1},{1,0},{2,7},{3,6},{4,5},{5,4},{6,3},{7,2},{8,9},{9,8},{10,15... | collective-permute-start | bytes 786440 | tf_op jit(solution)/shard_map/ppermute | solution.py:652
  96.8 9.7 %collective-permute-done.15 = bf16[256,512]{1,0:T(8,128)(2,1)S(1)} collective-permute-done((bf16[256,512]{1,0:T(8,128)(2,1)}, bf16[256,512]{1,0:T(8,128)(2,1)S(1)}, u32[]{:S(2)}, u32[]{:S(2)}) %collective-permute-start.15) | collective-permute-done | bytes 262176 | tf_op jit(solution)/shard_map/ppermute | solution.py:652
  107.7 1.2 %copy-done = bf16[512,2048]{1,0:T(8,128)(2,1)S(1)} copy-done((bf16[512,2048]{1,0:T(8,128)(2,1)S(1)}, bf16[512,2048]{1,0:T(8,128)(2,1)}, u32[]{:S(2)}) %copy-start) | copy-done | bytes 2097176
  110.9 2.9 %collective-permute-done.17 = bf16[256,512]{1,0:T(8,128)(2,1)S(1)} collective-permute-done((bf16[256,512]{1,0:T(8,128)(2,1)S(1)}, bf16[256,512]{1,0:T(8,128)(2,1)S(1)}, u32[]{:S(2)}, u32[]{:S(2)}) %collective-permute-start.17) | collective-permute-done | bytes 262176 | tf_op jit(solution)/shard_map/ppermute | solution.py:21
  113.8 1.8 %fusion.3 = bf16[1,512,2048]{2,1,0:T(8,128)(2,1)} fusion(bf16[1,512,2048]{2,1,0:T(8,128)(2,1)} %copy-done.3, s32[]{:T(128)S(6)} %select_n.126, f32[256,2048]{1,0:T(8,128)S(1)} %fusion.18, bf16[256,512]{1,0:T(8,128)(2,1)S(1)} %collective-permute-done.17, bf16[512,2048]{1,0:T(8,128)(2,1)S(1)} %get-tuple-element.71, bf16[256,2048]{1,0:T(8,128)(2,1)S(1)} %get-tuple-element.72), kind=kOutput, calls=%fused_computation.5 | convolution fusion | flops 538968064 | bytes 6553604 | tf_op jit(solution)/shard_map/dot_general | solution.py:661
  (65 shorter events, 9.9 us)
Async XLA Ops:
  0.0 1.9 %copy-start.8 = (bf16[1,1,1,256,1280]{4,3,2,1,0:T(8,128)(2,1)S(1)}, bf16[1,1,1,256,1280]{4,3,2,1,0:T(8,128)(2,1)}, u32[]{:S(2)}) copy-start(bf16[1,1,1,256,1280]{4,3,2,1,0:T(8,128)(2,1)} %param.18) | copy-start | bytes 1966084
  1.4 3.7 %collective-permute-start.1 = (bf16[256,2048]{1,0:T(8,128)(2,1)S(1)}, bf16[256,2048]{1,0:T(8,128)(2,1)S(1)}, u32[]{:S(2)}, u32[]{:S(2)}) collective-permute-start(bf16[256,2048]{1,0:T(8,128)(2,1)S(1)} %slice_bitcast_fusion), channel_id=1, source_target_pairs={{0,4},{4,0},{1,5},{5,1},{2,6},{6,2},{3,7},{7,3},{8,12},{12,8},{9,1... | collective-permute-start | bytes 3145736 | tf_op jit(solution)/shard_map/ppermute | solution.py:21
  1.9 3.2 %collective-permute-start = (bf16[256,1280]{1,0:T(8,128)(2,1)S(1)}, bf16[256,1280]{1,0:T(8,128)(2,1)S(1)}, u32[]{:S(2)}, u32[]{:S(2)}) collective-permute-start(bf16[256,1280]{1,0:T(8,128)(2,1)S(1)} %bitcast.41), channel_id=1, source_target_pairs={{0,4},{4,0},{1,5},{5,1},{2,6},{6,2},{3,7},{7,3},{8,12},{12,8},{9,1... | collective-permute-start | bytes 1966088 | tf_op jit(solution)/shard_map/ppermute | solution.py:21
  5.1 1.2 %copy-start.7 = (bf16[256,2048]{1,0:T(8,128)(2,1)}, bf16[256,2048]{1,0:T(8,128)(2,1)S(1)}, u32[]{:S(2)}) copy-start(bf16[256,2048]{1,0:T(8,128)(2,1)S(1)} %collective-permute-done.1.text_other) | copy-start | bytes 3145732
  18.8 10.3 %collective-permute-start.3 = (bf16[2,256,256]{2,1,0:T(8,128)(2,1)}, bf16[2,256,256]{2,1,0:T(8,128)(2,1)S(1)}, u32[]{:S(2)}, u32[]{:S(2)}) collective-permute-start(bf16[2,256,256]{2,1,0:T(8,128)(2,1)} %get-tuple-element.42), channel_id=1, source_target_pairs={{0,1},{1,0},{2,3},{3,2},{4,5},{5,4},{6,7},{7,6},{8,9},{9,8},{10,11... | collective-permute-start | bytes 786440 | tf_op jit(solution)/shard_map/ppermute | solution.py:21
  21.8 21.7 %collective-permute-start.2 = (bf16[2,272,512]{2,1,0:T(8,128)(2,1)}, bf16[2,272,512]{2,1,0:T(8,128)(2,1)}, u32[]{:S(2)}, u32[]{:S(2)}) collective-permute-start(bf16[2,272,512]{2,1,0:T(8,128)(2,1)} %get-tuple-element.40), channel_id=1, source_target_pairs={{0,1},{1,0},{2,3},{3,2},{4,5},{5,4},{6,7},{7,6},{8,9},{9,8},{10,11... | collective-permute-start | bytes 1671176 | tf_op jit(solution)/shard_map/ppermute | solution.py:21
  21.9 7.2 %copy-start.14 = (bf16[2,256,256]{2,1,0:T(8,128)(2,1)S(1)}, bf16[2,256,256]{2,1,0:T(8,128)(2,1)}, u32[]{:S(2)}) copy-start(bf16[2,256,256]{2,1,0:T(8,128)(2,1)} %get-tuple-element.41) | copy-start | bytes 786436
  21.9 21.6 %copy-start.10 = (bf16[2,272,512]{2,1,0:T(8,128)(2,1)S(1)}, bf16[2,272,512]{2,1,0:T(8,128)(2,1)}, u32[]{:S(2)}) copy-start(bf16[2,272,512]{2,1,0:T(8,128)(2,1)} %get-tuple-element.39) | copy-start | bytes 1671172
  27.8 22.1 %copy-start.1 = (bf16[1,512,2048]{2,1,0:T(8,128)(2,1)S(1)}, bf16[1,512,2048]{2,1,0:T(8,128)(2,1)}, u32[]{:S(2)}) copy-start(bf16[1,512,2048]{2,1,0:T(8,128)(2,1)} %param.17) | copy-start | bytes 6291460
  29.2 23.3 %copy-start.12 = (bf16[256,256]{1,0:T(8,128)(2,1)}, bf16[256,256]{1,0:T(8,128)(2,1)S(1)}, u32[]{:S(2)}) copy-start(bf16[256,256]{1,0:T(8,128)(2,1)S(1)} %get-tuple-element.58.refs_2_) | copy-start | bytes 393220
  29.2 16.2 %collective-permute-start.4 = (bf16[256,256]{1,0:T(8,128)(2,1)S(1)}, bf16[256,256]{1,0:T(8,128)(2,1)S(1)}, u32[]{:S(2)}, u32[]{:S(2)}) collective-permute-start(bf16[256,256]{1,0:T(8,128)(2,1)S(1)} %get-tuple-element.47), channel_id=1, source_target_pairs={{0,2},{1,3},{2,0},{3,1},{4,6},{5,7},{6,4},{7,5},{8,10},{9,11},{10,... | collective-permute-start | bytes 393224 | tf_op jit(solution)/shard_map/ppermute | solution.py:21
  45.4 16.3 %copy-start.6 = (bf16[272,512]{1,0:T(8,128)(2,1)}, bf16[272,512]{1,0:T(8,128)(2,1)S(1)}, u32[]{:S(2)}) copy-start(bf16[272,512]{1,0:T(8,128)(2,1)S(1)} %get-tuple-element.56.refs_0_) | copy-start | bytes 835588
  45.4 4.4 %copy-start.15 = (bf16[256,256]{1,0:T(8,128)(2,1)}, bf16[256,256]{1,0:T(8,128)(2,1)S(1)}, u32[]{:S(2)}) copy-start(bf16[256,256]{1,0:T(8,128)(2,1)S(1)} %collective-permute-done.4.refs_3_) | copy-start | bytes 393220
  45.4 7.0 %collective-permute-start.6 = (bf16[512,2048]{1,0:T(8,128)(2,1)}, bf16[512,2048]{1,0:T(8,128)(2,1)}, u32[]{:S(2)}, u32[]{:S(2)}) collective-permute-start(bf16[512,2048]{1,0:T(8,128)(2,1)} %param.33), channel_id=1, source_target_pairs={{0,4},{4,0},{1,5},{5,1},{2,6},{6,2},{3,7},{7,3},{8,12},{12,8},{9,1... | collective-permute-start | bytes 6291464 | tf_op jit(solution)/shard_map/ppermute | solution.py:21
  45.5 16.2 %collective-permute-start.5 = (bf16[272,512]{1,0:T(8,128)(2,1)}, bf16[272,512]{1,0:T(8,128)(2,1)S(1)}, u32[]{:S(2)}, u32[]{:S(2)}) collective-permute-start(bf16[272,512]{1,0:T(8,128)(2,1)} %get-tuple-element.51), channel_id=1, source_target_pairs={{0,2},{1,3},{2,0},{3,1},{4,6},{5,7},{6,4},{7,5},{8,10},{9,11},{10,... | collective-permute-start | bytes 835592 | tf_op jit(solution)/shard_map/ppermute | solution.py:21
  47.4 25.8 %collective-permute-start.8 = (bf16[2,256,512]{2,1,0:T(8,128)(2,1)}, bf16[2,256,512]{2,1,0:T(8,128)(2,1)}, u32[]{:S(2)}, u32[]{:S(2)}) collective-permute-start(bf16[2,256,512]{2,1,0:T(8,128)(2,1)} %get-tuple-element.63), channel_id=1, source_target_pairs={{0,1},{1,0},{2,3},{3,2},{4,5},{5,4},{6,7},{7,6},{8,9},{9,8},{10,11... | collective-permute-start | bytes 1572872 | tf_op jit(solution)/shard_map/ppermute | solution.py:21
  49.9 2.6 %copy-start.4 = (bf16[512,2048]{1,0:T(8,128)(2,1)S(1)}, bf16[512,2048]{1,0:T(8,128)(2,1)}, u32[]{:S(2)}) copy-start(bf16[512,2048]{1,0:T(8,128)(2,1)} %param.33) | copy-start | bytes 6291460
  62.4 3.5 %collective-permute-start.7 = (bf16[16,768]{1,0:T(8,128)(2,1)S(1)}, bf16[16,768]{1,0:T(8,128)(2,1)S(1)}, u32[]{:S(2)}, u32[]{:S(2)}) collective-permute-start(bf16[16,768]{1,0:T(8,128)(2,1)S(1)} %fusion.16), channel_id=1, source_target_pairs={{0,1},{2,3},{8,9},{10,11},{16,17},{18,19},{24,25},{26,27},{1,8},{3... | collective-permute-start | bytes 73736 | tf_op jit(solution)/shard_map/ppermute | solution.py:639
  70.1 7.6 %copy-start.11 = (bf16[136,512]{1,0:T(8,128)(2,1)S(1)}, bf16[136,512]{1,0:T(8,128)(2,1)}, u32[]{:S(2)}) copy-start(bf16[136,512]{1,0:T(8,128)(2,1)} %get-tuple-element.69) | copy-start | bytes 417796
  70.1 7.6 %collective-permute-start.10 = (bf16[136,512]{1,0:T(8,128)(2,1)}, bf16[136,512]{1,0:T(8,128)(2,1)S(1)}, u32[]{:S(2)}, u32[]{:S(2)}) collective-permute-start(bf16[136,512]{1,0:T(8,128)(2,1)} %get-tuple-element.69), channel_id=1, source_target_pairs={{0,1},{1,0},{2,3},{3,2},{4,5},{5,4},{6,7},{7,6},{8,9},{9,8},{10,11... | collective-permute-start | bytes 417800 | tf_op jit(solution)/shard_map/ppermute | solution.py:21
  75.2 13.6 %collective-permute-start.9 = (bf16[256,512]{1,0:T(8,128)(2,1)S(1)}, bf16[256,512]{1,0:T(8,128)(2,1)}, u32[]{:S(2)}, u32[]{:S(2)}) collective-permute-start(bf16[256,512]{1,0:T(8,128)(2,1)S(1)} %get-tuple-element.79), channel_id=1, source_target_pairs={{0,2},{1,3},{2,0},{3,1},{4,6},{5,7},{6,4},{7,5},{8,10},{9,11},{10,... | collective-permute-start | bytes 786440 | tf_op jit(solution)/shard_map/ppermute | solution.py:21
  77.8 12.0 %copy-start.5 = (bf16[136,512]{1,0:T(8,128)(2,1)}, bf16[136,512]{1,0:T(8,128)(2,1)S(1)}, u32[]{:S(2)}) copy-start(bf16[136,512]{1,0:T(8,128)(2,1)S(1)} %collective-permute-done.10.partner) | copy-start | bytes 417796
  78.6 10.3 %collective-permute-start.11 = (bf16[136,512]{1,0:T(8,128)(2,1)}, bf16[136,512]{1,0:T(8,128)(2,1)}, u32[]{:S(2)}, u32[]{:S(2)}) collective-permute-start(bf16[136,512]{1,0:T(8,128)(2,1)} %fusion.7), channel_id=1, source_target_pairs={{0,8},{8,0},{16,24},{24,16},{1,9},{9,1},{17,25},{25,17},{2,10},{10... | collective-permute-start | bytes 417800 | tf_op jit(solution)/shard_map/ppermute | solution.py:21
  82.0 6.9 %collective-permute-start.12 = (bf16[136,512]{1,0:T(8,128)(2,1)}, bf16[136,512]{1,0:T(8,128)(2,1)}, u32[]{:S(2)}, u32[]{:S(2)}) collective-permute-start(bf16[136,512]{1,0:T(8,128)(2,1)} %fusion.7), channel_id=1, source_target_pairs={{0,16},{8,24},{16,0},{24,8},{1,17},{9,25},{17,1},{25,9},{2,18},{10... | collective-permute-start | bytes 417800 | tf_op jit(solution)/shard_map/ppermute | solution.py:21
  83.5 6.3 %collective-permute-start.13 = (bf16[136,512]{1,0:T(8,128)(2,1)}, bf16[136,512]{1,0:T(8,128)(2,1)}, u32[]{:S(2)}, u32[]{:S(2)}) collective-permute-start(bf16[136,512]{1,0:T(8,128)(2,1)} %fusion.7), channel_id=1, source_target_pairs={{0,24},{8,16},{16,8},{24,0},{1,25},{9,17},{17,9},{25,1},{2,26},{10... | collective-permute-start | bytes 417800 | tf_op jit(solution)/shard_map/ppermute | solution.py:21
  92.8 13.7 %collective-permute-start.15 = (bf16[256,512]{1,0:T(8,128)(2,1)}, bf16[256,512]{1,0:T(8,128)(2,1)S(1)}, u32[]{:S(2)}, u32[]{:S(2)}) collective-permute-start(bf16[256,512]{1,0:T(8,128)(2,1)} %gate.1), channel_id=1, source_target_pairs={{0,2},{1,3},{2,4},{3,5},{4,6},{5,7},{6,0},{7,1},{8,10},{9,11},{10,... | collective-permute-start | bytes 786440 | tf_op jit(solution)/shard_map/ppermute | solution.py:652
  92.8 14.3 %collective-permute-start.14 = (bf16[256,512]{1,0:T(8,128)(2,1)}, bf16[256,512]{1,0:T(8,128)(2,1)S(1)}, u32[]{:S(2)}, u32[]{:S(2)}) collective-permute-start(bf16[256,512]{1,0:T(8,128)(2,1)} %gate.1), channel_id=1, source_target_pairs={{0,0},{1,1},{2,6},{3,7},{4,4},{5,5},{6,2},{7,3},{8,8},{9,9},{10,14... | collective-permute-start | bytes 786440 | tf_op jit(solution)/shard_map/ppermute | solution.py:652
  94.4 15.1 %collective-permute-start.16 = (bf16[256,512]{1,0:T(8,128)(2,1)}, bf16[256,512]{1,0:T(8,128)(2,1)S(1)}, u32[]{:S(2)}, u32[]{:S(2)}) collective-permute-start(bf16[256,512]{1,0:T(8,128)(2,1)} %gate.1), channel_id=1, source_target_pairs={{0,1},{1,0},{2,7},{3,6},{4,5},{5,4},{6,3},{7,2},{8,9},{9,8},{10,15... | collective-permute-start | bytes 786440 | tf_op jit(solution)/shard_map/ppermute | solution.py:652
  106.4 7.4 %collective-permute-start.17 = (bf16[256,512]{1,0:T(8,128)(2,1)S(1)}, bf16[256,512]{1,0:T(8,128)(2,1)S(1)}, u32[]{:S(2)}, u32[]{:S(2)}) collective-permute-start(bf16[256,512]{1,0:T(8,128)(2,1)S(1)} %collective-permute-done.15), channel_id=1, source_target_pairs={{0,1},{1,0},{2,3},{3,2},{4,5},{5,4},{6,7},{7,6},{8,9},{9,8},{10,11... | collective-permute-start | bytes 786440 | tf_op jit(solution)/shard_map/ppermute | solution.py:21
  106.4 1.2 %copy-start.2 = (bf16[256,2048]{1,0:T(8,128)(2,1)S(1)}, bf16[256,2048]{1,0:T(8,128)(2,1)}, u32[]{:S(2)}) copy-start(bf16[256,2048]{1,0:T(8,128)(2,1)} %get-tuple-element.55) | copy-start | bytes 3145732
  107.1 1.7 %copy-start = (bf16[512,2048]{1,0:T(8,128)(2,1)S(1)}, bf16[512,2048]{1,0:T(8,128)(2,1)}, u32[]{:S(2)}) copy-start(bf16[512,2048]{1,0:T(8,128)(2,1)} %get-tuple-element.70) | copy-start | bytes 6291460
  109.6 1.3 %copy-start.3 = (bf16[1,512,2048]{2,1,0:T(8,128)(2,1)}, bf16[1,512,2048]{2,1,0:T(8,128)(2,1)S(1)}, u32[]{:S(2)}) copy-start(bf16[1,512,2048]{2,1,0:T(8,128)(2,1)S(1)} %fusion.5) | copy-start | bytes 6291460
  (3 other events, 2.2 us)
